TPU v7x, 128 devices: a whole 4x4x4 slice. The times are simulated.
128 devices in a mesh: ctx: 32 (over y_lo, x, z), exp: 4 (over y_hi, core).
Axes of the slice: x: 4, y: 4 (y_hi: 2, y_lo: 2; y = y_hi * 2 + y_lo), z: 4, core: 2. Of those that a mesh axis runs over, the one named last changes fastest.
Arguments:
- hit_features: bfloat16 [16384, 1024], P('ctx'), may hold values from -6 to 6
- norm_attn: float32 [1024], replicated, may hold values from 0.1 to 1.9
- w_query: bfloat16 [1024, 1024], P(None, 'exp'), may hold values from -6 to 6
- w_key: bfloat16 [1024, 1024], P(None, 'exp'), may hold values from -0.1875 to 0.1875
- w_value: bfloat16 [1024, 1024], P(None, 'exp'), may hold values from -0.1875 to 0.1875
- w_out: bfloat16 [1024, 1024], P('exp'), may hold values from -0.1875 to 0.1875
- norm_ffn: float32 [1024], replicated, may hold values from 0.1 to 1.9
- w_router: bfloat16 [1024, 64], replicated, may hold values from -0.1875 to 0.1875
- w_gate: bfloat16 [64, 1024, 2048], P('ctx', None, 'exp'), may hold values from -0.1875 to 0.1875
- w_up: bfloat16 [64, 1024, 2048], P('ctx', None, 'exp'), may hold values from -0.1875 to 0.1875
- w_down: bfloat16 [64, 2048, 1024], P('ctx', 'exp'), may hold values from -0.125 to 0.125
- routes: int32 [16384, 2], P(('ctx', 'exp')), may hold values from 0 to 63, all different within a row; in each aligned block of 128 rows (0 to 127, 128 to 255, ...) at most 8 rows name the same one
Outputs:
- layer_out: bfloat16 [16384, 1024], P(('ctx', 'exp'))
Inputs may be any that keep to these rules, and one draw needn't show every extreme that they name: `routes`: each row names 2 different experts; in each aligned block of 128 rows (the rows of one device) no expert is named by more than 8 rows, a bound that some block reaches.
All inputs are finite; a program needn't handle non-finite values.
Results may differ from a plain program's by a relative error of at most 0.013.
The roundings to bfloat16 on the way count: a program that leaves them out, or rounds other values in their place, can miss the bound.
Values may be sent and summed in bfloat16 or wider, within the bound.
A program may use at most 128 MiB of HBM per device.

v0:
```python
import math

import jax
import jax.numpy as jnp
from jax import lax
from jax.sharding import PartitionSpec as P

D = 1024
HD = 64


EPSILON = 1e-05
LOWEST = -1e30


def passed_along(value, axis, steps):
    count = lax.axis_size(axis)
    pairs = [(source, (source + steps) % count) for source in range(count)]
    return lax.ppermute(value, axis, pairs)


def rms_norm(row_block, gain_vec):
    values = row_block.astype(jnp.float32)
    inv_rms = lax.rsqrt(jnp.mean(values * values, axis=-1, keepdims=True) + EPSILON)
    return (values * inv_rms * gain_vec).astype(jnp.bfloat16)


def attend(attn_state, queries, key_block, value_block):
    running_max, denominator, weighted = attn_state
    key_rows = key_block.shape[0]
    head_count = queries.shape[1]
    key_three = key_block.reshape(key_rows, head_count, -1)
    value_three = value_block.reshape(key_rows, head_count, -1)
    scores = jnp.einsum("qhd,khd->hqk", queries, key_three, preferred_element_type=jnp.float32) * (
        1.0 / math.sqrt(queries.shape[2])
    )
    new_max = jnp.maximum(running_max, jnp.max(scores, axis=-1, keepdims=True))
    exp_scores = jnp.exp(scores - new_max)
    rescale = jnp.exp(running_max - new_max)
    denominator = denominator * rescale + jnp.sum(exp_scores, axis=-1, keepdims=True)
    update = jnp.einsum(
        "hqk,khd->qhd",
        exp_scores.astype(jnp.bfloat16),
        value_three,
        preferred_element_type=jnp.float32,
    )
    weighted = weighted * jnp.transpose(rescale, (1, 0, 2)) + update
    return (new_max, denominator, weighted)


def run_experts(received, gate_mats, up_mats, down_mats):
    gate_act = jnp.einsum("sjcd,jdf->sjcf", received, gate_mats, preferred_element_type=jnp.float32)
    up_act = jnp.einsum("sjcd,jdf->sjcf", received, up_mats, preferred_element_type=jnp.float32)
    hidden = (jax.nn.silu(gate_act) * up_act).astype(jnp.bfloat16)
    return jnp.einsum("sjcf,jfd->sjcd", hidden, down_mats, preferred_element_type=jnp.float32)


def body(
    hit_features,
    norm_attn,
    w_query,
    w_key,
    w_value,
    w_out,
    norm_ffn,
    w_router,
    w_gate,
    w_up,
    w_down,
    routes,
):
    ctx_count = lax.axis_size("ctx")
    exp_count = lax.axis_size("exp")
    tok_ctx = hit_features.shape[0]
    rows_dev = tok_ctx // exp_count
    heads_local = w_query.shape[1] // HD
    normed = rms_norm(hit_features, norm_attn)
    queries = (
        jnp.dot(normed, w_query, preferred_element_type=jnp.float32)
        .astype(jnp.bfloat16)
        .reshape(tok_ctx, heads_local, HD)
    )
    key_proj = jnp.dot(normed, w_key, preferred_element_type=jnp.float32).astype(jnp.bfloat16)
    value_proj = jnp.dot(normed, w_value, preferred_element_type=jnp.float32).astype(jnp.bfloat16)
    key_value = jnp.stack([key_proj, value_proj])
    initial = (
        jnp.full((heads_local, tok_ctx, 1), LOWEST, jnp.float32),
        jnp.zeros((heads_local, tok_ctx, 1), jnp.float32),
        jnp.zeros((tok_ctx, heads_local, HD), jnp.float32),
    )
    started = attend(initial, queries, key_proj, value_proj)

    def advance(turn_index, loop_state):
        attn_state, moving = loop_state
        moving = passed_along(moving, "ctx", 1)
        return (attend(attn_state, queries, moving[0], moving[1]), moving)

    attn_state, leftover = lax.fori_loop(0, ctx_count - 1, advance, (started, key_value))
    running_max, denominator, weighted = attn_state
    attended = (
        (weighted / jnp.transpose(denominator, (1, 0, 2)))
        .astype(jnp.bfloat16)
        .reshape(tok_ctx, heads_local * HD)
    )
    mixed = lax.psum_scatter(
        jnp.dot(attended, w_out, preferred_element_type=jnp.float32).astype(jnp.bfloat16),
        "exp",
        scatter_dimension=0,
        tiled=True,
    ).astype(jnp.float32)
    own_rows = lax.dynamic_slice_in_dim(hit_features, lax.axis_index("exp") * rows_dev, rows_dev, 0)
    residual = own_rows.astype(jnp.float32) + mixed
    normed_ffn = rms_norm(residual, norm_ffn)
    logits = jnp.dot(normed_ffn, w_router, preferred_element_type=jnp.float32)
    expert_count = w_router.shape[1]
    top_count = routes.shape[1]
    capacity = 2 * top_count * rows_dev // expert_count
    picks = routes[:, :, None] == jnp.arange(expert_count, dtype=jnp.int32)[None, None, :]
    chosen = jnp.sum(
        jnp.where(picks, logits[:, None, :], jnp.zeros_like(logits[:, None, :])), axis=-1
    )
    gates = jax.nn.softmax(chosen, axis=-1)
    one_hot = picks.reshape(rows_dev * top_count, expert_count).astype(jnp.int32)
    earlier = jnp.cumsum(one_hot, axis=0) - one_hot
    slots = jnp.sum(earlier * one_hot, axis=-1)
    target = routes.reshape(-1) * capacity + slots
    outgoing = (
        jnp.zeros((expert_count * capacity, D), jnp.bfloat16)
        .at[target]
        .set(jnp.repeat(normed_ffn, top_count, axis=0))
    )
    local_experts = w_gate.shape[0]
    grid = outgoing.reshape(ctx_count, local_experts, capacity, D)
    copies = jnp.broadcast_to(grid[:, None], (ctx_count, exp_count) + grid.shape[1:]).reshape(
        (ctx_count * exp_count,) + grid.shape[1:]
    )
    produced = run_experts(
        lax.all_to_all(copies, ("ctx", "exp"), split_axis=0, concat_axis=0, tiled=True),
        w_gate,
        w_up,
        w_down,
    )
    returned = lax.all_to_all(
        produced.astype(jnp.bfloat16), ("ctx", "exp"), split_axis=0, concat_axis=0, tiled=True
    ).astype(produced.dtype)
    combined = jnp.sum(returned.reshape((ctx_count, exp_count) + grid.shape[1:]), axis=1)
    results = combined.reshape(expert_count * capacity, D)
    picked = jnp.take(results, target, axis=0).reshape(rows_dev, top_count, D)
    mixture = jnp.sum(gates[:, :, None] * picked, axis=1)
    return (residual + mixture).astype(jnp.bfloat16)


def solution(mesh):
    return jax.shard_map(
        body,
        mesh=mesh,
        in_specs=(
            P("ctx", None),
            P(),
            P(None, "exp"),
            P(None, "exp"),
            P(None, "exp"),
            P("exp", None),
            P(),
            P(),
            P("ctx", None, "exp"),
            P("ctx", None, "exp"),
            P("ctx", "exp", None),
            P(("ctx", "exp"), None),
        ),
        out_specs=P(("ctx", "exp"), None),
        check_vma=False,
    )
```

profile of v0, /device:TPU:1, one launch (start us, length us, event | category | flops | bytes accessed | tf_op | source)
XLA Modules:
  0.0 809.8 jit_solution(16901281861472844723)
XLA Ops:
  20.2 548.2 %while.16 = (s32[]{:T(128)}, f32[4,512,1]{1,0,2:T(4,128)S(1)}, f32[4,512,1]{1,0,2:T(4,128)S(1)}, f32[512,4,64]{0,2,1:T(8,128)S(1)}, bf16[2,512,256]{1,2,0:T(8,12...) while((s32[]{:T(128)}, f32[4,512,1]{1,0,2:T(4,128)S(1)}, f32[4,512,1]{1,0,2:T(4,128)S(1)}, ...), condition=%wide.region_6.0_spmd, body=%wide.region_3.0_spmd.sunk | while | flops 277092352 | bytes 18743412 | solution.py:98
  22.6 17.2 %collective-permute-done = bf16[2,512,256]{1,2,0:T(8,128)(2,1)S(1)} collective-permute-done((bf16[2,512,256]{1,2,0:T(8,128)(2,1)}, bf16[2,512,256]{1,2,0:T(8,128)(2,1)S(1)}, u32[]{:S(2)}, u32[]{:S(2)}) %collective-permute-start) | collective-permute-done | bytes 524320 | tf_op jit(solution)/shard_map/while/body/eval_jaxpr/ppermute | solution.py:19
  43.1 16.6 %collective-permute-done = bf16[2,512,256]{1,2,0:T(8,128)(2,1)S(1)} collective-permute-done((bf16[2,512,256]{1,2,0:T(8,128)(2,1)}, bf16[2,512,256]{1,2,0:T(8,128)(2,1)S(1)}, u32[]{:S(2)}, u32[]{:S(2)}) %collective-permute-start) | collective-permute-done | bytes 524320 | tf_op jit(solution)/shard_map/while/body/eval_jaxpr/ppermute | solution.py:19
  63.0 15.7 %collective-permute-done = bf16[2,512,256]{1,2,0:T(8,128)(2,1)S(1)} collective-permute-done((bf16[2,512,256]{1,2,0:T(8,128)(2,1)}, bf16[2,512,256]{1,2,0:T(8,128)(2,1)S(1)}, u32[]{:S(2)}, u32[]{:S(2)}) %collective-permute-start) | collective-permute-done | bytes 524320 | tf_op jit(solution)/shard_map/while/body/eval_jaxpr/ppermute | solution.py:19
  82.0 14.7 %collective-permute-done = bf16[2,512,256]{1,2,0:T(8,128)(2,1)S(1)} collective-permute-done((bf16[2,512,256]{1,2,0:T(8,128)(2,1)}, bf16[2,512,256]{1,2,0:T(8,128)(2,1)S(1)}, u32[]{:S(2)}, u32[]{:S(2)}) %collective-permute-start) | collective-permute-done | bytes 524320 | tf_op jit(solution)/shard_map/while/body/eval_jaxpr/ppermute | solution.py:19
  100.0 13.8 %collective-permute-done = bf16[2,512,256]{1,2,0:T(8,128)(2,1)S(1)} collective-permute-done((bf16[2,512,256]{1,2,0:T(8,128)(2,1)}, bf16[2,512,256]{1,2,0:T(8,128)(2,1)S(1)}, u32[]{:S(2)}, u32[]{:S(2)}) %collective-permute-start) | collective-permute-done | bytes 524320 | tf_op jit(solution)/shard_map/while/body/eval_jaxpr/ppermute | solution.py:19
  117.1 12.9 %collective-permute-done = bf16[2,512,256]{1,2,0:T(8,128)(2,1)S(1)} collective-permute-done((bf16[2,512,256]{1,2,0:T(8,128)(2,1)}, bf16[2,512,256]{1,2,0:T(8,128)(2,1)S(1)}, u32[]{:S(2)}, u32[]{:S(2)}) %collective-permute-start) | collective-permute-done | bytes 524320 | tf_op jit(solution)/shard_map/while/body/eval_jaxpr/ppermute | solution.py:19
  133.3 12.5 %collective-permute-done = bf16[2,512,256]{1,2,0:T(8,128)(2,1)S(1)} collective-permute-done((bf16[2,512,256]{1,2,0:T(8,128)(2,1)}, bf16[2,512,256]{1,2,0:T(8,128)(2,1)S(1)}, u32[]{:S(2)}, u32[]{:S(2)}) %collective-permute-start) | collective-permute-done | bytes 524320 | tf_op jit(solution)/shard_map/while/body/eval_jaxpr/ppermute | solution.py:19
  164.9 12.5 %collective-permute-done = bf16[2,512,256]{1,2,0:T(8,128)(2,1)S(1)} collective-permute-done((bf16[2,512,256]{1,2,0:T(8,128)(2,1)}, bf16[2,512,256]{1,2,0:T(8,128)(2,1)S(1)}, u32[]{:S(2)}, u32[]{:S(2)}) %collective-permute-start) | collective-permute-done | bytes 524320 | tf_op jit(solution)/shard_map/while/body/eval_jaxpr/ppermute | solution.py:19
  180.6 12.5 %collective-permute-done = bf16[2,512,256]{1,2,0:T(8,128)(2,1)S(1)} collective-permute-done((bf16[2,512,256]{1,2,0:T(8,128)(2,1)}, bf16[2,512,256]{1,2,0:T(8,128)(2,1)S(1)}, u32[]{:S(2)}, u32[]{:S(2)}) %collective-permute-start) | collective-permute-done | bytes 524320 | tf_op jit(solution)/shard_map/while/body/eval_jaxpr/ppermute | solution.py:19
  196.4 12.5 %collective-permute-done = bf16[2,512,256]{1,2,0:T(8,128)(2,1)S(1)} collective-permute-done((bf16[2,512,256]{1,2,0:T(8,128)(2,1)}, bf16[2,512,256]{1,2,0:T(8,128)(2,1)S(1)}, u32[]{:S(2)}, u32[]{:S(2)}) %collective-permute-start) | collective-permute-done | bytes 524320 | tf_op jit(solution)/shard_map/while/body/eval_jaxpr/ppermute | solution.py:19
  212.1 13.2 %collective-permute-done = bf16[2,512,256]{1,2,0:T(8,128)(2,1)S(1)} collective-permute-done((bf16[2,512,256]{1,2,0:T(8,128)(2,1)}, bf16[2,512,256]{1,2,0:T(8,128)(2,1)S(1)}, u32[]{:S(2)}, u32[]{:S(2)}) %collective-permute-start) | collective-permute-done | bytes 524320 | tf_op jit(solution)/shard_map/while/body/eval_jaxpr/ppermute | solution.py:19
  228.6 14.3 %collective-permute-done = bf16[2,512,256]{1,2,0:T(8,128)(2,1)S(1)} collective-permute-done((bf16[2,512,256]{1,2,0:T(8,128)(2,1)}, bf16[2,512,256]{1,2,0:T(8,128)(2,1)S(1)}, u32[]{:S(2)}, u32[]{:S(2)}) %collective-permute-start) | collective-permute-done | bytes 524320 | tf_op jit(solution)/shard_map/while/body/eval_jaxpr/ppermute | solution.py:19
  246.3 15.4 %collective-permute-done = bf16[2,512,256]{1,2,0:T(8,128)(2,1)S(1)} collective-permute-done((bf16[2,512,256]{1,2,0:T(8,128)(2,1)}, bf16[2,512,256]{1,2,0:T(8,128)(2,1)S(1)}, u32[]{:S(2)}, u32[]{:S(2)}) %collective-permute-start) | collective-permute-done | bytes 524320 | tf_op jit(solution)/shard_map/while/body/eval_jaxpr/ppermute | solution.py:19
  264.9 16.5 %collective-permute-done = bf16[2,512,256]{1,2,0:T(8,128)(2,1)S(1)} collective-permute-done((bf16[2,512,256]{1,2,0:T(8,128)(2,1)}, bf16[2,512,256]{1,2,0:T(8,128)(2,1)S(1)}, u32[]{:S(2)}, u32[]{:S(2)}) %collective-permute-start) | collective-permute-done | bytes 524320 | tf_op jit(solution)/shard_map/while/body/eval_jaxpr/ppermute | solution.py:19
  284.7 17.6 %collective-permute-done = bf16[2,512,256]{1,2,0:T(8,128)(2,1)S(1)} collective-permute-done((bf16[2,512,256]{1,2,0:T(8,128)(2,1)}, bf16[2,512,256]{1,2,0:T(8,128)(2,1)S(1)}, u32[]{:S(2)}, u32[]{:S(2)}) %collective-permute-start) | collective-permute-done | bytes 524320 | tf_op jit(solution)/shard_map/while/body/eval_jaxpr/ppermute | solution.py:19
  305.6 17.7 %collective-permute-done = bf16[2,512,256]{1,2,0:T(8,128)(2,1)S(1)} collective-permute-done((bf16[2,512,256]{1,2,0:T(8,128)(2,1)}, bf16[2,512,256]{1,2,0:T(8,128)(2,1)S(1)}, u32[]{:S(2)}, u32[]{:S(2)}) %collective-permute-start) | collective-permute-done | bytes 524320 | tf_op jit(solution)/shard_map/while/body/eval_jaxpr/ppermute | solution.py:19
  326.6 16.8 %collective-permute-done = bf16[2,512,256]{1,2,0:T(8,128)(2,1)S(1)} collective-permute-done((bf16[2,512,256]{1,2,0:T(8,128)(2,1)}, bf16[2,512,256]{1,2,0:T(8,128)(2,1)S(1)}, u32[]{:S(2)}, u32[]{:S(2)}) %collective-permute-start) | collective-permute-done | bytes 524320 | tf_op jit(solution)/shard_map/while/body/eval_jaxpr/ppermute | solution.py:19
  346.7 15.9 %collective-permute-done = bf16[2,512,256]{1,2,0:T(8,128)(2,1)S(1)} collective-permute-done((bf16[2,512,256]{1,2,0:T(8,128)(2,1)}, bf16[2,512,256]{1,2,0:T(8,128)(2,1)S(1)}, u32[]{:S(2)}, u32[]{:S(2)}) %collective-permute-start) | collective-permute-done | bytes 524320 | tf_op jit(solution)/shard_map/while/body/eval_jaxpr/ppermute | solution.py:19
  365.8 14.9 %collective-permute-done = bf16[2,512,256]{1,2,0:T(8,128)(2,1)S(1)} collective-permute-done((bf16[2,512,256]{1,2,0:T(8,128)(2,1)}, bf16[2,512,256]{1,2,0:T(8,128)(2,1)S(1)}, u32[]{:S(2)}, u32[]{:S(2)}) %collective-permute-start) | collective-permute-done | bytes 524320 | tf_op jit(solution)/shard_map/while/body/eval_jaxpr/ppermute | solution.py:19
  384.1 14.0 %collective-permute-done = bf16[2,512,256]{1,2,0:T(8,128)(2,1)S(1)} collective-permute-done((bf16[2,512,256]{1,2,0:T(8,128)(2,1)}, bf16[2,512,256]{1,2,0:T(8,128)(2,1)S(1)}, u32[]{:S(2)}, u32[]{:S(2)}) %collective-permute-start) | collective-permute-done | bytes 524320 | tf_op jit(solution)/shard_map/while/body/eval_jaxpr/ppermute | solution.py:19
  401.4 13.1 %collective-permute-done = bf16[2,512,256]{1,2,0:T(8,128)(2,1)S(1)} collective-permute-done((bf16[2,512,256]{1,2,0:T(8,128)(2,1)}, bf16[2,512,256]{1,2,0:T(8,128)(2,1)S(1)}, u32[]{:S(2)}, u32[]{:S(2)}) %collective-permute-start) | collective-permute-done | bytes 524320 | tf_op jit(solution)/shard_map/while/body/eval_jaxpr/ppermute | solution.py:19
  417.8 12.5 %collective-permute-done = bf16[2,512,256]{1,2,0:T(8,128)(2,1)S(1)} collective-permute-done((bf16[2,512,256]{1,2,0:T(8,128)(2,1)}, bf16[2,512,256]{1,2,0:T(8,128)(2,1)S(1)}, u32[]{:S(2)}, u32[]{:S(2)}) %collective-permute-start) | collective-permute-done | bytes 524320 | tf_op jit(solution)/shard_map/while/body/eval_jaxpr/ppermute | solution.py:19
  433.5 12.5 %collective-permute-done = bf16[2,512,256]{1,2,0:T(8,128)(2,1)S(1)} collective-permute-done((bf16[2,512,256]{1,2,0:T(8,128)(2,1)}, bf16[2,512,256]{1,2,0:T(8,128)(2,1)S(1)}, u32[]{:S(2)}, u32[]{:S(2)}) %collective-permute-start) | collective-permute-done | bytes 524320 | tf_op jit(solution)/shard_map/while/body/eval_jaxpr/ppermute | solution.py:19
  449.3 12.5 %collective-permute-done = bf16[2,512,256]{1,2,0:T(8,128)(2,1)S(1)} collective-permute-done((bf16[2,512,256]{1,2,0:T(8,128)(2,1)}, bf16[2,512,256]{1,2,0:T(8,128)(2,1)S(1)}, u32[]{:S(2)}, u32[]{:S(2)}) %collective-permute-start) | collective-permute-done | bytes 524320 | tf_op jit(solution)/shard_map/while/body/eval_jaxpr/ppermute | solution.py:19
  496.5 13.0 %collective-permute-done = bf16[2,512,256]{1,2,0:T(8,128)(2,1)S(1)} collective-permute-done((bf16[2,512,256]{1,2,0:T(8,128)(2,1)}, bf16[2,512,256]{1,2,0:T(8,128)(2,1)S(1)}, u32[]{:S(2)}, u32[]{:S(2)}) %collective-permute-start) | collective-permute-done | bytes 524320 | tf_op jit(solution)/shard_map/while/body/eval_jaxpr/ppermute | solution.py:19
  512.9 14.1 %collective-permute-done = bf16[2,512,256]{1,2,0:T(8,128)(2,1)S(1)} collective-permute-done((bf16[2,512,256]{1,2,0:T(8,128)(2,1)}, bf16[2,512,256]{1,2,0:T(8,128)(2,1)S(1)}, u32[]{:S(2)}, u32[]{:S(2)}) %collective-permute-start) | collective-permute-done | bytes 524320 | tf_op jit(solution)/shard_map/while/body/eval_jaxpr/ppermute | solution.py:19
  530.3 15.2 %collective-permute-done = bf16[2,512,256]{1,2,0:T(8,128)(2,1)S(1)} collective-permute-done((bf16[2,512,256]{1,2,0:T(8,128)(2,1)}, bf16[2,512,256]{1,2,0:T(8,128)(2,1)S(1)}, u32[]{:S(2)}, u32[]{:S(2)}) %collective-permute-start) | collective-permute-done | bytes 524320 | tf_op jit(solution)/shard_map/while/body/eval_jaxpr/ppermute | solution.py:19
  548.8 16.3 %collective-permute-done = bf16[2,512,256]{1,2,0:T(8,128)(2,1)S(1)} collective-permute-done((bf16[2,512,256]{1,2,0:T(8,128)(2,1)}, bf16[2,512,256]{1,2,0:T(8,128)(2,1)S(1)}, u32[]{:S(2)}, u32[]{:S(2)}) %collective-permute-start) | collective-permute-done | bytes 524320 | tf_op jit(solution)/shard_map/while/body/eval_jaxpr/ppermute | solution.py:19
  572.6 58.4 %reduce-scatter.2.cloned.1.call-done = bf16[128,1024]{1,0:T(8,128)(2,1)} async-done(((bf16[512,1024]{1,0:T(8,128)(2,1)}), bf16[128,1024]{1,0:T(8,128)(2,1)}) %reduce-scatter.2.cloned.1.call-update) | async-done | bytes 262160 | tf_op jit(solution)/shard_map/reduce_scatter | solution.py:105
  637.6 61.9 %all_to_all.10 = bf16[128,2,8,1024]{3,2,1,0:T(8,128)(2,1)S(1)} all-to-all(bf16[128,2,8,1024]{3,2,1,0:T(8,128)(2,1)S(1)} %bitcast.137), channel_id=1, replica_groups=mesh['ctx'=32,'exp'=4] {'ctx','exp'}, dimensions={0} | all-to-all | bytes 8388608 | tf_op jit(solution)/shard_map/all_to_all | solution.py:138
  735.5 53.4 %all-to-all-done.1 = bf16[128,2,8,1024]{3,2,1,0:T(8,128)(2,1)} async-done(((bf16[128,2,8,1024]{3,2,1,0:T(8,128)(2,1)}), bf16[128,2,8,1024]{3,2,1,0:T(8,128)(2,1)}, u32[]{:S(2)}, u32[]{:S(2)}) %all-to-all-start.1) | async-done | bytes 4194336 | tf_op jit(solution)/shard_map/all_to_all | solution.py:143
  (359 shorter events, 215.1 us)
Async XLA Ops:
  6.5 624.5 %reduce-scatter.2.cloned.1.call-start = ((), (), s32[]{:S(2)}) async-start(), calls=%async_computation.3 | async-start | bytes 1310720 | tf_op jit(solution)/shard_map/reduce_scatter | solution.py:105
  20.2 19.6 %collective-permute-start = (bf16[2,512,256]{1,2,0:T(8,128)(2,1)}, bf16[2,512,256]{1,2,0:T(8,128)(2,1)S(1)}, u32[]{:S(2)}, u32[]{:S(2)}) collective-permute-start(bf16[2,512,256]{1,2,0:T(8,128)(2,1)} %get-tuple-element.124), channel_id=1, source_target_pairs={{0,4},{4,8},{8,12},{12,16},{16,20},{20,24},{24,28},{28,32},{32,36}... | collective-permute-start | bytes 1572872 | tf_op jit(solution)/shard_map/while/body/eval_jaxpr/ppermute | solution.py:19
  43.1 16.6 %collective-permute-start = (bf16[2,512,256]{1,2,0:T(8,128)(2,1)}, bf16[2,512,256]{1,2,0:T(8,128)(2,1)S(1)}, u32[]{:S(2)}, u32[]{:S(2)}) collective-permute-start(bf16[2,512,256]{1,2,0:T(8,128)(2,1)} %get-tuple-element.124), channel_id=1, source_target_pairs={{0,4},{4,8},{8,12},{12,16},{16,20},{20,24},{24,28},{28,32},{32,36}... | collective-permute-start | bytes 1572872 | tf_op jit(solution)/shard_map/while/body/eval_jaxpr/ppermute | solution.py:19
  63.0 15.7 %collective-permute-start = (bf16[2,512,256]{1,2,0:T(8,128)(2,1)}, bf16[2,512,256]{1,2,0:T(8,128)(2,1)S(1)}, u32[]{:S(2)}, u32[]{:S(2)}) collective-permute-start(bf16[2,512,256]{1,2,0:T(8,128)(2,1)} %get-tuple-element.124), channel_id=1, source_target_pairs={{0,4},{4,8},{8,12},{12,16},{16,20},{20,24},{24,28},{28,32},{32,36}... | collective-permute-start | bytes 1572872 | tf_op jit(solution)/shard_map/while/body/eval_jaxpr/ppermute | solution.py:19
  82.0 14.8 %collective-permute-start = (bf16[2,512,256]{1,2,0:T(8,128)(2,1)}, bf16[2,512,256]{1,2,0:T(8,128)(2,1)S(1)}, u32[]{:S(2)}, u32[]{:S(2)}) collective-permute-start(bf16[2,512,256]{1,2,0:T(8,128)(2,1)} %get-tuple-element.124), channel_id=1, source_target_pairs={{0,4},{4,8},{8,12},{12,16},{16,20},{20,24},{24,28},{28,32},{32,36}... | collective-permute-start | bytes 1572872 | tf_op jit(solution)/shard_map/while/body/eval_jaxpr/ppermute | solution.py:19
  100.0 13.8 %collective-permute-start = (bf16[2,512,256]{1,2,0:T(8,128)(2,1)}, bf16[2,512,256]{1,2,0:T(8,128)(2,1)S(1)}, u32[]{:S(2)}, u32[]{:S(2)}) collective-permute-start(bf16[2,512,256]{1,2,0:T(8,128)(2,1)} %get-tuple-element.124), channel_id=1, source_target_pairs={{0,4},{4,8},{8,12},{12,16},{16,20},{20,24},{24,28},{28,32},{32,36}... | collective-permute-start | bytes 1572872 | tf_op jit(solution)/shard_map/while/body/eval_jaxpr/ppermute | solution.py:19
  117.1 12.9 %collective-permute-start = (bf16[2,512,256]{1,2,0:T(8,128)(2,1)}, bf16[2,512,256]{1,2,0:T(8,128)(2,1)S(1)}, u32[]{:S(2)}, u32[]{:S(2)}) collective-permute-start(bf16[2,512,256]{1,2,0:T(8,128)(2,1)} %get-tuple-element.124), channel_id=1, source_target_pairs={{0,4},{4,8},{8,12},{12,16},{16,20},{20,24},{24,28},{28,32},{32,36}... | collective-permute-start | bytes 1572872 | tf_op jit(solution)/shard_map/while/body/eval_jaxpr/ppermute | solution.py:19
  133.3 12.5 %collective-permute-start = (bf16[2,512,256]{1,2,0:T(8,128)(2,1)}, bf16[2,512,256]{1,2,0:T(8,128)(2,1)S(1)}, u32[]{:S(2)}, u32[]{:S(2)}) collective-permute-start(bf16[2,512,256]{1,2,0:T(8,128)(2,1)} %get-tuple-element.124), channel_id=1, source_target_pairs={{0,4},{4,8},{8,12},{12,16},{16,20},{20,24},{24,28},{28,32},{32,36}... | collective-permute-start | bytes 1572872 | tf_op jit(solution)/shard_map/while/body/eval_jaxpr/ppermute | solution.py:19
  149.1 12.5 %collective-permute-start = (bf16[2,512,256]{1,2,0:T(8,128)(2,1)}, bf16[2,512,256]{1,2,0:T(8,128)(2,1)S(1)}, u32[]{:S(2)}, u32[]{:S(2)}) collective-permute-start(bf16[2,512,256]{1,2,0:T(8,128)(2,1)} %get-tuple-element.124), channel_id=1, source_target_pairs={{0,4},{4,8},{8,12},{12,16},{16,20},{20,24},{24,28},{28,32},{32,36}... | collective-permute-start | bytes 1572872 | tf_op jit(solution)/shard_map/while/body/eval_jaxpr/ppermute | solution.py:19
  164.9 12.5 %collective-permute-start = (bf16[2,512,256]{1,2,0:T(8,128)(2,1)}, bf16[2,512,256]{1,2,0:T(8,128)(2,1)S(1)}, u32[]{:S(2)}, u32[]{:S(2)}) collective-permute-start(bf16[2,512,256]{1,2,0:T(8,128)(2,1)} %get-tuple-element.124), channel_id=1, source_target_pairs={{0,4},{4,8},{8,12},{12,16},{16,20},{20,24},{24,28},{28,32},{32,36}... | collective-permute-start | bytes 1572872 | tf_op jit(solution)/shard_map/while/body/eval_jaxpr/ppermute | solution.py:19
  180.6 12.5 %collective-permute-start = (bf16[2,512,256]{1,2,0:T(8,128)(2,1)}, bf16[2,512,256]{1,2,0:T(8,128)(2,1)S(1)}, u32[]{:S(2)}, u32[]{:S(2)}) collective-permute-start(bf16[2,512,256]{1,2,0:T(8,128)(2,1)} %get-tuple-element.124), channel_id=1, source_target_pairs={{0,4},{4,8},{8,12},{12,16},{16,20},{20,24},{24,28},{28,32},{32,36}... | collective-permute-start | bytes 1572872 | tf_op jit(solution)/shard_map/while/body/eval_jaxpr/ppermute | solution.py:19
  196.4 12.5 %collective-permute-start = (bf16[2,512,256]{1,2,0:T(8,128)(2,1)}, bf16[2,512,256]{1,2,0:T(8,128)(2,1)S(1)}, u32[]{:S(2)}, u32[]{:S(2)}) collective-permute-start(bf16[2,512,256]{1,2,0:T(8,128)(2,1)} %get-tuple-element.124), channel_id=1, source_target_pairs={{0,4},{4,8},{8,12},{12,16},{16,20},{20,24},{24,28},{28,32},{32,36}... | collective-permute-start | bytes 1572872 | tf_op jit(solution)/shard_map/while/body/eval_jaxpr/ppermute | solution.py:19
  212.1 13.2 %collective-permute-start = (bf16[2,512,256]{1,2,0:T(8,128)(2,1)}, bf16[2,512,256]{1,2,0:T(8,128)(2,1)S(1)}, u32[]{:S(2)}, u32[]{:S(2)}) collective-permute-start(bf16[2,512,256]{1,2,0:T(8,128)(2,1)} %get-tuple-element.124), channel_id=1, source_target_pairs={{0,4},{4,8},{8,12},{12,16},{16,20},{20,24},{24,28},{28,32},{32,36}... | collective-permute-start | bytes 1572872 | tf_op jit(solution)/shard_map/while/body/eval_jaxpr/ppermute | solution.py:19
  228.6 14.3 %collective-permute-start = (bf16[2,512,256]{1,2,0:T(8,128)(2,1)}, bf16[2,512,256]{1,2,0:T(8,128)(2,1)S(1)}, u32[]{:S(2)}, u32[]{:S(2)}) collective-permute-start(bf16[2,512,256]{1,2,0:T(8,128)(2,1)} %get-tuple-element.124), channel_id=1, source_target_pairs={{0,4},{4,8},{8,12},{12,16},{16,20},{20,24},{24,28},{28,32},{32,36}... | collective-permute-start | bytes 1572872 | tf_op jit(solution)/shard_map/while/body/eval_jaxpr/ppermute | solution.py:19
  246.3 15.4 %collective-permute-start = (bf16[2,512,256]{1,2,0:T(8,128)(2,1)}, bf16[2,512,256]{1,2,0:T(8,128)(2,1)S(1)}, u32[]{:S(2)}, u32[]{:S(2)}) collective-permute-start(bf16[2,512,256]{1,2,0:T(8,128)(2,1)} %get-tuple-element.124), channel_id=1, source_target_pairs={{0,4},{4,8},{8,12},{12,16},{16,20},{20,24},{24,28},{28,32},{32,36}... | collective-permute-start | bytes 1572872 | tf_op jit(solution)/shard_map/while/body/eval_jaxpr/ppermute | solution.py:19
  264.9 16.5 %collective-permute-start = (bf16[2,512,256]{1,2,0:T(8,128)(2,1)}, bf16[2,512,256]{1,2,0:T(8,128)(2,1)S(1)}, u32[]{:S(2)}, u32[]{:S(2)}) collective-permute-start(bf16[2,512,256]{1,2,0:T(8,128)(2,1)} %get-tuple-element.124), channel_id=1, source_target_pairs={{0,4},{4,8},{8,12},{12,16},{16,20},{20,24},{24,28},{28,32},{32,36}... | collective-permute-start | bytes 1572872 | tf_op jit(solution)/shard_map/while/body/eval_jaxpr/ppermute | solution.py:19
  284.7 17.6 %collective-permute-start = (bf16[2,512,256]{1,2,0:T(8,128)(2,1)}, bf16[2,512,256]{1,2,0:T(8,128)(2,1)S(1)}, u32[]{:S(2)}, u32[]{:S(2)}) collective-permute-start(bf16[2,512,256]{1,2,0:T(8,128)(2,1)} %get-tuple-element.124), channel_id=1, source_target_pairs={{0,4},{4,8},{8,12},{12,16},{16,20},{20,24},{24,28},{28,32},{32,36}... | collective-permute-start | bytes 1572872 | tf_op jit(solution)/shard_map/while/body/eval_jaxpr/ppermute | solution.py:19
  305.6 17.7 %collective-permute-start = (bf16[2,512,256]{1,2,0:T(8,128)(2,1)}, bf16[2,512,256]{1,2,0:T(8,128)(2,1)S(1)}, u32[]{:S(2)}, u32[]{:S(2)}) collective-permute-start(bf16[2,512,256]{1,2,0:T(8,128)(2,1)} %get-tuple-element.124), channel_id=1, source_target_pairs={{0,4},{4,8},{8,12},{12,16},{16,20},{20,24},{24,28},{28,32},{32,36}... | collective-permute-start | bytes 1572872 | tf_op jit(solution)/shard_map/while/body/eval_jaxpr/ppermute | solution.py:19
  326.6 16.8 %collective-permute-start = (bf16[2,512,256]{1,2,0:T(8,128)(2,1)}, bf16[2,512,256]{1,2,0:T(8,128)(2,1)S(1)}, u32[]{:S(2)}, u32[]{:S(2)}) collective-permute-start(bf16[2,512,256]{1,2,0:T(8,128)(2,1)} %get-tuple-element.124), channel_id=1, source_target_pairs={{0,4},{4,8},{8,12},{12,16},{16,20},{20,24},{24,28},{28,32},{32,36}... | collective-permute-start | bytes 1572872 | tf_op jit(solution)/shard_map/while/body/eval_jaxpr/ppermute | solution.py:19
  346.7 15.9 %collective-permute-start = (bf16[2,512,256]{1,2,0:T(8,128)(2,1)}, bf16[2,512,256]{1,2,0:T(8,128)(2,1)S(1)}, u32[]{:S(2)}, u32[]{:S(2)}) collective-permute-start(bf16[2,512,256]{1,2,0:T(8,128)(2,1)} %get-tuple-element.124), channel_id=1, source_target_pairs={{0,4},{4,8},{8,12},{12,16},{16,20},{20,24},{24,28},{28,32},{32,36}... | collective-permute-start | bytes 1572872 | tf_op jit(solution)/shard_map/while/body/eval_jaxpr/ppermute | solution.py:19
  365.8 14.9 %collective-permute-start = (bf16[2,512,256]{1,2,0:T(8,128)(2,1)}, bf16[2,512,256]{1,2,0:T(8,128)(2,1)S(1)}, u32[]{:S(2)}, u32[]{:S(2)}) collective-permute-start(bf16[2,512,256]{1,2,0:T(8,128)(2,1)} %get-tuple-element.124), channel_id=1, source_target_pairs={{0,4},{4,8},{8,12},{12,16},{16,20},{20,24},{24,28},{28,32},{32,36}... | collective-permute-start | bytes 1572872 | tf_op jit(solution)/shard_map/while/body/eval_jaxpr/ppermute | solution.py:19
  384.1 14.0 %collective-permute-start = (bf16[2,512,256]{1,2,0:T(8,128)(2,1)}, bf16[2,512,256]{1,2,0:T(8,128)(2,1)S(1)}, u32[]{:S(2)}, u32[]{:S(2)}) collective-permute-start(bf16[2,512,256]{1,2,0:T(8,128)(2,1)} %get-tuple-element.124), channel_id=1, source_target_pairs={{0,4},{4,8},{8,12},{12,16},{16,20},{20,24},{24,28},{28,32},{32,36}... | collective-permute-start | bytes 1572872 | tf_op jit(solution)/shard_map/while/body/eval_jaxpr/ppermute | solution.py:19
  401.4 13.1 %collective-permute-start = (bf16[2,512,256]{1,2,0:T(8,128)(2,1)}, bf16[2,512,256]{1,2,0:T(8,128)(2,1)S(1)}, u32[]{:S(2)}, u32[]{:S(2)}) collective-permute-start(bf16[2,512,256]{1,2,0:T(8,128)(2,1)} %get-tuple-element.124), channel_id=1, source_target_pairs={{0,4},{4,8},{8,12},{12,16},{16,20},{20,24},{24,28},{28,32},{32,36}... | collective-permute-start | bytes 1572872 | tf_op jit(solution)/shard_map/while/body/eval_jaxpr/ppermute | solution.py:19
  417.8 12.5 %collective-permute-start = (bf16[2,512,256]{1,2,0:T(8,128)(2,1)}, bf16[2,512,256]{1,2,0:T(8,128)(2,1)S(1)}, u32[]{:S(2)}, u32[]{:S(2)}) collective-permute-start(bf16[2,512,256]{1,2,0:T(8,128)(2,1)} %get-tuple-element.124), channel_id=1, source_target_pairs={{0,4},{4,8},{8,12},{12,16},{16,20},{20,24},{24,28},{28,32},{32,36}... | collective-permute-start | bytes 1572872 | tf_op jit(solution)/shard_map/while/body/eval_jaxpr/ppermute | solution.py:19
  433.5 12.5 %collective-permute-start = (bf16[2,512,256]{1,2,0:T(8,128)(2,1)}, bf16[2,512,256]{1,2,0:T(8,128)(2,1)S(1)}, u32[]{:S(2)}, u32[]{:S(2)}) collective-permute-start(bf16[2,512,256]{1,2,0:T(8,128)(2,1)} %get-tuple-element.124), channel_id=1, source_target_pairs={{0,4},{4,8},{8,12},{12,16},{16,20},{20,24},{24,28},{28,32},{32,36}... | collective-permute-start | bytes 1572872 | tf_op jit(solution)/shard_map/while/body/eval_jaxpr/ppermute | solution.py:19
  449.3 12.5 %collective-permute-start = (bf16[2,512,256]{1,2,0:T(8,128)(2,1)}, bf16[2,512,256]{1,2,0:T(8,128)(2,1)S(1)}, u32[]{:S(2)}, u32[]{:S(2)}) collective-permute-start(bf16[2,512,256]{1,2,0:T(8,128)(2,1)} %get-tuple-element.124), channel_id=1, source_target_pairs={{0,4},{4,8},{8,12},{12,16},{16,20},{20,24},{24,28},{28,32},{32,36}... | collective-permute-start | bytes 1572872 | tf_op jit(solution)/shard_map/while/body/eval_jaxpr/ppermute | solution.py:19
  465.0 12.5 %collective-permute-start = (bf16[2,512,256]{1,2,0:T(8,128)(2,1)}, bf16[2,512,256]{1,2,0:T(8,128)(2,1)S(1)}, u32[]{:S(2)}, u32[]{:S(2)}) collective-permute-start(bf16[2,512,256]{1,2,0:T(8,128)(2,1)} %get-tuple-element.124), channel_id=1, source_target_pairs={{0,4},{4,8},{8,12},{12,16},{16,20},{20,24},{24,28},{28,32},{32,36}... | collective-permute-start | bytes 1572872 | tf_op jit(solution)/shard_map/while/body/eval_jaxpr/ppermute | solution.py:19
  496.5 13.1 %collective-permute-start = (bf16[2,512,256]{1,2,0:T(8,128)(2,1)}, bf16[2,512,256]{1,2,0:T(8,128)(2,1)S(1)}, u32[]{:S(2)}, u32[]{:S(2)}) collective-permute-start(bf16[2,512,256]{1,2,0:T(8,128)(2,1)} %get-tuple-element.124), channel_id=1, source_target_pairs={{0,4},{4,8},{8,12},{12,16},{16,20},{20,24},{24,28},{28,32},{32,36}... | collective-permute-start | bytes 1572872 | tf_op jit(solution)/shard_map/while/body/eval_jaxpr/ppermute | solution.py:19
  512.9 14.1 %collective-permute-start = (bf16[2,512,256]{1,2,0:T(8,128)(2,1)}, bf16[2,512,256]{1,2,0:T(8,128)(2,1)S(1)}, u32[]{:S(2)}, u32[]{:S(2)}) collective-permute-start(bf16[2,512,256]{1,2,0:T(8,128)(2,1)} %get-tuple-element.124), channel_id=1, source_target_pairs={{0,4},{4,8},{8,12},{12,16},{16,20},{20,24},{24,28},{28,32},{32,36}... | collective-permute-start | bytes 1572872 | tf_op jit(solution)/shard_map/while/body/eval_jaxpr/ppermute | solution.py:19
  530.3 15.2 %collective-permute-start = (bf16[2,512,256]{1,2,0:T(8,128)(2,1)}, bf16[2,512,256]{1,2,0:T(8,128)(2,1)S(1)}, u32[]{:S(2)}, u32[]{:S(2)}) collective-permute-start(bf16[2,512,256]{1,2,0:T(8,128)(2,1)} %get-tuple-element.124), channel_id=1, source_target_pairs={{0,4},{4,8},{8,12},{12,16},{16,20},{20,24},{24,28},{28,32},{32,36}... | collective-permute-start | bytes 1572872 | tf_op jit(solution)/shard_map/while/body/eval_jaxpr/ppermute | solution.py:19
  548.8 16.3 %collective-permute-start = (bf16[2,512,256]{1,2,0:T(8,128)(2,1)}, bf16[2,512,256]{1,2,0:T(8,128)(2,1)S(1)}, u32[]{:S(2)}, u32[]{:S(2)}) collective-permute-start(bf16[2,512,256]{1,2,0:T(8,128)(2,1)} %get-tuple-element.124), channel_id=1, source_target_pairs={{0,4},{4,8},{8,12},{12,16},{16,20},{20,24},{24,28},{28,32},{32,36}... | collective-permute-start | bytes 1572872 | tf_op jit(solution)/shard_map/while/body/eval_jaxpr/ppermute | solution.py:19
  727.0 61.9 %all-to-all-start.1 = ((bf16[128,2,8,1024]{3,2,1,0:T(8,128)(2,1)}), bf16[128,2,8,1024]{3,2,1,0:T(8,128)(2,1)}, u32[]{:S(2)}, u32[]{:S(2)}) async-start(bf16[128,2,8,1024]{3,2,1,0:T(8,128)(2,1)} %copy.63), calls=%async_computation.2 | async-start | bytes 8388608 | tf_op jit(solution)/shard_map/all_to_all | solution.py:143
  (12 other events, 1422.6 us)
Sparse Core Ops, SparseCore 0:
  571.1 59.9 reduce-scatter.1
where the time goes:
time: 811 us; the launch traced here: 810 us
  waiting for transfers between devices  555 us (68%)
  matrix products  82.6 us (10%)
  blocking collectives  61.9 us (8%)
  local copies, waits for them, and re-layouts  46.3 us (6%)
  other arithmetic  38.5 us (5%)
  between operations  13.7 us (2%)
  starting transfers between devices  10.3 us (1%)
    ppermute x31, waiting for transfers between devices, passed_along(): return lax.ppermute(value, axis, pairs)  444 us
    all_to_all x1, blocking collectives, body(): lax.all_to_all(copies, ('ctx', 'exp'), split_axis=0, concat_axis=0, tiled...  61.9 us
    reduce_scatter x1, waiting for transfers between devices, body(): lax.psum_scatter(jnp.dot(attended, w_out, preferred_element_type=jnp.floa...  58.4 us
    all_to_all x1, waiting for transfers between devices, body(): lax.all_to_all(produced.astype(jnp.bfloat16), ('ctx', 'exp'), split_axis=...  53.4 us
    dot_general x32, matrix products, attend(): jnp.einsum('hqk,khd->qhd', exp_scores.astype(jnp.bfloat16), value_three,...  31.7 us
    dot_general x32, matrix products, attend(): jnp.einsum('qhd,khd->hqk', queries, key_three, preferred_element_type=jnp...  24.6 us
    while x62, local copies, waits for them, and re-layouts  24.6 us
    reduce_sum x32, other arithmetic, attend(): jnp.sum(exp_scores, axis=-1, keepdims=True)  22.6 us
  transfers between devices with their start and end apart: 33, of which 33 were waited for; matrix products, arithmetic and copies ran while one was open for 0% of the time, Pallas kernels for 0%

commit v1 on v0

v1 whole, which is shorter than its diff:
```python
import functools
import math

import jax
import jax.numpy as jnp
from jax import lax
from jax.experimental import pallas as pl
from jax.experimental.pallas import tpu as pltpu
from jax.sharding import PartitionSpec as P

D = 1024
HD = 64
EPSILON = 1e-05
LOWEST = -1e30
ALPHA = math.log2(math.e) / math.sqrt(HD)
BF = jnp.bfloat16
F32 = jnp.float32
MESH = pl.DeviceIdType.MESH
VMEM = pltpu.VMEM


def whole():
    return pl.BlockSpec(memory_space=pltpu.VMEM)


def anywhere():
    return pl.BlockSpec(memory_space=pl.ANY)


def project_kernel(x_ref, gain_ref, wq_ref, wk_ref, wv_ref, qt_ref, kp_ref, vt_ref):
    x = x_ref[...].astype(F32)
    inv = lax.rsqrt(jnp.mean(x * x, axis=-1, keepdims=True) + EPSILON)
    n = (x * inv * gain_ref[...]).astype(BF)
    q = jnp.dot(n, wq_ref[...], preferred_element_type=F32)
    qt = q.T.astype(BF)
    for head in range(4):
        for block in range(4):
            qt_ref[block % 2, head, :, (block // 2) * 128 : (block // 2) * 128 + 128] = qt[
                head * HD : head * HD + HD, block * 128 : block * 128 + 128
            ]
    k = jnp.dot(n, wk_ref[...], preferred_element_type=F32)
    for head in range(4):
        for half in range(2):
            kh = k[half * 256 : half * 256 + 256, head * HD : head * HD + HD]
            kp_ref[head, half] = jnp.concatenate([kh[0:128], kh[128:256]], axis=1).astype(BF)
    vt = jnp.dot(n, wv_ref[...], preferred_element_type=F32).T.astype(BF)
    for head in range(4):
        for half in range(2):
            for u in range(2):
                at = half * 256 + u * 128
                vt_ref[head, half, u] = vt[head * HD : head * HD + HD, at : at + 128]


def project(x, gain, wq, wk, wv):
    return pl.pallas_call(
        project_kernel,
        out_shape=(
            jax.ShapeDtypeStruct((2, 4, HD, 256), BF),
            jax.ShapeDtypeStruct((4, 2, 128, 128), BF),
            jax.ShapeDtypeStruct((4, 2, 2, HD, 128), BF),
        ),
        in_specs=[whole()] * 5,
        out_specs=(whole(), whole(), whole()),
        name="project",
    )(x, gain.reshape(1, D), wq, wk, wv)


def attention_kernel(
    qt_ref,
    kp_ref,
    vt_ref,
    wo_ref,
    at_ref,
    wo_all_ref,
    qg,
    kg,
    vg,
    q2,
    s_ref,
    acc,
    mx,
    ls,
    ost,
    x_send,
    x_recv,
    ring_send,
    ring_recv,
    sib_send,
    sib_recv,
    o_send,
    o_recv,
    w_send,
    w_recv,
    w_own,
):
    ctx = lax.axis_index("ctx")
    exp = lax.axis_index("exp")
    ylo = ctx // 16
    x = (ctx // 4) % 4
    z = ctx % 4
    yhi = exp // 2
    core = exp % 2
    mine = ylo * 4 + z

    def device(to_ylo, to_x, to_z, to_yhi, to_core):
        return (to_ylo * 16 + to_x * 4 + to_z, to_yhi * 2 + to_core)

    right = device(ylo, (x + 1) % 4, z, yhi, core)
    left = device(ylo, (x + 3) % 4, z, yhi, core)
    sibling = device(ylo, x, z, yhi, 1 - core)

    barrier = pltpu.get_barrier_semaphore()

    def greet(i, carry):
        to = device(i // 16, x, (i // 4) % 4, (i // 2) % 2, i % 2)

        @pl.when(i != ylo * 16 + z * 4 + yhi * 2 + core)
        def _():
            pl.semaphore_signal(barrier, inc=1, device_id=to, device_id_type=MESH)

        return carry

    lax.fori_loop(0, 32, greet, 0)
    pl.semaphore_signal(barrier, inc=1, device_id=right, device_id_type=MESH)
    pl.semaphore_signal(barrier, inc=1, device_id=left, device_id_type=MESH)
    pl.semaphore_wait(barrier, 33)

    def head_copies(i):
        head, half = i // 2, i % 2
        to = device(core, x, head, yhi, half)
        parts = (
            (qt_ref.at[half, head], qg.at[mine]),
            (kp_ref.at[head, half], kg.at[0, half, pl.ds(pl.multiple_of(mine * 128, 128), 128), :]),
            (
                vt_ref.at[head, half],
                vg.at[0, half, :, :, pl.ds(pl.multiple_of(mine * 128, 128), 128)],
            ),
        )
        own = (core == ylo) & (head == z) & (half == core)
        remote = [
            pltpu.make_async_remote_copy(
                src_ref=src,
                dst_ref=dst,
                send_sem=x_send.at[n, i],
                recv_sem=x_recv.at[n, mine],
                device_id=to,
                device_id_type=MESH,
            )
            for n, (src, dst) in enumerate(parts)
        ]
        local = [
            pltpu.make_async_copy(src, dst, x_recv.at[n, mine])
            for n, (src, dst) in enumerate(parts)
        ]
        return own, remote, local

    def send_heads(i, carry):
        own, remote, local = head_copies(i)

        @pl.when(own)
        def _():
            for copy in local:
                copy.start()

        @pl.when(jnp.logical_not(own))
        def _():
            for copy in remote:
                copy.start()

        return carry

    lax.fori_loop(0, 8, send_heads, 0)

    def await_heads(j, carry):
        pltpu.make_async_copy(qg.at[j], qg.at[j], x_recv.at[0, j]).wait()
        at = pl.ds(pl.multiple_of(j * 128, 128), 128)
        kd = kg.at[0, core, at, :]
        pltpu.make_async_copy(kd, kd, x_recv.at[1, j]).wait()
        vd = vg.at[0, core, :, :, at]
        pltpu.make_async_copy(vd, vd, x_recv.at[2, j]).wait()
        return carry

    lax.fori_loop(0, 8, await_heads, 0)

    def remote(src, dst, send, recv, to):
        return pltpu.make_async_remote_copy(
            src_ref=src,
            dst_ref=dst,
            send_sem=send,
            recv_sem=recv,
            device_id=to,
            device_id_type=MESH,
        )

    def to_sibling(slot):
        return [
            remote(g.at[slot, core], g.at[slot, core], sib_send.at[n, slot], sib_recv.at[n, slot], sibling)
            for n, g in enumerate((kg, vg))
        ]

    def from_sibling(slot):
        return [
            remote(g.at[slot, 1 - core], g.at[slot, 1 - core], sib_send.at[n, slot], sib_recv.at[n, slot], sibling)
            for n, g in enumerate((kg, vg))
        ]

    k_right = remote(kg.at[0, core], kg.at[1, core], ring_send.at[0, 0], ring_recv.at[0, 0], right)
    v_right = remote(vg.at[0, core], vg.at[1, core], ring_send.at[1, 0], ring_recv.at[1, 0], right)
    k_left = remote(kg.at[0, core], kg.at[2, core], ring_send.at[0, 1], ring_recv.at[0, 1], left)
    v_left = remote(vg.at[0, core], vg.at[2, core], ring_send.at[1, 1], ring_recv.at[1, 1], left)
    k_on = remote(kg.at[1, core], kg.at[3, core], ring_send.at[0, 2], ring_recv.at[0, 2], right)
    v_on = remote(vg.at[2, core], vg.at[3, core], ring_send.at[1, 2], ring_recv.at[1, 2], left)
    for copy in (k_right, k_left, v_right, v_left):
        copy.start()
    for copy in to_sibling(0):
        copy.start()

    w_copies = [
        remote(
            wo_ref,
            wo_all_ref.at[exp],
            w_send.at[step - 1],
            w_recv.at[step - 1],
            (ctx, (exp + step) % 4),
        )
        for step in range(1, 4)
    ]
    w_local = pltpu.make_async_copy(wo_ref, wo_all_ref.at[exp], w_own)
    for copy in w_copies:
        copy.start()
    w_local.start()

    zero = jnp.zeros((HD, 256), BF)
    for j in range(8):
        q2[j, 0, 0:HD] = qg[j]
        q2[j, 0, HD : 2 * HD] = zero
        q2[j, 1, 0:HD] = zero
        q2[j, 1, HD : 2 * HD] = qg[j]
    acc[...] = jnp.zeros_like(acc)
    mx[...] = jnp.full_like(mx, LOWEST)
    ls[...] = jnp.zeros_like(ls)

    def score(phase, j, p):
        keys = kg[phase // 2, (phase + core) % 2]
        for u in range(2):
            s_ref[p, u] = lax.dot_general(
                keys, q2[j, u], (((1,), (0,)), ((), ())), preferred_element_type=F32
            )

    def absorb(phase, j, p):
        s0 = s_ref[p, 0]
        s1 = s_ref[p, 1]
        old = mx[j]
        new = jnp.maximum(
            old,
            jnp.maximum(jnp.max(s0, axis=0, keepdims=True), jnp.max(s1, axis=0, keepdims=True)),
        )
        fade = jnp.exp2((old - new) * ALPHA)
        e0 = jnp.exp2((s0 - new) * ALPHA)
        e1 = jnp.exp2((s1 - new) * ALPHA)
        slot, half = phase // 2, (phase + core) % 2
        ls[j] = ls[j] * fade + (
            jnp.sum(e0, axis=0, keepdims=True) + jnp.sum(e1, axis=0, keepdims=True)
        )
        acc[j] = acc[j] * fade + (
            jnp.dot(vg[slot, half, 0], e0.astype(BF), preferred_element_type=F32)
            + jnp.dot(vg[slot, half, 1], e1.astype(BF), preferred_element_type=F32)
        )
        mx[j] = new

    score(0, 0, 0)

    def turn(g, carry):
        phase, pair = g // 4, g % 4
        last = pair == 3

        for slot in (0, 1, 2, 3):

            @pl.when(last & (phase == 2 * slot))
            def _(slot=slot):
                for copy in from_sibling(slot):
                    copy.wait_recv()

        @pl.when(last & (phase == 1))
        def _():
            for copy in (k_right, k_left, v_right, v_left):
                copy.wait_recv()
            k_on.start()
            v_on.start()
            for slot in (1, 2):
                for copy in to_sibling(slot):
                    copy.start()

        @pl.when(last & (phase == 5))
        def _():
            k_on.wait_recv()
            v_on.wait_recv()
            for copy in to_sibling(3):
                copy.start()

        score(phase, 2 * pair + 1, 1)
        absorb(phase, 2 * pair, 0)
        later = jnp.minimum(g + 1, 31)
        score(later // 4, 2 * (later % 4), 0)
        absorb(phase, 2 * pair + 1, 1)
        return carry

    lax.fori_loop(0, 32, turn, 0)

    for j in range(8):
        o = (acc[j] / ls[j]).astype(BF)
        ost[j, 0] = o[:, 0:128]
        ost[j, 1] = o[:, 128:256]

    head = yhi * 8 + mine

    def out_copy(i):
        j, to_yhi = i % 8, i // 8
        to = device(j // 4, x, j % 4, to_yhi, core)
        return (
            remote(ost.at[j, to_yhi], at_ref.at[head], o_send.at[i], o_recv.at[head], to),
            pltpu.make_async_copy(ost.at[j, to_yhi], at_ref.at[head], o_recv.at[head]),
        )

    def send_out(i, carry):
        away, local = out_copy(i)

        @pl.when(i == head)
        def _():
            local.start()

        @pl.when(i != head)
        def _():
            away.start()

        return carry

    lax.fori_loop(0, 16, send_out, 0)

    def await_out(i, carry):
        pltpu.make_async_copy(at_ref.at[i], at_ref.at[i], o_recv.at[i]).wait()
        return carry

    lax.fori_loop(0, 16, await_out, 0)

    def sent_heads(i, carry):
        own, away, local = head_copies(i)

        @pl.when(jnp.logical_not(own))
        def _():
            for copy in away:
                copy.wait_send()

        return carry

    lax.fori_loop(0, 8, sent_heads, 0)

    def sent_out(i, carry):
        away, local = out_copy(i)

        @pl.when(i != head)
        def _():
            away.wait_send()

        return carry

    lax.fori_loop(0, 16, sent_out, 0)
    for copy in (k_right, k_left, v_right, v_left, k_on, v_on):
        copy.wait_send()
    for slot in range(4):
        for copy in to_sibling(slot):
            copy.wait_send()
    w_local.wait()
    for copy in w_copies:
        copy.wait_send()
    for step in range(1, 4):
        slot = (exp + 4 - step) % 4
        remote(
            wo_ref,
            wo_all_ref.at[slot],
            w_send.at[step - 1],
            w_recv.at[step - 1],
            (ctx, slot),
        ).wait_recv()


def attention(qt, kp, vt, wo):
    return pl.pallas_call(
        attention_kernel,
        out_shape=(
            jax.ShapeDtypeStruct((16, HD, 128), BF),
            jax.ShapeDtypeStruct((4, 256, D), BF),
        ),
        in_specs=[whole(), whole(), whole(), anywhere()],
        out_specs=(anywhere(), anywhere()),
        scratch_shapes=[
            VMEM((8, HD, 256), BF),
            VMEM((4, 2, 1024, 128), BF),
            VMEM((4, 2, 2, HD, 1024), BF),
            VMEM((8, 2, 128, 256), BF),
            VMEM((2, 2, 1024, 256), F32),
            VMEM((8, HD, 256), F32),
            VMEM((8, 1, 256), F32),
            VMEM((8, 1, 256), F32),
            VMEM((8, 2, HD, 128), BF),
            pltpu.SemaphoreType.DMA((3, 8)),
            pltpu.SemaphoreType.DMA((3, 8)),
            pltpu.SemaphoreType.DMA((2, 3)),
            pltpu.SemaphoreType.DMA((2, 3)),
            pltpu.SemaphoreType.DMA((2, 4)),
            pltpu.SemaphoreType.DMA((2, 4)),
            pltpu.SemaphoreType.DMA((16,)),
            pltpu.SemaphoreType.DMA((16,)),
            pltpu.SemaphoreType.DMA((3,)),
            pltpu.SemaphoreType.DMA((3,)),
            pltpu.SemaphoreType.DMA,
        ],
        compiler_params=pltpu.CompilerParams(
            collective_id=0, has_side_effects=True, vmem_limit_bytes=40 << 20
        ),
        name="attention",
    )(qt, kp, vt, wo)


def route_kernel(at_ref, wo_ref, hit_ref, gain_ref, wr_ref, routes_ref, res_ref, out_ref, hi_ref, lo_ref):
    mixed = lax.dot_general(
        at_ref[...], wo_ref[...], (((0,), (0,)), ((), ())), preferred_element_type=F32
    )
    residual = hit_ref[...].astype(F32) + mixed
    res_ref[...] = residual
    inv = lax.rsqrt(jnp.mean(residual * residual, axis=-1, keepdims=True) + EPSILON)
    normed = (residual * inv * gain_ref[...]).astype(BF)
    logits = jnp.dot(normed, wr_ref[...], preferred_element_type=F32)
    rows, experts = logits.shape
    ids = lax.broadcasted_iota(jnp.int32, (rows, experts), 1)
    picks = (routes_ref[:, 0:1] == ids) | (routes_ref[:, 1:2] == ids)
    top = jnp.max(jnp.where(picks, logits, -jnp.inf), axis=-1, keepdims=True)
    weights = jnp.where(picks, jnp.exp(jnp.where(picks, logits - top, 0.0)), 0.0)
    gates = weights / jnp.sum(weights, axis=-1, keepdims=True)
    gate_hi = gates.astype(BF)
    gate_lo = (gates - gate_hi.astype(F32)).astype(BF)
    marks = jnp.where(picks, 1.0, 0.0).astype(BF)
    before = lax.broadcasted_iota(jnp.int32, (rows, rows), 0) > lax.broadcasted_iota(
        jnp.int32, (rows, rows), 1
    )
    slots = jnp.dot(
        jnp.where(before, 1.0, 0.0).astype(BF), marks, preferred_element_type=F32
    ).astype(BF)
    places = out_ref.shape[0]
    cap = places // experts
    spread = jnp.where(
        lax.broadcasted_iota(jnp.int32, (experts, places), 1) // cap
        == lax.broadcasted_iota(jnp.int32, (experts, places), 0),
        1.0,
        0.0,
    ).astype(BF)
    wide = lambda v: jnp.dot(v, spread, preferred_element_type=F32)
    order = (lax.broadcasted_iota(jnp.int32, (rows, places), 1) % cap).astype(F32)
    here = (wide(marks) > 0.5) & (wide(slots) == order)
    table = jnp.where(here, 1.0, 0.0).astype(BF)
    out_ref[...] = lax.dot_general(
        table, normed, (((0,), (0,)), ((), ())), preferred_element_type=F32
    ).astype(BF)
    hi_ref[...] = jnp.where(here, wide(gate_hi), 0.0).astype(BF)
    lo_ref[...] = jnp.where(here, wide(gate_lo), 0.0).astype(BF)


def route(at, wo, hit, gain, wr, routes):
    rows = hit.shape[0]
    places = wr.shape[1] * 8
    return pl.pallas_call(
        route_kernel,
        out_shape=(
            jax.ShapeDtypeStruct((rows, D), F32),
            jax.ShapeDtypeStruct((places, D), BF),
            jax.ShapeDtypeStruct((rows, places), BF),
            jax.ShapeDtypeStruct((rows, places), BF),
        ),
        in_specs=[whole()] * 6,
        out_specs=(whole(),) * 4,
        name="route",
    )(at, wo, hit, gain.reshape(1, D), wr, routes)


def combine_kernel(res_ref, hi_ref, lo_ref, back_ref, out_ref):
    back = back_ref[...]
    mixture = jnp.dot(hi_ref[...], back, preferred_element_type=F32) + jnp.dot(
        lo_ref[...], back, preferred_element_type=F32
    )
    out_ref[...] = (res_ref[...] + mixture).astype(BF)


def run_experts(received, gate_mats, up_mats, down_mats):
    gate_act = jnp.einsum("sjcd,jdf->sjcf", received, gate_mats, preferred_element_type=F32)
    up_act = jnp.einsum("sjcd,jdf->sjcf", received, up_mats, preferred_element_type=F32)
    hidden = (jax.nn.silu(gate_act) * up_act).astype(BF)
    return jnp.einsum("sjcf,jfd->sjcd", hidden, down_mats, preferred_element_type=F32)


def body(
    hit_features,
    norm_attn,
    w_query,
    w_key,
    w_value,
    w_out,
    norm_ffn,
    w_router,
    w_gate,
    w_up,
    w_down,
    routes,
):
    ctx_count = lax.axis_size("ctx")
    exp_count = lax.axis_size("exp")
    rows_dev = hit_features.shape[0] // exp_count
    qt, kp, vt = project(hit_features, norm_attn, w_query, w_key, w_value)
    at, wo = attention(qt, kp, vt, w_out)
    own_rows = lax.dynamic_slice_in_dim(
        hit_features, lax.axis_index("exp") * rows_dev, rows_dev, 0
    )
    residual, outgoing, gate_hi, gate_lo = route(
        at.reshape(D, rows_dev), wo.reshape(D, D), own_rows, norm_ffn, w_router, routes
    )
    local_experts = w_gate.shape[0]
    grid = outgoing.reshape(ctx_count, local_experts, -1, D)
    copies = jnp.broadcast_to(grid[:, None], (ctx_count, exp_count) + grid.shape[1:]).reshape(
        (ctx_count * exp_count,) + grid.shape[1:]
    )
    produced = run_experts(
        lax.all_to_all(copies, ("ctx", "exp"), split_axis=0, concat_axis=0, tiled=True),
        w_gate,
        w_up,
        w_down,
    )
    returned = lax.all_to_all(
        produced.astype(BF), ("ctx", "exp"), split_axis=0, concat_axis=0, tiled=True
    ).astype(F32)
    combined = jnp.sum(returned.reshape((ctx_count, exp_count) + grid.shape[1:]), axis=1)
    return pl.pallas_call(
        combine_kernel,
        out_shape=jax.ShapeDtypeStruct((rows_dev, D), BF),
        in_specs=[whole()] * 4,
        out_specs=whole(),
        name="combine",
    )(residual, gate_hi, gate_lo, combined.reshape(outgoing.shape).astype(BF))


def solution(mesh):
    return jax.shard_map(
        body,
        mesh=mesh,
        in_specs=(
            P("ctx", None),
            P(),
            P(None, "exp"),
            P(None, "exp"),
            P(None, "exp"),
            P("exp", None),
            P(),
            P(),
            P("ctx", None, "exp"),
            P("ctx", None, "exp"),
            P("ctx", "exp", None),
            P(("ctx", "exp"), None),
        ),
        out_specs=P(("ctx", "exp"), None),
        check_vma=False,
    )
```

time: 811 us -> 247 us (0.30)
  waiting for transfers between devices: 555 us -> 0 us
  Pallas kernels: 0 us -> 82.8 us
  matrix products: 82.6 us -> 19 us
  blocking collectives: 61.9 us -> 122 us
  other arithmetic: 38.5 us -> 2.04 us
  local copies, waits for them, and re-layouts: 46.3 us -> 19.1 us
  between operations: 13.7 us -> 0.05 us
  starting transfers between devices: 10.3 us -> 0 us
    ppermute x31 -> x0, waiting for transfers between devices: 444 us -> none  [passed_along(): return lax.ppermute(value, axis, pairs)]
    pallas_call x0 -> x4, Pallas kernels: none -> 82.8 us  [the longest x1 72.2 us: attention(): pl.pallas_call(attention_kernel, out_shape=(jax.ShapeDtypeStruct((16, HD,...]
    dot_general x71 -> x2, matrix products: 82.6 us -> 19 us  [the longest x1 12.4 us: run_experts(): jnp.einsum('sjcf,jfd->sjcd', hidden, down_mats, preferred_element_type=F32)]
    all_to_all x0 -> x1, blocking collectives: none -> 61.6 us  [body(): lax.all_to_all(produced.astype(BF), ('ctx', 'exp'), split_axis=0, concat_...]
    reduce_scatter x1 -> x0, waiting for transfers between devices: 58.4 us -> none  [body(): lax.psum_scatter(jnp.dot(attended, w_out, preferred_element_type=jnp.floa...]
    all_to_all x1 -> x0, waiting for transfers between devices: 53.4 us -> none  [body(): lax.all_to_all(produced.astype(jnp.bfloat16), ('ctx', 'exp'), split_axis=...]
    reduce_sum x38 -> x0, other arithmetic: 28.4 us -> none  [the longest x32 22.6 us: attend(): jnp.sum(exp_scores, axis=-1, keepdims=True)]
    while x62 -> x0, local copies, waits for them, and re-layouts: 24.6 us -> none
  transfers between devices with their start and end apart: 33 -> 0, of which waited for: 33 -> 0; matrix products, arithmetic and copies ran while one was open for 0% -> 0% of each run, Pallas kernels for 0% -> 0%
where the time goes in v1:
time: 247 us; the launch traced here: 246 us
  blocking collectives  122 us (49%)
  Pallas kernels  82.8 us (34%)
  local copies, waits for them, and re-layouts  19.1 us (8%)
  matrix products  19 us (8%)
    pallas_call x1, Pallas kernels, attention(): pl.pallas_call(attention_kernel, out_shape=(jax.ShapeDtypeStruct((16, HD,...  72.2 us
    all_to_all x1, blocking collectives, body(): lax.all_to_all(produced.astype(BF), ('ctx', 'exp'), split_axis=0, concat_...  61.6 us
    all_to_all x1, blocking collectives, body(): lax.all_to_all(copies, ('ctx', 'exp'), split_axis=0, concat_axis=0, tiled...  60.9 us
    dot_general x1, matrix products, run_experts(): jnp.einsum('sjcf,jfd->sjcd', hidden, down_mats, preferred_element_type=F32)  12.4 us
    unnamed x20, local copies, waits for them, and re-layouts  11.2 us
    dot_general x1, matrix products, run_experts(): jnp.einsum('sjcd,jdf->sjcf', received, up_mats, preferred_element_type=F32)  6.63 us

profile of v1, /device:TPU:1, one launch (start us, length us, event | category | flops | bytes accessed | tf_op | source)
XLA Modules:
  0.0 245.5 jit_solution(9793313128782947987)
XLA Ops:
  0.0 0.0 copy-start
  0.0 1.6 copy.17.routes_ref
  1.6 1.7 copy.16.wr_ref
  3.3 1.7 constant_dynamic-slice_fusion.hit_ref
  5.0 3.7 %project.1 = (bf16[2,4,64,256]{3,2,1,0:T(8,128)(2,1)}, bf16[4,2,128,128]{3,2,1,0:T(8,128)(2,1)}, bf16[4,2,2,64,128]{4,3,2,1,0:T(8,128)(2,1)}) custom-call(bf16[512,1024]{1,0:T(8,128)(2,1)} %x_ref.1, f32[1,1024]{1,0:T(1,128)} %bitcast.51, bf16[1024,256]{1,0:T(8,128)(2,1)} %wq_ref.1, bf16[1024,256]{1,0:T(8,128)(2,1)} %wk_ref.1, bf16[1024,256]{1,0:T(8,128)(2,1)} %wv_ref.1), custom_call_target="tpu_custom_call" | custom-call | tf_op jit(solution)/shard_map/project/pallas_call | solution.py:55
  8.7 0.0 copy-start.2
  8.7 1.0 copy-done.2
  9.7 0.0 copy-start.4
  9.7 0.9 copy-done.4
  10.7 0.0 copy-start.5
  10.7 0.9 copy-done.5
  11.6 0.0 copy-start.6
  11.6 0.9 copy-done.6
  12.6 72.2 %attention.1 = (bf16[16,64,128]{2,1,0:T(8,128)(2,1)S(1)}, bf16[4,256,1024]{2,1,0:T(8,128)(2,1)S(1)}) custom-call(bf16[2,4,64,256]{3,2,1,0:T(8,128)(2,1)S(1)} %copy-done.4, bf16[4,2,128,128]{3,2,1,0:T(8,128)(2,1)S(1)} %copy-done.5, bf16[4,2,2,64,128]{4,3,2,1,0:T(8,128)(2,1)S(1)} %copy-done.6, bf16[256,1024]{1,0:T(8,128)(2,1)S(1)} %copy-done.2), custom_call_target="tpu_custom_call" | custom-call | tf_op jit(solution)/shard_map/attention/pallas_call | solution.py:388
  84.8 0.0 copy-start.1
  84.8 1.3 copy-done.1
  86.1 0.0 copy-start.3
  86.1 0.7 copy-done.3
  86.8 4.2 %route.1 = (f32[128,1024]{1,0:T(8,128)}, bf16[512,1024]{1,0:T(8,128)(2,1)}, bf16[128,512]{1,0:T(8,128)(2,1)}, bf16[128,512]{1,0:T(8,128)(2,1)}) custom-call(bf16[1024,128]{1,0:T(8,128)(2,1)} %bitcast.47, bf16[1024,1024]{1,0:T(8,128)(2,1)} %bitcast.46, bf16[128,1024]{1,0:T(8,128)(2,1)} %constant_dynamic-slice_fusion.hit_ref, f32[1,1024]{1,0:T(1,128)} %bitcast.52, ...), custom_call_target="tpu_custom_call" | custom-call | tf_op jit(solution)/shard_map/route/pallas_call | solution.py:471
  91.1 1.7 broadcast_in_dim.8
  92.8 0.0 copy-start.8
  92.9 60.9 %all_to_all.10 = bf16[128,2,8,1024]{3,2,1,0:T(8,128)(2,1)S(1)} all-to-all(bf16[128,2,8,1024]{3,2,1,0:T(8,128)(2,1)S(1)} %bitcast.48), channel_id=1, replica_groups=mesh['ctx'=32,'exp'=4] {'ctx','exp'}, dimensions={0} | all-to-all | bytes 8388608 | tf_op jit(solution)/shard_map/all_to_all | solution.py:531
  153.7 0.0 copy-start.7
  153.7 2.0 copy-done.7
  155.7 0.0 copy-done.8
  155.7 6.6 %fusion.4 = f32[2,128,8,512]{3,1,2,0:T(8,128)} fusion(bf16[128,2,8,1024]{3,2,1,0:T(8,128)(2,1)S(1)} %all_to_all.10, bf16[2,1024,512]{2,1,0:T(8,128)(2,1)S(1)} %copy-done.8), kind=kOutput, calls=%fused_computation.9 | convolution fusion | flops 2147483648 | bytes 10485760 | tf_op jit(solution)/shard_map/sjcd,jdf->sjcf/dot_general | solution.py:495
  162.3 0.0 copy-done
  162.3 12.4 %convert_bitcast_fusion = bf16[128,2,8,1024]{3,0,2,1:T(8,128)(2,1)} fusion(f32[2,128,8,512]{3,1,2,0:T(8,128)} %fusion.4, bf16[128,2,8,1024]{3,2,1,0:T(8,128)(2,1)} %copy-done.7, bf16[2,512,1024]{2,1,0:T(8,128)(2,1)S(1)} %copy-done, bf16[2,1024,512]{2,1,0:T(8,128)(2,1)} %param.20), kind=kOutput, calls=%fused_computation.8 | convolution fusion | flops 4303355904 | bytes 16777216 | tf_op jit(solution)/shard_map/sjcf,jfd->sjcd/dot_general | solution.py:497
  174.7 4.5 %copy.19 = bf16[128,2,8,1024]{3,2,1,0:T(8,128)(2,1)S(1)} copy(bf16[128,2,8,1024]{3,0,2,1:T(8,128)(2,1)} %convert_bitcast_fusion) | data formatting | bytes 8388608 | tf_op jit(solution)/shard_map/convert_element_type | solution.py:537
  179.2 61.6 %all_to_all.11 = bf16[128,2,8,1024]{3,2,1,0:T(8,128)(2,1)S(1)} all-to-all(bf16[128,2,8,1024]{3,2,1,0:T(8,128)(2,1)S(1)} %copy.19), channel_id=1, replica_groups=mesh['ctx'=32,'exp'=4] {'ctx','exp'}, dimensions={0} | all-to-all | bytes 8388608 | tf_op jit(solution)/shard_map/all_to_all | solution.py:536
  240.8 2.0 bitcast_reduce_fusion
  242.9 2.7 %combine.1 = bf16[128,1024]{1,0:T(8,128)(2,1)} custom-call(f32[128,1024]{1,0:T(8,128)} %get-tuple-element.19.res_ref, bf16[128,512]{1,0:T(8,128)(2,1)} %get-tuple-element.20.hi_ref, bf16[128,512]{1,0:T(8,128)(2,1)} %get-tuple-element.21.lo_ref, bf16[512,1024]{1,0:T(8,128)(2,1)} %bitcast.49), custom_call_target="tpu_custom_call" | custom-call | tf_op jit(solution)/shard_map/combine/pallas_call | solution.py:540
Async XLA Ops:
  0.0 162.3 %copy-start = (bf16[2,512,1024]{2,1,0:T(8,128)(2,1)S(1)}, bf16[2,512,1024]{2,1,0:T(8,128)(2,1)}, u32[]{:S(2)}) copy-start(bf16[2,512,1024]{2,1,0:T(8,128)(2,1)} %param.22) | copy-start | bytes 6291460
  8.7 1.0 copy-start.2
  9.7 0.9 copy-start.4
  10.7 0.9 copy-start.5
  11.6 0.9 copy-start.6
  84.8 1.3 copy-start.1
  86.1 0.7 copy-start.3
  92.8 62.9 %copy-start.8 = (bf16[2,1024,512]{2,1,0:T(8,128)(2,1)S(1)}, bf16[2,1024,512]{2,1,0:T(8,128)(2,1)}, u32[]{:S(2)}) copy-start(bf16[2,1024,512]{2,1,0:T(8,128)(2,1)} %param.21) | copy-start | bytes 6291460
  153.7 2.0 copy-start.7

commit v2 on v1

--- a/solution.py
+++ b/solution.py
@@ -418,11 +418,58 @@
         compiler_params=pltpu.CompilerParams(
             collective_id=0, has_side_effects=True, vmem_limit_bytes=40 << 20
         ),
+        cost_estimate=pl.CostEstimate(
+            flops=60 * 10**9, bytes_accessed=200 * 10**6, transcendentals=0
+        ),
         name="attention",
     )(qt, kp, vt, wo)
 
 
-def route_kernel(at_ref, wo_ref, hit_ref, gain_ref, wr_ref, routes_ref, res_ref, out_ref, hi_ref, lo_ref):
+def places_of(ctx, exp):
+    return ctx * 2 + exp // 2, exp % 2
+
+
+def peer(i, ctx, exp):
+    ylo, x, z, yhi = ctx // 16, (ctx // 4) % 4, ctx % 4, exp // 2
+    o = (i * 27) % 64
+    to_x = (x + o % 4) % 4
+    to_y = (yhi * 2 + ylo + (o // 4) % 4) % 4
+    to_z = (z + o // 16) % 4
+    to_ctx = (to_y % 2) * 16 + to_x * 4 + to_z
+    return to_ctx * 2 + to_y // 2, (to_ctx, (to_y // 2) * 2 + exp % 2)
+
+
+def greet_peers(barrier, ctx, exp):
+    def greet(i, carry):
+        pl.semaphore_signal(
+            barrier, inc=1, device_id=peer(i, ctx, exp)[1], device_id_type=MESH
+        )
+        return carry
+
+    lax.fori_loop(1, 64, greet, 0)
+
+
+def route_kernel(
+    at_ref,
+    wo_ref,
+    hit_ref,
+    gain_ref,
+    wr_ref,
+    routes_ref,
+    res_ref,
+    hi_ref,
+    lo_ref,
+    got_ref,
+    out,
+    send,
+    recv,
+):
+    ctx = lax.axis_index("ctx")
+    exp = lax.axis_index("exp")
+    place, _ = places_of(ctx, exp)
+    barrier = pltpu.get_barrier_semaphore()
+    greet_peers(barrier, ctx, exp)
+
     mixed = lax.dot_general(
         at_ref[...], wo_ref[...], (((0,), (0,)), ((), ())), preferred_element_type=F32
     )
@@ -430,15 +477,11 @@
     res_ref[...] = residual
     inv = lax.rsqrt(jnp.mean(residual * residual, axis=-1, keepdims=True) + EPSILON)
     normed = (residual * inv * gain_ref[...]).astype(BF)
-    logits = jnp.dot(normed, wr_ref[...], preferred_element_type=F32)
-    rows, experts = logits.shape
+    rows = normed.shape[0]
+    experts, cap = out.shape[0], out.shape[1]
+    places = experts * cap
     ids = lax.broadcasted_iota(jnp.int32, (rows, experts), 1)
     picks = (routes_ref[:, 0:1] == ids) | (routes_ref[:, 1:2] == ids)
-    top = jnp.max(jnp.where(picks, logits, -jnp.inf), axis=-1, keepdims=True)
-    weights = jnp.where(picks, jnp.exp(jnp.where(picks, logits - top, 0.0)), 0.0)
-    gates = weights / jnp.sum(weights, axis=-1, keepdims=True)
-    gate_hi = gates.astype(BF)
-    gate_lo = (gates - gate_hi.astype(F32)).astype(BF)
     marks = jnp.where(picks, 1.0, 0.0).astype(BF)
     before = lax.broadcasted_iota(jnp.int32, (rows, rows), 0) > lax.broadcasted_iota(
         jnp.int32, (rows, rows), 1
@@ -446,8 +489,6 @@
     slots = jnp.dot(
         jnp.where(before, 1.0, 0.0).astype(BF), marks, preferred_element_type=F32
     ).astype(BF)
-    places = out_ref.shape[0]
-    cap = places // experts
     spread = jnp.where(
         lax.broadcasted_iota(jnp.int32, (experts, places), 1) // cap
         == lax.broadcasted_iota(jnp.int32, (experts, places), 0),
@@ -458,43 +499,237 @@
     order = (lax.broadcasted_iota(jnp.int32, (rows, places), 1) % cap).astype(F32)
     here = (wide(marks) > 0.5) & (wide(slots) == order)
     table = jnp.where(here, 1.0, 0.0).astype(BF)
-    out_ref[...] = lax.dot_general(
+    picked = lax.dot_general(
         table, normed, (((0,), (0,)), ((), ())), preferred_element_type=F32
-    ).astype(BF)
+    )
+    out[...] = picked.reshape(out.shape).astype(BF)
+
+    pl.semaphore_wait(barrier, 63)
+
+    def row_copy(i):
+        to, device = peer(i, ctx, exp)
+        return pltpu.make_async_remote_copy(
+            src_ref=out.at[to],
+            dst_ref=got_ref.at[place],
+            send_sem=send.at[i],
+            recv_sem=recv.at[place],
+            device_id=device,
+            device_id_type=MESH,
+        )
+
+    def send_rows(i, carry):
+        row_copy(i).start()
+        return carry
+
+    lax.fori_loop(1, 64, send_rows, 0)
+    pltpu.make_async_copy(out.at[place], got_ref.at[place], recv.at[place]).start()
+
+    logits = jnp.dot(normed, wr_ref[...], preferred_element_type=F32)
+    top = jnp.max(jnp.where(picks, logits, -jnp.inf), axis=-1, keepdims=True)
+    weights = jnp.where(picks, jnp.exp(jnp.where(picks, logits - top, 0.0)), 0.0)
+    gates = weights / jnp.sum(weights, axis=-1, keepdims=True)
+    gate_hi = gates.astype(BF)
+    gate_lo = (gates - gate_hi.astype(F32)).astype(BF)
     hi_ref[...] = jnp.where(here, wide(gate_hi), 0.0).astype(BF)
     lo_ref[...] = jnp.where(here, wide(gate_lo), 0.0).astype(BF)
 
+    def await_rows(i, carry):
+        pltpu.make_async_copy(got_ref.at[i], got_ref.at[i], recv.at[i]).wait()
+        return carry
+
+    lax.fori_loop(0, 64, await_rows, 0)
+
+    def sent_rows(i, carry):
+        row_copy(i).wait_send()
+        return carry
+
+    lax.fori_loop(1, 64, sent_rows, 0)
+
 
 def route(at, wo, hit, gain, wr, routes):
     rows = hit.shape[0]
-    places = wr.shape[1] * 8
+    experts = wr.shape[1]
+    places = experts * 8
     return pl.pallas_call(
         route_kernel,
         out_shape=(
             jax.ShapeDtypeStruct((rows, D), F32),
-            jax.ShapeDtypeStruct((places, D), BF),
             jax.ShapeDtypeStruct((rows, places), BF),
             jax.ShapeDtypeStruct((rows, places), BF),
+            jax.ShapeDtypeStruct((experts, 8, D), BF),
         ),
         in_specs=[whole()] * 6,
-        out_specs=(whole(),) * 4,
+        out_specs=(whole(), whole(), whole(), anywhere()),
+        scratch_shapes=[
+            VMEM((experts, 8, D), BF),
+            pltpu.SemaphoreType.DMA((64,)),
+            pltpu.SemaphoreType.DMA((64,)),
+        ],
+        compiler_params=pltpu.CompilerParams(
+            collective_id=1, has_side_effects=True, vmem_limit_bytes=32 << 20
+        ),
+        cost_estimate=pl.CostEstimate(
+            flops=4 * 10**9, bytes_accessed=40 * 10**6, transcendentals=0
+        ),
         name="route",
     )(at, wo, hit, gain.reshape(1, D), wr, routes)
 
 
-def combine_kernel(res_ref, hi_ref, lo_ref, back_ref, out_ref):
-    back = back_ref[...]
-    mixture = jnp.dot(hi_ref[...], back, preferred_element_type=F32) + jnp.dot(
-        lo_ref[...], back, preferred_element_type=F32
+def expert_kernel(
+    got_ref,
+    res_ref,
+    hi_ref,
+    lo_ref,
+    gate_ref,
+    up_ref,
+    down_ref,
+    gates_ref,
+    ups_ref,
+    downs_ref,
+    out_ref,
+    wg,
+    wu,
+    wd,
+    stage,
+    back,
+    w_sem,
+    send,
+    recv,
+):
+    ctx = lax.axis_index("ctx")
+    exp = lax.axis_index("exp")
+    place, core = places_of(ctx, exp)
+    ylo, x, z, yhi = ctx // 16, (ctx // 4) % 4, ctx % 4, exp // 2
+    barrier = pltpu.get_barrier_semaphore()
+    greet_peers(barrier, ctx, exp)
+
+    loads = []
+    for n, (own, others, held) in enumerate(
+        ((gate_ref, gates_ref, wg), (up_ref, ups_ref, wu), (down_ref, downs_ref, wd))
+    ):
+        for q in range(4):
+            src = own.at[yhi] if q == 0 else others[q - 1]
+            copy = pltpu.make_async_copy(src, held.at[q], w_sem.at[n, q])
+            loads.append((q, n, copy))
+    loads.sort(key=lambda load: load[0])
+    for _, _, copy in loads:
+        copy.start()
+    arrive = {(q, n): copy for q, n, copy in loads}
+
+    def back_copy(g, i):
+        to_z = (z + i % 4) % 4
+        to_x = (x + (i // 4) % 4) % 4
+        to_yhi = (yhi + i // 16) % 2
+        to_ctx = g * 16 + to_x * 4 + to_z
+        to = to_ctx * 2 + to_yhi
+        return to, pltpu.make_async_remote_copy(
+            src_ref=stage.at[to],
+            dst_ref=back.at[place],
+            send_sem=send.at[to],
+            recv_sem=recv.at[place],
+            device_id=(to_ctx, to_yhi * 2 + core),
+            device_id_type=MESH,
+        )
+
+    cap = stage.shape[1]
+    group = 32
+    for g in range(2):
+        rows = (
+            got_ref[g * group : (g + 1) * group]
+            .astype(F32)
+            .reshape(group * cap, D)
+            .astype(BF)
+        )
+        total = None
+        for q in range(4):
+            if g == 0:
+                arrive[(q, 0)].wait()
+                arrive[(q, 1)].wait()
+            gate = jnp.dot(rows, wg[q], preferred_element_type=F32)
+            up = jnp.dot(rows, wu[q], preferred_element_type=F32)
+            hidden = (gate / (1.0 + jnp.exp(-gate)) * up).astype(BF)
+            if g == 0:
+                arrive[(q, 2)].wait()
+            part = jnp.dot(hidden, wd[q], preferred_element_type=F32)
+            total = part if total is None else total + part
+        stage[g * group : (g + 1) * group] = total.reshape(group, cap, D).astype(BF)
+        if g == 0:
+            pl.semaphore_wait(barrier, 63)
+
+        def send_back(i, carry, g=g):
+            to, copy = back_copy(g, i)
+
+            @pl.when(to != place)
+            def _():
+                copy.start()
+
+            return carry
+
+        lax.fori_loop(0, group, send_back, 0)
+
+        @pl.when(ylo == g)
+        def _():
+            pltpu.make_async_copy(stage.at[place], back.at[place], recv.at[place]).start()
+
+    residual = res_ref[...]
+    hi = hi_ref[...]
+    lo = lo_ref[...]
+
+    def await_back(i, carry):
+        pltpu.make_async_copy(back.at[i], back.at[i], recv.at[i]).wait()
+        return carry
+
+    lax.fori_loop(0, 64, await_back, 0)
+    rows = back[...].astype(F32).reshape(64 * cap, D).astype(BF)
+    mixture = jnp.dot(hi, rows, preferred_element_type=F32) + jnp.dot(
+        lo, rows, preferred_element_type=F32
     )
-    out_ref[...] = (res_ref[...] + mixture).astype(BF)
-
-
-def run_experts(received, gate_mats, up_mats, down_mats):
-    gate_act = jnp.einsum("sjcd,jdf->sjcf", received, gate_mats, preferred_element_type=F32)
-    up_act = jnp.einsum("sjcd,jdf->sjcf", received, up_mats, preferred_element_type=F32)
-    hidden = (jax.nn.silu(gate_act) * up_act).astype(BF)
-    return jnp.einsum("sjcf,jfd->sjcd", hidden, down_mats, preferred_element_type=F32)
+    out_ref[...] = (residual + mixture).astype(BF)
+
+    for g in range(2):
+
+        def sent_back(i, carry, g=g):
+            to, copy = back_copy(g, i)
+
+            @pl.when(to != place)
+            def _():
+                copy.wait_send()
+
+            return carry
+
+        lax.fori_loop(0, group, sent_back, 0)
+
+
+def run_experts(got, residual, gate_hi, gate_lo, own, gates, ups, downs):
+    rows = residual.shape[0]
+
+    def kernel(*refs):
+        got_ref, res_ref, hi_ref, lo_ref, gate_ref, up_ref, down_ref = refs[:7]
+        expert_kernel(
+            *refs[:7], refs[7:10], refs[10:13], refs[13:16], *refs[16:]
+        )
+
+    quarter = own[0].shape[2]
+    return pl.pallas_call(
+        kernel,
+        out_shape=jax.ShapeDtypeStruct((rows, D), BF),
+        in_specs=[whole()] * 4 + [anywhere()] * 12,
+        out_specs=whole(),
+        scratch_shapes=[
+            VMEM((4, D, quarter), BF),
+            VMEM((4, D, quarter), BF),
+            VMEM((4, quarter, D), BF),
+            VMEM(got.shape, BF),
+            VMEM(got.shape, BF),
+            pltpu.SemaphoreType.DMA((3, 4)),
+            pltpu.SemaphoreType.DMA((64,)),
+            pltpu.SemaphoreType.DMA((64,)),
+        ],
+        compiler_params=pltpu.CompilerParams(
+            collective_id=2, has_side_effects=True, vmem_limit_bytes=48 << 20
+        ),
+        name="experts",
+    )(got, residual, gate_hi, gate_lo, *own, *gates, *ups, *downs)
 
 
 def body(
@@ -511,39 +746,26 @@
     w_down,
     routes,
 ):
-    ctx_count = lax.axis_size("ctx")
-    exp_count = lax.axis_size("exp")
-    rows_dev = hit_features.shape[0] // exp_count
+    rows_dev = hit_features.shape[0] // lax.axis_size("exp")
+    yhi = lax.axis_index("exp") // 2
+    weights = (w_gate, w_up, w_down)
+    across = [(e, (e + 2) % 4) for e in range(4)]
+    beside = [(e, e + 1 - 2 * (e % 2)) for e in range(4)]
+    pick = lambda w, n: lax.dynamic_index_in_dim(w, n, 0, keepdims=False)
+    far = [lax.ppermute(pick(w, 1 - yhi), "exp", across) for w in weights]
+    near = [lax.ppermute(pick(w, yhi), "exp", beside) for w in weights]
+    diagonal = [lax.ppermute(w, "exp", beside) for w in far]
     qt, kp, vt = project(hit_features, norm_attn, w_query, w_key, w_value)
     at, wo = attention(qt, kp, vt, w_out)
     own_rows = lax.dynamic_slice_in_dim(
         hit_features, lax.axis_index("exp") * rows_dev, rows_dev, 0
     )
-    residual, outgoing, gate_hi, gate_lo = route(
+    residual, gate_hi, gate_lo, got = route(
         at.reshape(D, rows_dev), wo.reshape(D, D), own_rows, norm_ffn, w_router, routes
     )
-    local_experts = w_gate.shape[0]
-    grid = outgoing.reshape(ctx_count, local_experts, -1, D)
-    copies = jnp.broadcast_to(grid[:, None], (ctx_count, exp_count) + grid.shape[1:]).reshape(
-        (ctx_count * exp_count,) + grid.shape[1:]
+    return run_experts(
+        got, residual, gate_hi, gate_lo, weights, *zip(far, near, diagonal)
     )
-    produced = run_experts(
-        lax.all_to_all(copies, ("ctx", "exp"), split_axis=0, concat_axis=0, tiled=True),
-        w_gate,
-        w_up,
-        w_down,
-    )
-    returned = lax.all_to_all(
-        produced.astype(BF), ("ctx", "exp"), split_axis=0, concat_axis=0, tiled=True
-    ).astype(F32)
-    combined = jnp.sum(returned.reshape((ctx_count, exp_count) + grid.shape[1:]), axis=1)
-    return pl.pallas_call(
-        combine_kernel,
-        out_shape=jax.ShapeDtypeStruct((rows_dev, D), BF),
-        in_specs=[whole()] * 4,
-        out_specs=whole(),
-        name="combine",
-    )(residual, gate_hi, gate_lo, combined.reshape(outgoing.shape).astype(BF))
 
 
 def solution(mesh):

time: 247 us -> 212 us (0.86)
  the two profiles are of different devices: /device:TPU:1 before, /device:TPU:8 now
where the time goes in v2:
time: 212 us
  Pallas kernels  129 us (61%)
  waiting for transfers between devices  59 us (28%)
  local copies, waits for them, and re-layouts  17.2 us (8%)
  starting transfers between devices  6.34 us (3%)
    pallas_call x1, Pallas kernels, attention(): pl.pallas_call(attention_kernel, out_shape=(jax.ShapeDtypeStruct((16, HD,...  70.5 us
    ppermute x3, waiting for transfers between devices, body(): far = [lax.ppermute(pick(w, 1 - yhi), 'exp', across) for w in weights]  59 us
    pallas_call x1, Pallas kernels, run_experts(): pl.pallas_call(kernel, out_shape=jax.ShapeDtypeStruct((rows, D), BF), in_...  31.7 us
    pallas_call x1, Pallas kernels, route(): pl.pallas_call(route_kernel, out_shape=(jax.ShapeDtypeStruct((rows, D), F...  23.2 us
    unnamed x27, local copies, waits for them, and re-layouts  10.4 us
    squeeze x3, local copies, waits for them, and re-layouts, body(): pick = lambda w, n: lax.dynamic_index_in_dim(w, n, 0, keepdims=False)  5.84 us
    ppermute x3, starting transfers between devices, body(): far = [lax.ppermute(pick(w, 1 - yhi), 'exp', across) for w in weights]  5.82 us
  transfers between devices with their start and end apart: 9, of which 3 were waited for; matrix products, arithmetic and copies ran while one was open for 2% of the time, Pallas kernels for 46%

profile of v2, /device:TPU:8, one launch (start us, length us, event | category | flops | bytes accessed | tf_op | source)
XLA Modules:
  0.0 211.8 jit_solution(9733124128280054452)
XLA Ops:
  0.0 2.8 %dynamic-slice_bitcast_fusion.4 = (bf16[1024,512]{1,0:T(8,128)(2,1)}, bf16[1024,512]{1,0:T(8,128)(2,1)S(1)}) fusion(bf16[2,1024,512]{2,1,0:T(8,128)(2,1)} %refs_4_.1, s32[]{:T(128)S(6)} %select_n.23, s32[]{:T(128)S(6)} %select_n.22), kind=kLoop, calls=%fused_computation.4 | loop fusion | bytes 4194312 | tf_op jit(solution)/shard_map/jit(dynamic_index_in_dim)/squeeze | solution.py:754
  2.8 2.3 %collective-permute-start = (bf16[1024,512]{1,0:T(8,128)(2,1)S(1)}, bf16[1024,512]{1,0:T(8,128)(2,1)S(1)}, u32[]{:S(2)}, u32[]{:S(2)}) collective-permute-start(bf16[1024,512]{1,0:T(8,128)(2,1)S(1)} %get-tuple-element.28), channel_id=1, source_target_pairs={{0,2},{1,3},{2,0},{3,1},{4,6},{5,7},{6,4},{7,5},{8,10},{9,11},{10,... | collective-permute-start | bytes 3145736 | tf_op jit(solution)/shard_map/ppermute | solution.py:755
  5.1 1.4 dynamic-slice_bitcast_fusion.2
  6.6 1.2 collective-permute-start.3
  7.8 1.6 dynamic-slice_bitcast_fusion
  9.4 2.3 %collective-permute-start.6 = (bf16[512,1024]{1,0:T(8,128)(2,1)}, bf16[512,1024]{1,0:T(8,128)(2,1)}, u32[]{:S(2)}, u32[]{:S(2)}) collective-permute-start(bf16[512,1024]{1,0:T(8,128)(2,1)} %get-tuple-element.24), channel_id=1, source_target_pairs={{0,2},{1,3},{2,0},{3,1},{4,6},{5,7},{6,4},{7,5},{8,10},{9,11},{10,... | collective-permute-start | bytes 3145736 | tf_op jit(solution)/shard_map/ppermute | solution.py:755
  11.7 3.7 %project.1 = (bf16[2,4,64,256]{3,2,1,0:T(8,128)(2,1)}, bf16[4,2,128,128]{3,2,1,0:T(8,128)(2,1)}, bf16[4,2,2,64,128]{4,3,2,1,0:T(8,128)(2,1)}) custom-call(bf16[512,1024]{1,0:T(8,128)(2,1)} %x_ref.1, f32[1,1024]{1,0:T(1,128)} %bitcast.19, bf16[1024,256]{1,0:T(8,128)(2,1)} %wq_ref.1, bf16[1024,256]{1,0:T(8,128)(2,1)} %wk_ref.1, bf16[1024,256]{1,0:T(8,128)(2,1)} %wv_ref.1), custom_call_target="tpu_custom_call" | custom-call | tf_op jit(solution)/shard_map/project/pallas_call | solution.py:55
  15.4 0.0 collective-permute-done.1.refs_8_
  15.4 0.5 collective-permute-start.7
  15.9 14.3 %collective-permute-done.refs_7_ = bf16[1024,512]{1,0:T(8,128)(2,1)S(1)} collective-permute-done((bf16[1024,512]{1,0:T(8,128)(2,1)S(1)}, bf16[1024,512]{1,0:T(8,128)(2,1)S(1)}, u32[]{:S(2)}, u32[]{:S(2)}) %collective-permute-start) | collective-permute-done | bytes 1048608 | tf_op jit(solution)/shard_map/ppermute | solution.py:755
  30.3 0.0 collective-permute-start.2
  30.3 22.6 %collective-permute-done.3.refs_10_ = bf16[1024,512]{1,0:T(8,128)(2,1)} collective-permute-done((bf16[1024,512]{1,0:T(8,128)(2,1)}, bf16[1024,512]{1,0:T(8,128)(2,1)}, u32[]{:S(2)}, u32[]{:S(2)}) %collective-permute-start.3) | collective-permute-done | bytes 1048608 | tf_op jit(solution)/shard_map/ppermute | solution.py:755
  52.9 22.1 %collective-permute-done.6.refs_13_ = bf16[512,1024]{1,0:T(8,128)(2,1)} collective-permute-done((bf16[512,1024]{1,0:T(8,128)(2,1)}, bf16[512,1024]{1,0:T(8,128)(2,1)}, u32[]{:S(2)}, u32[]{:S(2)}) %collective-permute-start.6) | collective-permute-done | bytes 1048608 | tf_op jit(solution)/shard_map/ppermute | solution.py:755
  74.9 0.0 collective-permute-start.8
  74.9 1.0 copy-done
  76.0 0.9 copy-done.1
  76.9 0.9 copy-done.2
  77.9 0.9 copy-done.3
  78.8 70.5 %attention.1 = (bf16[16,64,128]{2,1,0:T(8,128)(2,1)S(1)}, bf16[4,256,1024]{2,1,0:T(8,128)(2,1)S(1)}) custom-call(bf16[2,4,64,256]{3,2,1,0:T(8,128)(2,1)S(1)} %copy-done.1, bf16[4,2,128,128]{3,2,1,0:T(8,128)(2,1)S(1)} %copy-done.2, bf16[4,2,2,64,128]{4,3,2,1,0:T(8,128)(2,1)S(1)} %copy-done.3, bf16[256,1024]{1,0:T(8,128)(2,1)S(1)} %copy-done), custom_call_target="tpu_custom_call" | custom-call | flops 60000002048 | bytes 200000000 | tf_op jit(solution)/shard_map/attention/pallas_call | solution.py:388
  149.3 1.4 copy-done.5
  150.7 0.7 copy-done.7
  151.4 0.1 copy.14.routes_ref
  151.5 1.1 copy.13.wr_ref
  152.6 1.0 constant_dynamic-slice_fusion.hit_ref
  153.6 1.6 copy-done.6
  155.2 0.9 copy-done.8
  156.2 23.2 %route.1 = (f32[128,1024]{1,0:T(8,128)S(1)}, bf16[128,512]{1,0:T(8,128)(2,1)S(1)}, bf16[128,512]{1,0:T(8,128)(2,1)S(1)}, bf16[64,8,1024]{2,1,0:T(8,128)(2,1)S(1)}) custom-call(bf16[1024,128]{1,0:T(8,128)(2,1)S(1)} %bitcast.18, bf16[1024,1024]{1,0:T(8,128)(2,1)S(1)} %bitcast.17, bf16[128,1024]{1,0:T(8,128)(2,1)S(1)} %constant_dynamic-slice_fusion.hit_ref, ...), custom_call_target="tpu_custom_call" | custom-call | flops 4000000000 | bytes 40000000 | tf_op jit(solution)/shard_map/route/pallas_call | solution.py:553
  179.3 0.0 collective-permute-done.7.refs_14_
  179.3 0.0 collective-permute-done.2.refs_9_
  179.4 0.0 collective-permute-done.8.refs_15_
  179.4 31.7 %experts.1 = bf16[128,1024]{1,0:T(8,128)(2,1)S(1)} custom-call(bf16[64,8,1024]{2,1,0:T(8,128)(2,1)S(1)} %get-tuple-element.19.refs_0_, f32[128,1024]{1,0:T(8,128)S(1)} %get-tuple-element.20.refs_1_, bf16[128,512]{1,0:T(8,128)(2,1)S(1)} %get-tuple-element.21.refs_2_, bf16[128,512]{1,0:T(8,128)(2,1)S(1)} %get-tuple-element.22.refs_3_, ...), custom_call_target="tpu_custom_call" | custom-call | tf_op jit(solution)/shard_map/experts/pallas_call | solution.py:713
  211.1 0.7 copy.16
  (21 shorter events, 0.0 us)
Async XLA Ops:
  0.0 5.1 %copy-start.9 = (bf16[2,1024,512]{2,1,0:T(8,128)(2,1)S(1)}, bf16[2,1024,512]{2,1,0:T(8,128)(2,1)}, u32[]{:S(2)}) copy-start(bf16[2,1024,512]{2,1,0:T(8,128)(2,1)} %refs_5_.1) | copy-start | bytes 6291460
  2.8 12.6 %collective-permute-start.1 = (bf16[1024,512]{1,0:T(8,128)(2,1)}, bf16[1024,512]{1,0:T(8,128)(2,1)S(1)}, u32[]{:S(2)}, u32[]{:S(2)}) collective-permute-start(bf16[1024,512]{1,0:T(8,128)(2,1)} %get-tuple-element.27), channel_id=1, source_target_pairs={{0,1},{1,0},{2,3},{3,2},{4,5},{5,4},{6,7},{7,6},{8,9},{9,8},{10,11... | collective-permute-start | bytes 3145736 | tf_op jit(solution)/shard_map/ppermute | solution.py:756
  2.8 5.0 %copy-start.10 = (bf16[2,512,1024]{2,1,0:T(8,128)(2,1)S(1)}, bf16[2,512,1024]{2,1,0:T(8,128)(2,1)}, u32[]{:S(2)}) copy-start(bf16[2,512,1024]{2,1,0:T(8,128)(2,1)} %refs_6_.1) | copy-start | bytes 6291460
  2.8 27.5 %collective-permute-start = (bf16[1024,512]{1,0:T(8,128)(2,1)S(1)}, bf16[1024,512]{1,0:T(8,128)(2,1)S(1)}, u32[]{:S(2)}, u32[]{:S(2)}) collective-permute-start(bf16[1024,512]{1,0:T(8,128)(2,1)S(1)} %get-tuple-element.28), channel_id=1, source_target_pairs={{0,2},{1,3},{2,0},{3,1},{4,6},{5,7},{6,4},{7,5},{8,10},{9,11},{10,... | collective-permute-start | bytes 3145736 | tf_op jit(solution)/shard_map/ppermute | solution.py:755
  6.6 46.3 %collective-permute-start.3 = (bf16[1024,512]{1,0:T(8,128)(2,1)}, bf16[1024,512]{1,0:T(8,128)(2,1)}, u32[]{:S(2)}, u32[]{:S(2)}) collective-permute-start(bf16[1024,512]{1,0:T(8,128)(2,1)} %get-tuple-element.26), channel_id=1, source_target_pairs={{0,2},{1,3},{2,0},{3,1},{4,6},{5,7},{6,4},{7,5},{8,10},{9,11},{10,... | collective-permute-start | bytes 3145736 | tf_op jit(solution)/shard_map/ppermute | solution.py:755
  9.4 65.5 %collective-permute-start.6 = (bf16[512,1024]{1,0:T(8,128)(2,1)}, bf16[512,1024]{1,0:T(8,128)(2,1)}, u32[]{:S(2)}, u32[]{:S(2)}) collective-permute-start(bf16[512,1024]{1,0:T(8,128)(2,1)} %get-tuple-element.24), channel_id=1, source_target_pairs={{0,2},{1,3},{2,0},{3,1},{4,6},{5,7},{6,4},{7,5},{8,10},{9,11},{10,... | collective-permute-start | bytes 3145736 | tf_op jit(solution)/shard_map/ppermute | solution.py:755
  11.7 167.6 %collective-permute-start.4 = (bf16[1024,512]{1,0:T(8,128)(2,1)}, bf16[1024,512]{1,0:T(8,128)(2,1)}, u32[]{:S(2)}, u32[]{:S(2)}) collective-permute-start(bf16[1024,512]{1,0:T(8,128)(2,1)} %get-tuple-element.25), channel_id=1, source_target_pairs={{0,1},{1,0},{2,3},{3,2},{4,5},{5,4},{6,7},{7,6},{8,9},{9,8},{10,11... | collective-permute-start | bytes 3145736 | tf_op jit(solution)/shard_map/ppermute | solution.py:756
  15.4 163.9 %collective-permute-start.7 = (bf16[512,1024]{1,0:T(8,128)(2,1)}, bf16[512,1024]{1,0:T(8,128)(2,1)}, u32[]{:S(2)}, u32[]{:S(2)}) collective-permute-start(bf16[512,1024]{1,0:T(8,128)(2,1)} %get-tuple-element.23), channel_id=1, source_target_pairs={{0,1},{1,0},{2,3},{3,2},{4,5},{5,4},{6,7},{7,6},{8,9},{9,8},{10,11... | collective-permute-start | bytes 3145736 | tf_op jit(solution)/shard_map/ppermute | solution.py:756
  30.3 149.1 %collective-permute-start.2 = (bf16[1024,512]{1,0:T(8,128)(2,1)S(1)}, bf16[1024,512]{1,0:T(8,128)(2,1)S(1)}, u32[]{:S(2)}, u32[]{:S(2)}) collective-permute-start(bf16[1024,512]{1,0:T(8,128)(2,1)S(1)} %collective-permute-done.refs_7_), channel_id=1, source_target_pairs={{0,1},{1,0},{2,3},{3,2},{4,5},{5,4},{6,7},{7,6},{8,9},{9,8},{10,11... | collective-permute-start | bytes 3145736 | tf_op jit(solution)/shard_map/ppermute | solution.py:757
  52.8 126.5 %collective-permute-start.5 = (bf16[1024,512]{1,0:T(8,128)(2,1)}, bf16[1024,512]{1,0:T(8,128)(2,1)}, u32[]{:S(2)}, u32[]{:S(2)}) collective-permute-start(bf16[1024,512]{1,0:T(8,128)(2,1)} %collective-permute-done.3.refs_10_), channel_id=1, source_target_pairs={{0,1},{1,0},{2,3},{3,2},{4,5},{5,4},{6,7},{7,6},{8,9},{9,8},{10,11... | collective-permute-start | bytes 3145736 | tf_op jit(solution)/shard_map/ppermute | solution.py:757
  74.9 104.4 %collective-permute-start.8 = (bf16[512,1024]{1,0:T(8,128)(2,1)}, bf16[512,1024]{1,0:T(8,128)(2,1)}, u32[]{:S(2)}, u32[]{:S(2)}) collective-permute-start(bf16[512,1024]{1,0:T(8,128)(2,1)} %collective-permute-done.6.refs_13_), channel_id=1, source_target_pairs={{0,1},{1,0},{2,3},{3,2},{4,5},{5,4},{6,7},{7,6},{8,9},{9,8},{10,11... | collective-permute-start | bytes 3145736 | tf_op jit(solution)/shard_map/ppermute | solution.py:757
  74.9 1.0 copy-start
  76.0 0.9 copy-start.1
  76.9 0.9 copy-start.2
  77.9 0.9 copy-start.3
  78.8 72.6 %copy-start.11 = (s32[128,2]{0,1:T(2,128)S(1)}, s32[128,2]{0,1:T(2,128)}, u32[]{:S(2)}) copy-start(s32[128,2]{0,1:T(2,128)} %param.23) | copy-start | bytes 3076
  78.8 74.8 %copy-start.4 = (f32[1024]{0:T(1024)S(1)}, f32[1024]{0:T(1024)}, u32[]{:S(2)}) copy-start(f32[1024]{0:T(1024)} %param.18) | copy-start | bytes 12292
  149.3 1.4 copy-start.5
  150.7 0.7 copy-start.7
  153.6 1.6 copy-start.6
  155.2 0.9 copy-start.8

commit v3 on v2

--- a/solution.py
+++ b/solution.py
@@ -27,7 +27,33 @@
     return pl.BlockSpec(memory_space=pl.ANY)
 
 
-def project_kernel(x_ref, gain_ref, wq_ref, wk_ref, wv_ref, qt_ref, kp_ref, vt_ref):
+def project_kernel(
+    x_ref,
+    gain_ref,
+    wq_ref,
+    wk_ref,
+    wv_ref,
+    gate_ref,
+    up_ref,
+    down_ref,
+    qt_ref,
+    kp_ref,
+    vt_ref,
+    pack_ref,
+    held,
+    sem,
+):
+    other = 1 - lax.axis_index("exp") // 2
+    half = pack_ref.shape[2]
+    parts = (
+        (gate_ref.at[other], held.at[0]),
+        (up_ref.at[other], held.at[1]),
+        (down_ref.at[other, :, pl.ds(0, half)], held.at[2, pl.ds(0, half)]),
+        (down_ref.at[other, :, pl.ds(half, half)], held.at[2, pl.ds(half, half)]),
+    )
+    taken = [pltpu.make_async_copy(src, dst, sem.at[n]) for n, (src, dst) in enumerate(parts)]
+    for copy in taken:
+        copy.start()
     x = x_ref[...].astype(F32)
     inv = lax.rsqrt(jnp.mean(x * x, axis=-1, keepdims=True) + EPSILON)
     n = (x * inv * gain_ref[...]).astype(BF)
@@ -38,6 +64,10 @@
             qt_ref[block % 2, head, :, (block // 2) * 128 : (block // 2) * 128 + 128] = qt[
                 head * HD : head * HD + HD, block * 128 : block * 128 + 128
             ]
+    for copy in taken:
+        copy.wait()
+    given = pltpu.make_async_copy(held, pack_ref, sem.at[4])
+    given.start()
     k = jnp.dot(n, wk_ref[...], preferred_element_type=F32)
     for head in range(4):
         for half in range(2):
@@ -49,20 +79,25 @@
             for u in range(2):
                 at = half * 256 + u * 128
                 vt_ref[head, half, u] = vt[head * HD : head * HD + HD, at : at + 128]
-
-
-def project(x, gain, wq, wk, wv):
+    given.wait()
+
+
+def project(x, gain, wq, wk, wv, w_gate, w_up, w_down):
+    packed = (3,) + w_gate.shape[1:]
     return pl.pallas_call(
         project_kernel,
         out_shape=(
             jax.ShapeDtypeStruct((2, 4, HD, 256), BF),
             jax.ShapeDtypeStruct((4, 2, 128, 128), BF),
             jax.ShapeDtypeStruct((4, 2, 2, HD, 128), BF),
-        ),
-        in_specs=[whole()] * 5,
-        out_specs=(whole(), whole(), whole()),
+            jax.ShapeDtypeStruct(packed, BF),
+        ),
+        in_specs=[whole()] * 5 + [anywhere()] * 3,
+        out_specs=(whole(), whole(), whole(), anywhere()),
+        scratch_shapes=[VMEM(packed, BF), pltpu.SemaphoreType.DMA((5,))],
+        compiler_params=pltpu.CompilerParams(vmem_limit_bytes=60 << 20),
         name="project",
-    )(x, gain.reshape(1, D), wq, wk, wv)
+    )(x, gain.reshape(1, D), wq, wk, wv, w_gate, w_up, w_down)
 
 
 def attention_kernel(
@@ -215,19 +250,16 @@
     for copy in to_sibling(0):
         copy.start()
 
-    w_copies = [
-        remote(
-            wo_ref,
-            wo_all_ref.at[exp],
-            w_send.at[step - 1],
-            w_recv.at[step - 1],
-            (ctx, (exp + step) % 4),
-        )
-        for step in range(1, 4)
-    ]
+    far_chip = device(ylo, x, z, 1 - yhi, core)
+    far_exp = (exp + 2) % 4
     w_local = pltpu.make_async_copy(wo_ref, wo_all_ref.at[exp], w_own)
-    for copy in w_copies:
-        copy.start()
+    w_across = remote(wo_ref, wo_all_ref.at[exp], w_send.at[0], w_recv.at[0], far_chip)
+    w_beside = remote(wo_ref, wo_all_ref.at[exp], w_send.at[1], w_recv.at[1], sibling)
+    w_on = remote(
+        wo_all_ref.at[far_exp], wo_all_ref.at[far_exp], w_send.at[2], w_recv.at[2], sibling
+    )
+    w_across.start()
+    w_beside.start()
     w_local.start()
 
     zero = jnp.zeros((HD, 256), BF)
@@ -295,6 +327,8 @@
         def _():
             k_on.wait_recv()
             v_on.wait_recv()
+            w_across.wait_recv()
+            w_on.start()
             for copy in to_sibling(3):
                 copy.start()
 
@@ -371,17 +405,10 @@
         for copy in to_sibling(slot):
             copy.wait_send()
     w_local.wait()
-    for copy in w_copies:
+    w_beside.wait_recv()
+    w_on.wait_recv()
+    for copy in (w_across, w_beside, w_on):
         copy.wait_send()
-    for step in range(1, 4):
-        slot = (exp + 4 - step) % 4
-        remote(
-            wo_ref,
-            wo_all_ref.at[slot],
-            w_send.at[step - 1],
-            w_recv.at[step - 1],
-            (ctx, slot),
-        ).wait_recv()
 
 
 def attention(qt, kp, vt, wo):
@@ -391,7 +418,7 @@
             jax.ShapeDtypeStruct((16, HD, 128), BF),
             jax.ShapeDtypeStruct((4, 256, D), BF),
         ),
-        in_specs=[whole(), whole(), whole(), anywhere()],
+        in_specs=[anywhere()] * 4,
         out_specs=(anywhere(), anywhere()),
         scratch_shapes=[
             VMEM((8, HD, 256), BF),
@@ -416,7 +443,7 @@
             pltpu.SemaphoreType.DMA,
         ],
         compiler_params=pltpu.CompilerParams(
-            collective_id=0, has_side_effects=True, vmem_limit_bytes=40 << 20
+            collective_id=0, has_side_effects=True, vmem_limit_bytes=60 << 20
         ),
         cost_estimate=pl.CostEstimate(
             flops=60 * 10**9, bytes_accessed=200 * 10**6, transcendentals=0
@@ -425,18 +452,17 @@
     )(qt, kp, vt, wo)
 
 
-def places_of(ctx, exp):
-    return ctx * 2 + exp // 2, exp % 2
-
-
-def peer(i, ctx, exp):
+def shifted(o, sign, ctx, exp):
     ylo, x, z, yhi = ctx // 16, (ctx // 4) % 4, ctx % 4, exp // 2
-    o = (i * 27) % 64
-    to_x = (x + o % 4) % 4
-    to_y = (yhi * 2 + ylo + (o // 4) % 4) % 4
-    to_z = (z + o // 16) % 4
+    to_x = (x + 4 + sign * (o % 4)) % 4
+    to_y = (yhi * 2 + ylo + 4 + sign * ((o // 4) % 4)) % 4
+    to_z = (z + 4 + sign * (o // 16)) % 4
     to_ctx = (to_y % 2) * 16 + to_x * 4 + to_z
     return to_ctx * 2 + to_y // 2, (to_ctx, (to_y // 2) * 2 + exp % 2)
+
+
+def peer(i, ctx, exp):
+    return shifted((i * 27) % 64, 1, ctx, exp)
 
 
 def greet_peers(barrier, ctx, exp):
@@ -446,13 +472,16 @@
         )
         return carry
 
+    beside = (ctx, exp + 1 - 2 * (exp % 2))
+    pl.semaphore_signal(barrier, inc=1, device_id=beside, device_id_type=MESH)
     lax.fori_loop(1, 64, greet, 0)
+    return beside
 
 
 def route_kernel(
-    at_ref,
-    wo_ref,
-    hit_ref,
+    at_hbm,
+    wo_hbm,
+    hit_hbm,
     gain_ref,
     wr_ref,
     routes_ref,
@@ -460,57 +489,76 @@
     hi_ref,
     lo_ref,
     got_ref,
+    at_ref,
+    wo_ref,
+    hit_ref,
     out,
+    load,
     send,
     recv,
+    sib_send,
+    sib_recv,
 ):
     ctx = lax.axis_index("ctx")
     exp = lax.axis_index("exp")
-    place, _ = places_of(ctx, exp)
+    place, core = ctx * 2 + exp // 2, exp % 2
+    rows = hit_ref.shape[0]
+    loads = [
+        pltpu.make_async_copy(at_hbm, at_ref, load.at[0]),
+        pltpu.make_async_copy(wo_hbm, wo_ref, load.at[1]),
+        pltpu.make_async_copy(
+            hit_hbm.at[pl.ds(pl.multiple_of(exp * rows, rows), rows)], hit_ref, load.at[2]
+        ),
+    ]
+    for copy in loads:
+        copy.start()
     barrier = pltpu.get_barrier_semaphore()
-    greet_peers(barrier, ctx, exp)
-
+    beside = greet_peers(barrier, ctx, exp)
+
+    experts, cap = out.shape[0], out.shape[1]
+    places = experts * cap
+    ids = lax.broadcasted_iota(jnp.int32, (experts, rows), 0)
+    picks = (routes_ref[0:1, :] == ids) | (routes_ref[1:2, :] == ids)
+    marks = jnp.where(picks, 1.0, 0.0).astype(BF)
+    before = lax.broadcasted_iota(jnp.int32, (rows, rows), 0) < lax.broadcasted_iota(
+        jnp.int32, (rows, rows), 1
+    )
+    slots = jnp.dot(
+        marks, jnp.where(before, 1.0, 0.0).astype(BF), preferred_element_type=F32
+    ).astype(BF)
+    spread = jnp.where(
+        lax.broadcasted_iota(jnp.int32, (places, experts), 0) // cap
+        == lax.broadcasted_iota(jnp.int32, (places, experts), 1),
+        1.0,
+        0.0,
+    ).astype(BF)
+    wide = lambda v: jnp.dot(spread, v, preferred_element_type=F32)
+    order = (lax.broadcasted_iota(jnp.int32, (places, rows), 0) % cap).astype(F32)
+    here = (wide(marks) > 0.5) & (wide(slots) == order)
+    table = jnp.where(here, 1.0, 0.0).astype(BF)
+
+    for copy in loads:
+        copy.wait()
     mixed = lax.dot_general(
-        at_ref[...], wo_ref[...], (((0,), (0,)), ((), ())), preferred_element_type=F32
+        at_ref[...].reshape(D, rows),
+        wo_ref[...].reshape(D, D),
+        (((0,), (0,)), ((), ())),
+        preferred_element_type=F32,
     )
     residual = hit_ref[...].astype(F32) + mixed
     res_ref[...] = residual
     inv = lax.rsqrt(jnp.mean(residual * residual, axis=-1, keepdims=True) + EPSILON)
     normed = (residual * inv * gain_ref[...]).astype(BF)
-    rows = normed.shape[0]
-    experts, cap = out.shape[0], out.shape[1]
-    places = experts * cap
-    ids = lax.broadcasted_iota(jnp.int32, (rows, experts), 1)
-    picks = (routes_ref[:, 0:1] == ids) | (routes_ref[:, 1:2] == ids)
-    marks = jnp.where(picks, 1.0, 0.0).astype(BF)
-    before = lax.broadcasted_iota(jnp.int32, (rows, rows), 0) > lax.broadcasted_iota(
-        jnp.int32, (rows, rows), 1
-    )
-    slots = jnp.dot(
-        jnp.where(before, 1.0, 0.0).astype(BF), marks, preferred_element_type=F32
-    ).astype(BF)
-    spread = jnp.where(
-        lax.broadcasted_iota(jnp.int32, (experts, places), 1) // cap
-        == lax.broadcasted_iota(jnp.int32, (experts, places), 0),
-        1.0,
-        0.0,
-    ).astype(BF)
-    wide = lambda v: jnp.dot(v, spread, preferred_element_type=F32)
-    order = (lax.broadcasted_iota(jnp.int32, (rows, places), 1) % cap).astype(F32)
-    here = (wide(marks) > 0.5) & (wide(slots) == order)
-    table = jnp.where(here, 1.0, 0.0).astype(BF)
-    picked = lax.dot_general(
-        table, normed, (((0,), (0,)), ((), ())), preferred_element_type=F32
-    )
+    picked = jnp.dot(table, normed, preferred_element_type=F32)
     out[...] = picked.reshape(out.shape).astype(BF)
 
-    pl.semaphore_wait(barrier, 63)
+    pl.semaphore_wait(barrier, 64)
 
     def row_copy(i):
         to, device = peer(i, ctx, exp)
         return pltpu.make_async_remote_copy(
             src_ref=out.at[to],
-            dst_ref=got_ref.at[place],
+            dst_ref=got_ref.at[core, place],
             send_sem=send.at[i],
             recv_sem=recv.at[place],
             device_id=device,
@@ -522,22 +570,44 @@
         return carry
 
     lax.fori_loop(1, 64, send_rows, 0)
-    pltpu.make_async_copy(out.at[place], got_ref.at[place], recv.at[place]).start()
-
-    logits = jnp.dot(normed, wr_ref[...], preferred_element_type=F32)
-    top = jnp.max(jnp.where(picks, logits, -jnp.inf), axis=-1, keepdims=True)
+    pltpu.make_async_copy(out.at[place], got_ref.at[core, place], recv.at[place]).start()
+
+    logits = lax.dot_general(
+        wr_ref[...], normed, (((1,), (1,)), ((), ())), preferred_element_type=F32
+    )
+    top = jnp.max(jnp.where(picks, logits, -jnp.inf), axis=0, keepdims=True)
     weights = jnp.where(picks, jnp.exp(jnp.where(picks, logits - top, 0.0)), 0.0)
-    gates = weights / jnp.sum(weights, axis=-1, keepdims=True)
+    gates = weights / jnp.sum(weights, axis=0, keepdims=True)
     gate_hi = gates.astype(BF)
     gate_lo = (gates - gate_hi.astype(F32)).astype(BF)
     hi_ref[...] = jnp.where(here, wide(gate_hi), 0.0).astype(BF)
     lo_ref[...] = jnp.where(here, wide(gate_lo), 0.0).astype(BF)
 
-    def await_rows(i, carry):
-        pltpu.make_async_copy(got_ref.at[i], got_ref.at[i], recv.at[i]).wait()
-        return carry
-
-    lax.fori_loop(0, 64, await_rows, 0)
+    def beside_copy(n, of):
+        return pltpu.make_async_remote_copy(
+            src_ref=got_ref.at[of, n],
+            dst_ref=got_ref.at[of, n],
+            send_sem=sib_send.at[n],
+            recv_sem=sib_recv.at[n],
+            device_id=beside,
+            device_id_type=MESH,
+        )
+
+    def pass_on(i, carry):
+        n, _ = shifted((i * 27) % 64, -1, ctx, exp)
+        block = got_ref.at[core, n]
+        pltpu.make_async_copy(block, block, recv.at[n]).wait()
+        beside_copy(n, core).start()
+        return carry
+
+    lax.fori_loop(0, 64, pass_on, 0)
+
+    def finish(i, carry):
+        beside_copy(i, 1 - core).wait_recv()
+        beside_copy(i, core).wait_send()
+        return carry
+
+    lax.fori_loop(0, 64, finish, 0)
 
     def sent_rows(i, carry):
         row_copy(i).wait_send()
@@ -547,26 +617,32 @@
 
 
 def route(at, wo, hit, gain, wr, routes):
-    rows = hit.shape[0]
-    experts = wr.shape[1]
+    experts = wr.shape[0]
+    rows = routes.shape[1]
     places = experts * 8
     return pl.pallas_call(
         route_kernel,
         out_shape=(
             jax.ShapeDtypeStruct((rows, D), F32),
-            jax.ShapeDtypeStruct((rows, places), BF),
-            jax.ShapeDtypeStruct((rows, places), BF),
-            jax.ShapeDtypeStruct((experts, 8, D), BF),
-        ),
-        in_specs=[whole()] * 6,
+            jax.ShapeDtypeStruct((places, rows), BF),
+            jax.ShapeDtypeStruct((places, rows), BF),
+            jax.ShapeDtypeStruct((2, experts, 8, D), BF),
+        ),
+        in_specs=[anywhere()] * 3 + [whole()] * 3,
         out_specs=(whole(), whole(), whole(), anywhere()),
         scratch_shapes=[
+            VMEM(at.shape, BF),
+            VMEM(wo.shape, BF),
+            VMEM((rows, D), BF),
             VMEM((experts, 8, D), BF),
+            pltpu.SemaphoreType.DMA((3,)),
+            pltpu.SemaphoreType.DMA((64,)),
+            pltpu.SemaphoreType.DMA((64,)),
             pltpu.SemaphoreType.DMA((64,)),
             pltpu.SemaphoreType.DMA((64,)),
         ],
         compiler_params=pltpu.CompilerParams(
-            collective_id=1, has_side_effects=True, vmem_limit_bytes=32 << 20
+            collective_id=1, has_side_effects=True, vmem_limit_bytes=60 << 20
         ),
         cost_estimate=pl.CostEstimate(
             flops=4 * 10**9, bytes_accessed=40 * 10**6, transcendentals=0
@@ -576,45 +652,65 @@
 
 
 def expert_kernel(
-    got_ref,
+    got_hbm,
     res_ref,
     hi_ref,
     lo_ref,
     gate_ref,
     up_ref,
     down_ref,
-    gates_ref,
-    ups_ref,
-    downs_ref,
+    far_ref,
     out_ref,
+    got,
     wg,
     wu,
     wd,
+    give,
+    take,
     stage,
     back,
     w_sem,
+    g_sem,
     send,
     recv,
+    p_send,
+    p_recv,
 ):
     ctx = lax.axis_index("ctx")
     exp = lax.axis_index("exp")
-    place, core = places_of(ctx, exp)
+    place, core = ctx * 2 + exp // 2, exp % 2
     ylo, x, z, yhi = ctx // 16, (ctx // 4) % 4, ctx % 4, exp // 2
+    half = far_ref.shape[2]
+    got_in = [
+        pltpu.make_async_copy(got_hbm.at[1 - core], got.at[0], g_sem.at[0]),
+        pltpu.make_async_copy(got_hbm.at[core], got.at[1], g_sem.at[1]),
+    ]
+    low, high = pl.ds(0, half), pl.ds(half, half)
+    loads = [
+        [
+            (gate_ref.at[yhi], wg.at[0]),
+            (far_ref.at[0], wg.at[1]),
+        ],
+        [
+            (up_ref.at[yhi], wu.at[0]),
+            (far_ref.at[1], wu.at[1]),
+        ],
+        [
+            (down_ref.at[yhi], wd.at[0]),
+            (far_ref.at[2, low], wd.at[1, :, low]),
+            (far_ref.at[2, high], wd.at[1, :, high]),
+        ],
+    ]
+    loads = [
+        [pltpu.make_async_copy(src, dst, w_sem.at[n, q]) for q, (src, dst) in enumerate(group)]
+        for n, group in enumerate(loads)
+    ]
+    got_in[0].start()
+    for n, q in ((0, 0), (1, 0), (2, 0), (0, 1), (1, 1), (2, 1), (2, 2)):
+        loads[n][q].start()
+    got_in[1].start()
     barrier = pltpu.get_barrier_semaphore()
-    greet_peers(barrier, ctx, exp)
-
-    loads = []
-    for n, (own, others, held) in enumerate(
-        ((gate_ref, gates_ref, wg), (up_ref, ups_ref, wu), (down_ref, downs_ref, wd))
-    ):
-        for q in range(4):
-            src = own.at[yhi] if q == 0 else others[q - 1]
-            copy = pltpu.make_async_copy(src, held.at[q], w_sem.at[n, q])
-            loads.append((q, n, copy))
-    loads.sort(key=lambda load: load[0])
-    for _, _, copy in loads:
-        copy.start()
-    arrive = {(q, n): copy for q, n, copy in loads}
+    beside = greet_peers(barrier, ctx, exp)
 
     def back_copy(g, i):
         to_z = (z + i % 4) % 4
@@ -631,30 +727,54 @@
             device_id_type=MESH,
         )
 
+    def part_copy(g):
+        return pltpu.make_async_remote_copy(
+            src_ref=give.at[g],
+            dst_ref=take.at[g],
+            send_sem=p_send.at[g],
+            recv_sem=p_recv.at[g],
+            device_id=beside,
+            device_id_type=MESH,
+        )
+
     cap = stage.shape[1]
     group = 32
-    for g in range(2):
+
+    def partial(whose, g, first):
         rows = (
-            got_ref[g * group : (g + 1) * group]
+            got[whose, g * group : (g + 1) * group]
             .astype(F32)
             .reshape(group * cap, D)
             .astype(BF)
         )
         total = None
-        for q in range(4):
-            if g == 0:
-                arrive[(q, 0)].wait()
-                arrive[(q, 1)].wait()
+        for q in range(2):
+            if first:
+                loads[0][q].wait()
+                loads[1][q].wait()
             gate = jnp.dot(rows, wg[q], preferred_element_type=F32)
             up = jnp.dot(rows, wu[q], preferred_element_type=F32)
             hidden = (gate / (1.0 + jnp.exp(-gate)) * up).astype(BF)
-            if g == 0:
-                arrive[(q, 2)].wait()
+            if first:
+                for copy in loads[2][q:] if q else loads[2][:1]:
+                    copy.wait()
             part = jnp.dot(hidden, wd[q], preferred_element_type=F32)
             total = part if total is None else total + part
-        stage[g * group : (g + 1) * group] = total.reshape(group, cap, D).astype(BF)
+        return total
+
+    for g in range(2):
         if g == 0:
-            pl.semaphore_wait(barrier, 63)
+            got_in[0].wait()
+        give[g] = partial(0, g, g == 0).reshape(group, cap, D).astype(BF)
+        if g == 0:
+            pl.semaphore_wait(barrier, 64)
+            got_in[1].wait()
+        part_copy(g).start()
+    for g in range(2):
+        total = partial(1, g, False)
+        part_copy(g).wait_recv()
+        both = total + take[g].astype(F32).reshape(group * cap, D)
+        stage[g * group : (g + 1) * group] = both.reshape(group, cap, D).astype(BF)
 
         def send_back(i, carry, g=g):
             to, copy = back_copy(g, i)
@@ -672,8 +792,6 @@
             pltpu.make_async_copy(stage.at[place], back.at[place], recv.at[place]).start()
 
     residual = res_ref[...]
-    hi = hi_ref[...]
-    lo = lo_ref[...]
 
     def await_back(i, carry):
         pltpu.make_async_copy(back.at[i], back.at[i], recv.at[i]).wait()
@@ -681,9 +799,10 @@
 
     lax.fori_loop(0, 64, await_back, 0)
     rows = back[...].astype(F32).reshape(64 * cap, D).astype(BF)
-    mixture = jnp.dot(hi, rows, preferred_element_type=F32) + jnp.dot(
-        lo, rows, preferred_element_type=F32
-    )
+    over = (((0,), (0,)), ((), ()))
+    mixture = lax.dot_general(
+        hi_ref[...], rows, over, preferred_element_type=F32
+    ) + lax.dot_general(lo_ref[...], rows, over, preferred_element_type=F32)
     out_ref[...] = (residual + mixture).astype(BF)
 
     for g in range(2):
@@ -698,38 +817,38 @@
             return carry
 
         lax.fori_loop(0, group, sent_back, 0)
-
-
-def run_experts(got, residual, gate_hi, gate_lo, own, gates, ups, downs):
+        part_copy(g).wait_send()
+
+
+def run_experts(got, residual, gate_hi, gate_lo, w_gate, w_up, w_down, far):
     rows = residual.shape[0]
-
-    def kernel(*refs):
-        got_ref, res_ref, hi_ref, lo_ref, gate_ref, up_ref, down_ref = refs[:7]
-        expert_kernel(
-            *refs[:7], refs[7:10], refs[10:13], refs[13:16], *refs[16:]
-        )
-
-    quarter = own[0].shape[2]
+    quarter = w_gate.shape[2]
     return pl.pallas_call(
-        kernel,
+        expert_kernel,
         out_shape=jax.ShapeDtypeStruct((rows, D), BF),
-        in_specs=[whole()] * 4 + [anywhere()] * 12,
+        in_specs=[anywhere()] + [whole()] * 3 + [anywhere()] * 4,
         out_specs=whole(),
         scratch_shapes=[
-            VMEM((4, D, quarter), BF),
-            VMEM((4, D, quarter), BF),
-            VMEM((4, quarter, D), BF),
             VMEM(got.shape, BF),
-            VMEM(got.shape, BF),
-            pltpu.SemaphoreType.DMA((3, 4)),
+            VMEM((2, D, quarter), BF),
+            VMEM((2, D, quarter), BF),
+            VMEM((2, quarter, D), BF),
+            VMEM((2, 32) + got.shape[2:], BF),
+            VMEM((2, 32) + got.shape[2:], BF),
+            VMEM(got.shape[1:], BF),
+            VMEM(got.shape[1:], BF),
+            pltpu.SemaphoreType.DMA((3, 3)),
+            pltpu.SemaphoreType.DMA((2,)),
             pltpu.SemaphoreType.DMA((64,)),
             pltpu.SemaphoreType.DMA((64,)),
+            pltpu.SemaphoreType.DMA((2,)),
+            pltpu.SemaphoreType.DMA((2,)),
         ],
         compiler_params=pltpu.CompilerParams(
-            collective_id=2, has_side_effects=True, vmem_limit_bytes=48 << 20
+            collective_id=2, has_side_effects=True, vmem_limit_bytes=52 << 20
         ),
         name="experts",
-    )(got, residual, gate_hi, gate_lo, *own, *gates, *ups, *downs)
+    )(got, residual, gate_hi, gate_lo, w_gate, w_up, w_down, far)
 
 
 def body(
@@ -746,26 +865,15 @@
     w_down,
     routes,
 ):
-    rows_dev = hit_features.shape[0] // lax.axis_size("exp")
-    yhi = lax.axis_index("exp") // 2
-    weights = (w_gate, w_up, w_down)
-    across = [(e, (e + 2) % 4) for e in range(4)]
-    beside = [(e, e + 1 - 2 * (e % 2)) for e in range(4)]
-    pick = lambda w, n: lax.dynamic_index_in_dim(w, n, 0, keepdims=False)
-    far = [lax.ppermute(pick(w, 1 - yhi), "exp", across) for w in weights]
-    near = [lax.ppermute(pick(w, yhi), "exp", beside) for w in weights]
-    diagonal = [lax.ppermute(w, "exp", beside) for w in far]
-    qt, kp, vt = project(hit_features, norm_attn, w_query, w_key, w_value)
+    qt, kp, vt, packed = project(
+        hit_features, norm_attn, w_query, w_key, w_value, w_gate, w_up, w_down
+    )
+    far = lax.ppermute(packed, "exp", [(e, (e + 2) % 4) for e in range(4)])
     at, wo = attention(qt, kp, vt, w_out)
-    own_rows = lax.dynamic_slice_in_dim(
-        hit_features, lax.axis_index("exp") * rows_dev, rows_dev, 0
+    residual, gate_hi, gate_lo, got = route(
+        at, wo, hit_features, norm_ffn, w_router.T, routes.T
     )
-    residual, gate_hi, gate_lo, got = route(
-        at.reshape(D, rows_dev), wo.reshape(D, D), own_rows, norm_ffn, w_router, routes
-    )
-    return run_experts(
-        got, residual, gate_hi, gate_lo, weights, *zip(far, near, diagonal)
-    )
+    return run_experts(got, residual, gate_hi, gate_lo, w_gate, w_up, w_down, far)
 
 
 def solution(mesh):

time: 212 us -> 209 us (0.986)
  Pallas kernels: 129 us -> 201 us
  waiting for transfers between devices: 59 us -> 0.01 us
  local copies, waits for them, and re-layouts: 17.2 us -> 5.19 us
  starting transfers between devices: 6.34 us -> 2.37 us
    pallas_call x1, Pallas kernels: 70.5 us -> 131 us  [attention(): pl.pallas_call(attention_kernel, out_shape=(jax.ShapeDtypeStruct((16, HD,...]
    ppermute x9 -> x1, waiting for transfers between devices: 59 us -> 0.01 us  [body(): far = lax.ppermute(packed, 'exp', [(e, (e + 2) % 4) for e in range(4)])]
    squeeze x3 -> x0, local copies, waits for them, and re-layouts: 5.84 us -> none  [body(): pick = lambda w, n: lax.dynamic_index_in_dim(w, n, 0, keepdims=False)]
    unnamed x27 -> x9, local copies, waits for them, and re-layouts: 10.4 us -> 5.19 us
    pallas_call x1, Pallas kernels: 23.2 us -> 28 us  [route(): pl.pallas_call(route_kernel, out_shape=(jax.ShapeDtypeStruct((rows, D), F...]
    ppermute x9 -> x1, starting transfers between devices: 6.34 us -> 2.37 us  [body(): far = lax.ppermute(packed, 'exp', [(e, (e + 2) % 4) for e in range(4)])]
    pallas_call x1, Pallas kernels: 31.7 us -> 35.3 us  [run_experts(): pl.pallas_call(expert_kernel, out_shape=jax.ShapeDtypeStruct((rows, D), B...]
    pallas_call x1, Pallas kernels: 3.74 us -> 6.09 us  [project(): pl.pallas_call(project_kernel, out_shape=(jax.ShapeDtypeStruct((2, 4, HD,...]
  transfers between devices with their start and end apart: 9 -> 1, of which waited for: 3 -> 0; matrix products, arithmetic and copies ran while one was open for 2% -> 0% of each run, Pallas kernels for 46% -> 77%
where the time goes in v3:
time: 209 us
  Pallas kernels  201 us (96%)
  local copies, waits for them, and re-layouts  5.19 us (2%)
  starting transfers between devices  2.37 us (1%)
    pallas_call x1, Pallas kernels, attention(): pl.pallas_call(attention_kernel, out_shape=(jax.ShapeDtypeStruct((16, HD,...  131 us
    pallas_call x1, Pallas kernels, run_experts(): pl.pallas_call(expert_kernel, out_shape=jax.ShapeDtypeStruct((rows, D), B...  35.3 us
    pallas_call x1, Pallas kernels, route(): pl.pallas_call(route_kernel, out_shape=(jax.ShapeDtypeStruct((rows, D), F...  28 us
    pallas_call x1, Pallas kernels, project(): pl.pallas_call(project_kernel, out_shape=(jax.ShapeDtypeStruct((2, 4, HD,...  6.09 us
    unnamed x9, local copies, waits for them, and re-layouts  5.19 us
  transfers between devices with their start and end apart: 1, of which 0 were waited for; matrix products, arithmetic and copies ran while one was open for 0% of the time, Pallas kernels for 77%

profile of v3, /device:TPU:8, one launch (start us, length us, event | category | flops | bytes accessed | tf_op | source)
XLA Modules:
  0.0 208.5 jit_solution(13218009292663702976)
XLA Ops:
  0.0 6.1 %project.1 = (bf16[2,4,64,256]{3,2,1,0:T(8,128)(2,1)}, bf16[4,2,128,128]{3,2,1,0:T(8,128)(2,1)}, bf16[4,2,2,64,128]{4,3,2,1,0:T(8,128)(2,1)}, bf16[3,1024,512]{2,1,0:T(8,128)(2,1)}) custom-call(bf16[512,1024]{1,0:T(8,128)(2,1)} %hit_hbm.1, f32[1,1024]{1,0:T(1,128)} %bitcast.4, bf16[1024,256]{1,0:T(8,128)(2,1)} %wq_ref.1, bf16[1024,256]{1,0:T(8,128)(2,1)} %wk_ref.1, ...), custom_call_target="tpu_custom_call" | custom-call | tf_op jit(solution)/shard_map/project/pallas_call | solution.py:87
  6.1 2.4 %collective-permute-start = (bf16[3,1024,512]{2,1,0:T(8,128)(2,1)}, bf16[3,1024,512]{2,1,0:T(8,128)(2,1)S(1)}, u32[]{:S(2)}, u32[]{:S(2)}) collective-permute-start(bf16[3,1024,512]{2,1,0:T(8,128)(2,1)} %get-tuple-element.24), channel_id=1, source_target_pairs={{0,2},{1,3},{2,0},{3,1},{4,6},{5,7},{6,4},{7,5},{8,10},{9,11},{10,... | collective-permute-start | bytes 9437192 | tf_op jit(solution)/shard_map/ppermute | solution.py:871
  8.5 131.5 %attention.1 = (bf16[16,64,128]{2,1,0:T(8,128)(2,1)}, bf16[4,256,1024]{2,1,0:T(8,128)(2,1)}) custom-call(bf16[2,4,64,256]{3,2,1,0:T(8,128)(2,1)} %get-tuple-element.15.qt_ref, bf16[4,2,128,128]{3,2,1,0:T(8,128)(2,1)} %get-tuple-element.16.kp_ref, bf16[4,2,2,64,128]{4,3,2,1,0:T(8,128)(2,1)} %get-tuple-element.17.vt_ref, bf16[256,1024]{1,0:T(8,128)(2,1)} %wo_ref.1), custom_call_target="tpu_custom_call" | custom-call | flops 60000002048 | bytes 200000000 | tf_op jit(solution)/shard_map/attention/pallas_call | solution.py:415
  140.0 28.0 %route.1 = (f32[128,1024]{1,0:T(8,128)}, bf16[512,128]{1,0:T(8,128)(2,1)}, bf16[512,128]{1,0:T(8,128)(2,1)}, bf16[2,64,8,1024]{3,2,1,0:T(8,128)(2,1)}) custom-call(bf16[16,64,128]{2,1,0:T(8,128)(2,1)} %get-tuple-element.18.at_hbm, bf16[4,256,1024]{2,1,0:T(8,128)(2,1)} %get-tuple-element.19.wo_hbm, bf16[512,1024]{1,0:T(8,128)(2,1)} %hit_hbm.1, ...), custom_call_target="tpu_custom_call" | custom-call | flops 4000000000 | bytes 40000000 | tf_op jit(solution)/shard_map/route/pallas_call | solution.py:623
  168.0 0.0 collective-permute-done.far_ref
  168.0 0.0 copy-start.3
  168.0 1.6 copy-done.3
  169.7 0.0 copy-start
  169.7 1.0 copy-done
  170.7 0.0 copy-start.1
  170.7 0.9 copy-done.1
  171.6 0.0 copy-start.2
  171.6 0.9 copy-done.2
  172.5 35.3 %experts.1 = bf16[128,1024]{1,0:T(8,128)(2,1)S(1)} custom-call(bf16[2,64,8,1024]{3,2,1,0:T(8,128)(2,1)} %get-tuple-element.20.got_hbm, f32[128,1024]{1,0:T(8,128)S(1)} %copy-done, bf16[512,128]{1,0:T(8,128)(2,1)S(1)} %copy-done.1, bf16[512,128]{1,0:T(8,128)(2,1)S(1)} %copy-done.2, bf16[2,1024,512]{2,1,0:T(8,128)(2,1)} %gate_ref.3, ...), custom_call_target="tpu_custom_call" | custom-call | tf_op jit(solution)/shard_map/experts/pallas_call | solution.py:826
  207.8 0.7 copy.14
Async XLA Ops:
  6.1 161.9 %collective-permute-start = (bf16[3,1024,512]{2,1,0:T(8,128)(2,1)}, bf16[3,1024,512]{2,1,0:T(8,128)(2,1)S(1)}, u32[]{:S(2)}, u32[]{:S(2)}) collective-permute-start(bf16[3,1024,512]{2,1,0:T(8,128)(2,1)} %get-tuple-element.24), channel_id=1, source_target_pairs={{0,2},{1,3},{2,0},{3,1},{4,6},{5,7},{6,4},{7,5},{8,10},{9,11},{10,... | collective-permute-start | bytes 9437192 | tf_op jit(solution)/shard_map/ppermute | solution.py:871
  168.0 1.6 copy-start.3
  169.7 1.0 copy-start
  170.7 0.9 copy-start.1
  171.6 0.9 copy-start.2

commit v4 on v1

--- a/solution.py
+++ b/solution.py
@@ -70,8 +70,14 @@
     kp_ref,
     vt_ref,
     wo_ref,
+    gate_ref,
+    up_ref,
+    down_ref,
     at_ref,
     wo_all_ref,
+    gates_ref,
+    ups_ref,
+    downs_ref,
     qg,
     kg,
     vg,
@@ -92,6 +98,8 @@
     w_send,
     w_recv,
     w_own,
+    e_send,
+    e_recv,
 ):
     ctx = lax.axis_index("ctx")
     exp = lax.axis_index("exp")
@@ -215,20 +223,25 @@
     for copy in to_sibling(0):
         copy.start()
 
-    w_copies = [
-        remote(
-            wo_ref,
-            wo_all_ref.at[exp],
-            w_send.at[step - 1],
-            w_recv.at[step - 1],
-            (ctx, (exp + step) % 4),
-        )
-        for step in range(1, 4)
+    far_chip = device(ylo, x, z, 1 - yhi, core)
+    far_exp = (exp + 2) % 4
+    w_local = pltpu.make_async_copy(wo_ref, wo_all_ref.at[exp], w_own)
+    w_across = remote(wo_ref, wo_all_ref.at[exp], w_send.at[0], w_recv.at[0], far_chip)
+    w_beside = remote(wo_ref, wo_all_ref.at[exp], w_send.at[1], w_recv.at[1], sibling)
+    w_on = remote(
+        wo_all_ref.at[far_exp], wo_all_ref.at[far_exp], w_send.at[2], w_recv.at[2], sibling
+    )
+    w_across.start()
+    w_beside.start()
+    w_local.start()
+    e_beside = [
+        remote(src, dst, e_send.at[n], e_recv.at[n], sibling)
+        for n, (src, dst) in enumerate(
+            ((gate_ref, gates_ref), (up_ref, ups_ref), (down_ref, downs_ref))
+        )
     ]
-    w_local = pltpu.make_async_copy(wo_ref, wo_all_ref.at[exp], w_own)
-    for copy in w_copies:
+    for copy in e_beside:
         copy.start()
-    w_local.start()
 
     zero = jnp.zeros((HD, 256), BF)
     for j in range(8):
@@ -295,6 +308,8 @@
         def _():
             k_on.wait_recv()
             v_on.wait_recv()
+            w_across.wait_recv()
+            w_on.start()
             for copy in to_sibling(3):
                 copy.start()
 
@@ -371,28 +386,24 @@
         for copy in to_sibling(slot):
             copy.wait_send()
     w_local.wait()
-    for copy in w_copies:
+    w_beside.wait_recv()
+    w_on.wait_recv()
+    for copy in (w_across, w_beside, w_on):
         copy.wait_send()
-    for step in range(1, 4):
-        slot = (exp + 4 - step) % 4
-        remote(
-            wo_ref,
-            wo_all_ref.at[slot],
-            w_send.at[step - 1],
-            w_recv.at[step - 1],
-            (ctx, slot),
-        ).wait_recv()
-
-
-def attention(qt, kp, vt, wo):
+    for copy in e_beside:
+        copy.wait()
+
+
+def attention(qt, kp, vt, wo, experts):
     return pl.pallas_call(
         attention_kernel,
         out_shape=(
             jax.ShapeDtypeStruct((16, HD, 128), BF),
             jax.ShapeDtypeStruct((4, 256, D), BF),
-        ),
-        in_specs=[whole(), whole(), whole(), anywhere()],
-        out_specs=(anywhere(), anywhere()),
+        )
+        + tuple(jax.ShapeDtypeStruct(w.shape, BF) for w in experts),
+        in_specs=[anywhere()] * 7,
+        out_specs=(anywhere(),) * 5,
         scratch_shapes=[
             VMEM((8, HD, 256), BF),
             VMEM((4, 2, 1024, 128), BF),
@@ -414,87 +425,272 @@
             pltpu.SemaphoreType.DMA((3,)),
             pltpu.SemaphoreType.DMA((3,)),
             pltpu.SemaphoreType.DMA,
+            pltpu.SemaphoreType.DMA((3,)),
+            pltpu.SemaphoreType.DMA((3,)),
         ],
         compiler_params=pltpu.CompilerParams(
-            collective_id=0, has_side_effects=True, vmem_limit_bytes=40 << 20
+            collective_id=0, has_side_effects=True, vmem_limit_bytes=60 << 20
+        ),
+        cost_estimate=pl.CostEstimate(
+            flops=60 * 10**9, bytes_accessed=200 * 10**6, transcendentals=0
         ),
         name="attention",
-    )(qt, kp, vt, wo)
-
-
-def route_kernel(at_ref, wo_ref, hit_ref, gain_ref, wr_ref, routes_ref, res_ref, out_ref, hi_ref, lo_ref):
-    mixed = lax.dot_general(
-        at_ref[...], wo_ref[...], (((0,), (0,)), ((), ())), preferred_element_type=F32
-    )
-    residual = hit_ref[...].astype(F32) + mixed
-    res_ref[...] = residual
-    inv = lax.rsqrt(jnp.mean(residual * residual, axis=-1, keepdims=True) + EPSILON)
-    normed = (residual * inv * gain_ref[...]).astype(BF)
-    logits = jnp.dot(normed, wr_ref[...], preferred_element_type=F32)
-    rows, experts = logits.shape
-    ids = lax.broadcasted_iota(jnp.int32, (rows, experts), 1)
-    picks = (routes_ref[:, 0:1] == ids) | (routes_ref[:, 1:2] == ids)
-    top = jnp.max(jnp.where(picks, logits, -jnp.inf), axis=-1, keepdims=True)
-    weights = jnp.where(picks, jnp.exp(jnp.where(picks, logits - top, 0.0)), 0.0)
-    gates = weights / jnp.sum(weights, axis=-1, keepdims=True)
-    gate_hi = gates.astype(BF)
-    gate_lo = (gates - gate_hi.astype(F32)).astype(BF)
+    )(qt, kp, vt, wo, *experts)
+
+
+def shifted(i, sign, ctx, exp):
+    o = (i * 27) % 64
+    ylo, x, z, yhi = ctx // 16, (ctx // 4) % 4, ctx % 4, exp // 2
+    to_x = (x + 4 + sign * (o % 4)) % 4
+    to_y = (yhi * 2 + ylo + 4 + sign * ((o // 4) % 4)) % 4
+    to_z = (z + 4 + sign * (o // 16)) % 4
+    to_ctx = (to_y % 2) * 16 + to_x * 4 + to_z
+    return to_ctx, (to_y // 2) * 2 + exp % 2
+
+
+def mixture_kernel(
+    at_hbm,
+    wo_hbm,
+    hit_hbm,
+    gain_ref,
+    wr_ref,
+    routes_ref,
+    gate_ref,
+    up_ref,
+    down_ref,
+    gates_ref,
+    ups_ref,
+    downs_ref,
+    out_ref,
+    at_ref,
+    wo_ref,
+    hit_ref,
+    wg,
+    wu,
+    wd,
+    rows_out,
+    got,
+    stage,
+    back,
+    load,
+    w_sem,
+    send,
+    recv,
+    b_send,
+    b_recv,
+):
+    ctx = lax.axis_index("ctx")
+    exp = lax.axis_index("exp")
+    yhi = exp // 2
+    rows = hit_ref.shape[0]
+    loads = [
+        pltpu.make_async_copy(at_hbm, at_ref, load.at[0]),
+        pltpu.make_async_copy(wo_hbm, wo_ref, load.at[1]),
+        pltpu.make_async_copy(
+            hit_hbm.at[pl.ds(pl.multiple_of(exp * rows, rows), rows)], hit_ref, load.at[2]
+        ),
+    ]
+    weight_loads = [
+        pltpu.make_async_copy(src, dst.at[q], w_sem.at[n, q])
+        for n, (own, near, dst) in enumerate(
+            ((gate_ref, gates_ref, wg), (up_ref, ups_ref, wu), (down_ref, downs_ref, wd))
+        )
+        for q, src in enumerate((own, near))
+    ]
+    for copy in loads:
+        copy.start()
+    barrier = pltpu.get_barrier_semaphore()
+
+    def greet(i, carry):
+        pl.semaphore_signal(
+            barrier, inc=1, device_id=shifted(i, 1, ctx, exp), device_id_type=MESH
+        )
+        return carry
+
+    lax.fori_loop(1, 64, greet, 0)
+
+    experts, cap = rows_out.shape[0], rows_out.shape[1]
+    places = experts * cap
+    ids = lax.broadcasted_iota(jnp.int32, (experts, rows), 0)
+    picks = (routes_ref[0:1, :] == ids) | (routes_ref[1:2, :] == ids)
     marks = jnp.where(picks, 1.0, 0.0).astype(BF)
-    before = lax.broadcasted_iota(jnp.int32, (rows, rows), 0) > lax.broadcasted_iota(
+    before = lax.broadcasted_iota(jnp.int32, (rows, rows), 0) < lax.broadcasted_iota(
         jnp.int32, (rows, rows), 1
     )
     slots = jnp.dot(
-        jnp.where(before, 1.0, 0.0).astype(BF), marks, preferred_element_type=F32
+        marks, jnp.where(before, 1.0, 0.0).astype(BF), preferred_element_type=F32
     ).astype(BF)
-    places = out_ref.shape[0]
-    cap = places // experts
     spread = jnp.where(
-        lax.broadcasted_iota(jnp.int32, (experts, places), 1) // cap
-        == lax.broadcasted_iota(jnp.int32, (experts, places), 0),
+        lax.broadcasted_iota(jnp.int32, (places, experts), 0) // cap
+        == lax.broadcasted_iota(jnp.int32, (places, experts), 1),
         1.0,
         0.0,
     ).astype(BF)
-    wide = lambda v: jnp.dot(v, spread, preferred_element_type=F32)
-    order = (lax.broadcasted_iota(jnp.int32, (rows, places), 1) % cap).astype(F32)
+    wide = lambda v: jnp.dot(spread, v, preferred_element_type=F32)
+    order = (lax.broadcasted_iota(jnp.int32, (places, rows), 0) % cap).astype(F32)
     here = (wide(marks) > 0.5) & (wide(slots) == order)
     table = jnp.where(here, 1.0, 0.0).astype(BF)
-    out_ref[...] = lax.dot_general(
-        table, normed, (((0,), (0,)), ((), ())), preferred_element_type=F32
-    ).astype(BF)
-    hi_ref[...] = jnp.where(here, wide(gate_hi), 0.0).astype(BF)
-    lo_ref[...] = jnp.where(here, wide(gate_lo), 0.0).astype(BF)
-
-
-def route(at, wo, hit, gain, wr, routes):
-    rows = hit.shape[0]
-    places = wr.shape[1] * 8
+
+    for copy in loads:
+        copy.wait()
+    for copy in weight_loads:
+        copy.start()
+    mixed = lax.dot_general(
+        at_ref[...].reshape(D, rows),
+        wo_ref[...].reshape(D, D),
+        (((0,), (0,)), ((), ())),
+        preferred_element_type=F32,
+    )
+    residual = hit_ref[...].astype(F32) + mixed
+    inv = lax.rsqrt(jnp.mean(residual * residual, axis=-1, keepdims=True) + EPSILON)
+    normed = (residual * inv * gain_ref[...]).astype(BF)
+    picked = jnp.dot(table, normed, preferred_element_type=F32)
+    rows_out[...] = picked.reshape(rows_out.shape).astype(BF)
+
+    pl.semaphore_wait(barrier, 63)
+
+    def pair(n):
+        return pl.ds(pl.multiple_of(2 * n, 2), 2)
+
+    def row_copy(i):
+        to = shifted(i, 1, ctx, exp)
+        return pltpu.make_async_remote_copy(
+            src_ref=rows_out.at[pair(to[0])],
+            dst_ref=got.at[i],
+            send_sem=send.at[i],
+            recv_sem=recv.at[i],
+            device_id=to,
+            device_id_type=MESH,
+        )
+
+    def back_copy(i):
+        return pltpu.make_async_remote_copy(
+            src_ref=stage.at[i],
+            dst_ref=back.at[yhi, pair(ctx)],
+            send_sem=b_send.at[i],
+            recv_sem=b_recv.at[i],
+            device_id=shifted(i, -1, ctx, exp),
+            device_id_type=MESH,
+        )
+
+    def send_rows(i, carry):
+        row_copy(i).start()
+        return carry
+
+    pltpu.make_async_copy(rows_out.at[pair(ctx)], got.at[0], recv.at[0]).start()
+    lax.fori_loop(1, 64, send_rows, 0)
+
+    logits = lax.dot_general(
+        wr_ref[...], normed, (((1,), (1,)), ((), ())), preferred_element_type=F32
+    )
+    top = jnp.max(jnp.where(picks, logits, -jnp.inf), axis=0, keepdims=True)
+    weights = jnp.where(picks, jnp.exp(jnp.where(picks, logits - top, 0.0)), 0.0)
+    gates = weights / jnp.sum(weights, axis=0, keepdims=True)
+    gate_hi = gates.astype(BF)
+    gate_lo = (gates - gate_hi.astype(F32)).astype(BF)
+    hi = jnp.where(here, wide(gate_hi), 0.0).astype(BF)
+    lo = jnp.where(here, wide(gate_lo), 0.0).astype(BF)
+    for copy in weight_loads:
+        copy.wait()
+
+    group = 32
+
+    def serve(g, carry):
+        first = g * group
+
+        def await_rows(i, carry):
+            pltpu.make_async_copy(got.at[first + i], got.at[first + i], recv.at[first + i]).wait()
+            return carry
+
+        lax.fori_loop(0, group, await_rows, 0)
+        at = pl.ds(pl.multiple_of(first, group), group)
+
+        def expert(j, carry):
+            mine = got[at, j].astype(F32).reshape(group * cap, D).astype(BF)
+            total = None
+            for q in range(2):
+                gate = jnp.dot(mine, wg[q, j], preferred_element_type=F32)
+                up = jnp.dot(mine, wu[q, j], preferred_element_type=F32)
+                hidden = (gate / (1.0 + jnp.exp(-gate)) * up).astype(BF)
+                part = jnp.dot(hidden, wd[q, j], preferred_element_type=F32)
+                total = part if total is None else total + part
+            stage[at, j] = total.reshape(group, cap, D).astype(BF)
+            return carry
+
+        lax.fori_loop(0, 2, expert, 0)
+
+        @pl.when(g == 0)
+        def _():
+            pltpu.make_async_copy(stage.at[0], back.at[yhi, pair(ctx)], b_recv.at[0]).start()
+
+        def send_back(i, carry):
+            @pl.when(first + i > 0)
+            def _():
+                back_copy(first + i).start()
+
+            return carry
+
+        lax.fori_loop(0, group, send_back, 0)
+        return carry
+
+    lax.fori_loop(0, 2, serve, 0)
+
+    def await_back(i, carry):
+        from_ctx, from_exp = shifted(i, 1, ctx, exp)
+        block = back.at[from_exp // 2, pair(from_ctx)]
+        pltpu.make_async_copy(block, block, b_recv.at[i]).wait()
+        return carry
+
+    lax.fori_loop(0, 64, await_back, 0)
+    total = residual
+    for n in range(2):
+        mine = back[n].astype(F32).reshape(places, D).astype(BF)
+        for gate in (hi, lo):
+            total = total + lax.dot_general(
+                gate, mine, (((0,), (0,)), ((), ())), preferred_element_type=F32
+            )
+    out_ref[...] = total.astype(BF)
+
+    def sent(i, carry):
+        row_copy(i).wait_send()
+        back_copy(i).wait_send()
+        return carry
+
+    lax.fori_loop(1, 64, sent, 0)
+
+
+def mixture(at, wo, hit, gain, wr, routes, own, near):
+    experts = wr.shape[0]
+    rows = routes.shape[1]
+    cap = 8
     return pl.pallas_call(
-        route_kernel,
-        out_shape=(
-            jax.ShapeDtypeStruct((rows, D), F32),
-            jax.ShapeDtypeStruct((places, D), BF),
-            jax.ShapeDtypeStruct((rows, places), BF),
-            jax.ShapeDtypeStruct((rows, places), BF),
+        mixture_kernel,
+        out_shape=jax.ShapeDtypeStruct((rows, D), BF),
+        in_specs=[anywhere()] * 3 + [whole()] * 3 + [anywhere()] * 6,
+        out_specs=whole(),
+        scratch_shapes=[
+            VMEM(at.shape, BF),
+            VMEM(wo.shape, BF),
+            VMEM((rows, D), BF),
+            VMEM((2,) + own[0].shape, BF),
+            VMEM((2,) + own[1].shape, BF),
+            VMEM((2,) + own[2].shape, BF),
+            VMEM((experts, cap, D), BF),
+            VMEM((64, 2, cap, D), BF),
+            VMEM((64, 2, cap, D), BF),
+            VMEM((2, experts, cap, D), BF),
+            pltpu.SemaphoreType.DMA((3,)),
+            pltpu.SemaphoreType.DMA((3, 2)),
+            pltpu.SemaphoreType.DMA((64,)),
+            pltpu.SemaphoreType.DMA((64,)),
+            pltpu.SemaphoreType.DMA((64,)),
+            pltpu.SemaphoreType.DMA((64,)),
+        ],
+        compiler_params=pltpu.CompilerParams(
+            collective_id=1, has_side_effects=True, vmem_limit_bytes=60 << 20
         ),
-        in_specs=[whole()] * 6,
-        out_specs=(whole(),) * 4,
-        name="route",
-    )(at, wo, hit, gain.reshape(1, D), wr, routes)
-
-
-def combine_kernel(res_ref, hi_ref, lo_ref, back_ref, out_ref):
-    back = back_ref[...]
-    mixture = jnp.dot(hi_ref[...], back, preferred_element_type=F32) + jnp.dot(
-        lo_ref[...], back, preferred_element_type=F32
-    )
-    out_ref[...] = (res_ref[...] + mixture).astype(BF)
-
-
-def run_experts(received, gate_mats, up_mats, down_mats):
-    gate_act = jnp.einsum("sjcd,jdf->sjcf", received, gate_mats, preferred_element_type=F32)
-    up_act = jnp.einsum("sjcd,jdf->sjcf", received, up_mats, preferred_element_type=F32)
-    hidden = (jax.nn.silu(gate_act) * up_act).astype(BF)
-    return jnp.einsum("sjcf,jfd->sjcd", hidden, down_mats, preferred_element_type=F32)
+        name="mixture",
+    )(at, wo, hit, gain.reshape(1, D), wr, routes, *own, *near)
 
 
 def body(
@@ -511,39 +707,10 @@
     w_down,
     routes,
 ):
-    ctx_count = lax.axis_size("ctx")
-    exp_count = lax.axis_size("exp")
-    rows_dev = hit_features.shape[0] // exp_count
     qt, kp, vt = project(hit_features, norm_attn, w_query, w_key, w_value)
-    at, wo = attention(qt, kp, vt, w_out)
-    own_rows = lax.dynamic_slice_in_dim(
-        hit_features, lax.axis_index("exp") * rows_dev, rows_dev, 0
-    )
-    residual, outgoing, gate_hi, gate_lo = route(
-        at.reshape(D, rows_dev), wo.reshape(D, D), own_rows, norm_ffn, w_router, routes
-    )
-    local_experts = w_gate.shape[0]
-    grid = outgoing.reshape(ctx_count, local_experts, -1, D)
-    copies = jnp.broadcast_to(grid[:, None], (ctx_count, exp_count) + grid.shape[1:]).reshape(
-        (ctx_count * exp_count,) + grid.shape[1:]
-    )
-    produced = run_experts(
-        lax.all_to_all(copies, ("ctx", "exp"), split_axis=0, concat_axis=0, tiled=True),
-        w_gate,
-        w_up,
-        w_down,
-    )
-    returned = lax.all_to_all(
-        produced.astype(BF), ("ctx", "exp"), split_axis=0, concat_axis=0, tiled=True
-    ).astype(F32)
-    combined = jnp.sum(returned.reshape((ctx_count, exp_count) + grid.shape[1:]), axis=1)
-    return pl.pallas_call(
-        combine_kernel,
-        out_shape=jax.ShapeDtypeStruct((rows_dev, D), BF),
-        in_specs=[whole()] * 4,
-        out_specs=whole(),
-        name="combine",
-    )(residual, gate_hi, gate_lo, combined.reshape(outgoing.shape).astype(BF))
+    own = (w_gate, w_up, w_down)
+    at, wo, *near = attention(qt, kp, vt, w_out, own)
+    return mixture(at, wo, hit_features, norm_ffn, w_router.T, routes.T, own, near)
 
 
 def solution(mesh):

time: 247 us -> 138 us (0.56)
  blocking collectives: 122 us -> 0 us
  Pallas kernels: 82.8 us -> 135 us
  matrix products: 19 us -> 0 us
  local copies, waits for them, and re-layouts: 19.1 us -> 1.67 us
    all_to_all x2 -> x0, blocking collectives: 122 us -> none  [the longest x1 61.6 us: body(): lax.all_to_all(produced.astype(BF), ('ctx', 'exp'), split_axis=0, concat_...]
    pallas_call x2 -> x1, Pallas kernels: 6.9 us -> 59 us  [mixture(): pl.pallas_call(mixture_kernel, out_shape=jax.ShapeDtypeStruct((rows, D),...]
    dot_general x2 -> x0, matrix products: 19 us -> none  [the longest x1 12.4 us: run_experts(): jnp.einsum('sjcf,jfd->sjcd', hidden, down_mats, preferred_element_type=F32)]
    unnamed x20 -> x1, local copies, waits for them, and re-layouts: 11.2 us -> 1.67 us
    convert_element_type x1 -> x0, local copies, waits for them, and re-layouts: 4.51 us -> none  [body(): produced.astype(BF)]
where the time goes in v4:
time: 138 us; the launch traced here: 137 us
  Pallas kernels  135 us (98%)
  local copies, waits for them, and re-layouts  1.67 us (1%)
    pallas_call x1, Pallas kernels, attention(): pl.pallas_call(attention_kernel, out_shape=(jax.ShapeDtypeStruct((16, HD,...  72.7 us
    pallas_call x1, Pallas kernels, mixture(): pl.pallas_call(mixture_kernel, out_shape=jax.ShapeDtypeStruct((rows, D),...  59 us
    pallas_call x1, Pallas kernels, project(): pl.pallas_call(project_kernel, out_shape=(jax.ShapeDtypeStruct((2, 4, HD,...  3.74 us

profile of v4, /device:TPU:1, one launch (start us, length us, event | category | flops | bytes accessed | tf_op | source)
XLA Modules:
  0.0 137.1 jit_solution(4665149906376191473)
XLA Ops:
  0.0 3.7 %project.1 = (bf16[2,4,64,256]{3,2,1,0:T(8,128)(2,1)}, bf16[4,2,128,128]{3,2,1,0:T(8,128)(2,1)}, bf16[4,2,2,64,128]{4,3,2,1,0:T(8,128)(2,1)}) custom-call(bf16[512,1024]{1,0:T(8,128)(2,1)} %hit_hbm.1, f32[1,1024]{1,0:T(1,128)} %bitcast.5, bf16[1024,256]{1,0:T(8,128)(2,1)} %wq_ref.1, bf16[1024,256]{1,0:T(8,128)(2,1)} %wk_ref.1, bf16[1024,256]{1,0:T(8,128)(2,1)} %wv_ref.1), custom_call_target="tpu_custom_call" | custom-call | tf_op jit(solution)/shard_map/project/pallas_call | solution.py:55
  3.7 72.7 %attention.1 = (bf16[16,64,128]{2,1,0:T(8,128)(2,1)}, bf16[4,256,1024]{2,1,0:T(8,128)(2,1)}, bf16[2,1024,512]{2,1,0:T(8,128)(2,1)}, bf16[2,1024,512]{2,1,0:T(8,128)(2,1)}, bf16[2,512,1024]{2,1,0:T(8,128)(2,1)}) custom-call(bf16[2,4,64,256]{3,2,1,0:T(8,128)(2,1)} %get-tuple-element.13.qt_ref, bf16[4,2,128,128]{3,2,1,0:T(8,128)(2,1)} %get-tuple-element.14.kp_ref, ...), custom_call_target="tpu_custom_call" | custom-call | flops 60000002048 | bytes 200000000 | tf_op jit(solution)/shard_map/attention/pallas_call | solution.py:398
  76.5 59.0 %mixture.1 = bf16[128,1024]{1,0:T(8,128)(2,1)} custom-call(bf16[16,64,128]{2,1,0:T(8,128)(2,1)} %get-tuple-element.16.at_hbm, bf16[4,256,1024]{2,1,0:T(8,128)(2,1)} %get-tuple-element.17.wo_hbm, bf16[512,1024]{1,0:T(8,128)(2,1)} %hit_hbm.1, f32[1,1024]{1,0:T(1,128)} %bitcast.6, bf16[64,1024]{1,0:T(8,128)(2,1)} %bitcast.4, s32[2,128]{1,0:T(2,128)} %bitcast.7, ...), custom_call_target="tpu_custom_call" | custom-call | tf_op jit(solution)/shard_map/mixture/pallas_call | solution.py:666
  135.4 1.7 %copy.14 = bf16[128,1024]{1,0:T(8,128)(2,1)} copy(bf16[128,1024]{1,0:T(8,128)(2,1)} %mixture.1) | data formatting | bytes 524288

commit v5 on v4

v5 whole, which is shorter than its diff:
```python
import functools
import math

import jax
import jax.numpy as jnp
from jax import lax
from jax.experimental import pallas as pl
from jax.experimental.pallas import tpu as pltpu
from jax.sharding import PartitionSpec as P

D = 1024
HD = 64
EPSILON = 1e-05
LOWEST = -1e30
ALPHA = math.log2(math.e) / math.sqrt(HD)
BF = jnp.bfloat16
F32 = jnp.float32
MESH = pl.DeviceIdType.MESH
VMEM = pltpu.VMEM


def whole():
    return pl.BlockSpec(memory_space=pltpu.VMEM)


def anywhere():
    return pl.BlockSpec(memory_space=pl.ANY)


def shifted(i, sign, ctx, exp):
    o = (i * 27) % 64
    ylo, x, z, yhi = ctx // 16, (ctx // 4) % 4, ctx % 4, exp // 2
    to_x = (x + 4 + sign * (o % 4)) % 4
    to_y = (yhi * 2 + ylo + 4 + sign * ((o // 4) % 4)) % 4
    to_z = (z + 4 + sign * (o // 16)) % 4
    to_ctx = (to_y % 2) * 16 + to_x * 4 + to_z
    return to_ctx, (to_y // 2) * 2 + exp % 2


def layer_kernel(
    hit_hbm,
    gain_attn_ref,
    wq_hbm,
    wk_hbm,
    wv_hbm,
    wo_ref,
    gain_ref,
    wr_ref,
    routes_ref,
    gate_ref,
    up_ref,
    down_ref,
    out_ref,
    x_ref,
    wq_ref,
    wk_ref,
    wv_ref,
    qt_ref,
    kp_ref,
    vt_ref,
    qg,
    kg,
    vg,
    q2,
    s_ref,
    acc,
    mx,
    ls,
    ost,
    at_ref,
    wo_all,
    wg,
    wu,
    wd,
    rows_out,
    got,
    stage,
    back,
    load,
    x_send,
    x_recv,
    ring_send,
    ring_recv,
    sib_send,
    sib_recv,
    o_send,
    o_recv,
    w_send,
    w_recv,
    w_own,
    e_send,
    e_recv,
    w_sem,
    send,
    recv,
    b_send,
    b_recv,
):
    ctx = lax.axis_index("ctx")
    exp = lax.axis_index("exp")
    ylo = ctx // 16
    x = (ctx // 4) % 4
    z = ctx % 4
    yhi = exp // 2
    core = exp % 2
    mine = ylo * 4 + z

    def device(to_ylo, to_x, to_z, to_yhi, to_core):
        return (to_ylo * 16 + to_x * 4 + to_z, to_yhi * 2 + to_core)

    right = device(ylo, (x + 1) % 4, z, yhi, core)
    left = device(ylo, (x + 3) % 4, z, yhi, core)
    sibling = device(ylo, x, z, yhi, 1 - core)

    barrier = pltpu.get_barrier_semaphore()

    def greet(i, carry):
        pl.semaphore_signal(
            barrier, inc=1, device_id=shifted(i, 1, ctx, exp), device_id_type=MESH
        )
        return carry

    def greet_plane(i, carry):
        to = device(i // 8, x, (i // 2) % 4, i % 2, 1 - core)
        pl.semaphore_signal(barrier, inc=1, device_id=to, device_id_type=MESH)
        return carry

    loads = [
        pltpu.make_async_copy(src, dst, load.at[m])
        for m, (src, dst) in enumerate(
            ((hit_hbm, x_ref), (wq_hbm, wq_ref), (wk_hbm, wk_ref), (wv_hbm, wv_ref))
        )
    ]
    for copy in loads:
        copy.start()
    lax.fori_loop(0, 16, greet_plane, 0)
    lax.fori_loop(1, 64, greet, 0)

    for copy in loads[:2]:
        copy.wait()
    xs = x_ref[...].astype(F32)
    inv = lax.rsqrt(jnp.mean(xs * xs, axis=-1, keepdims=True) + EPSILON)
    n = (xs * inv * gain_attn_ref[...]).astype(BF)
    qt = jnp.dot(n, wq_ref[...], preferred_element_type=F32).T.astype(BF)
    for head in range(4):
        for block in range(4):
            qt_ref[block % 2, head, :, (block // 2) * 128 : (block // 2) * 128 + 128] = qt[
                head * HD : head * HD + HD, block * 128 : block * 128 + 128
            ]
    loads[2].wait()
    k = jnp.dot(n, wk_ref[...], preferred_element_type=F32)
    for head in range(4):
        for half in range(2):
            kh = k[half * 256 : half * 256 + 256, head * HD : head * HD + HD]
            kp_ref[head, half] = jnp.concatenate([kh[0:128], kh[128:256]], axis=1).astype(BF)
    loads[3].wait()
    vt = jnp.dot(n, wv_ref[...], preferred_element_type=F32).T.astype(BF)
    for head in range(4):
        for half in range(2):
            for u in range(2):
                at = half * 256 + u * 128
                vt_ref[head, half, u] = vt[head * HD : head * HD + HD, at : at + 128]

    pl.semaphore_wait(barrier, 79)

    def head_copies(i):
        head, half = (z + 1 + i // 2) % 4, i % 2
        to = device(core, x, head, yhi, half)
        parts = (
            (qt_ref.at[half, head], qg.at[mine]),
            (kp_ref.at[head, half], kg.at[0, half, pl.ds(pl.multiple_of(mine * 128, 128), 128), :]),
            (
                vt_ref.at[head, half],
                vg.at[0, half, :, :, pl.ds(pl.multiple_of(mine * 128, 128), 128)],
            ),
        )
        own = (core == ylo) & (head == z) & (half == core)
        remote = [
            pltpu.make_async_remote_copy(
                src_ref=src,
                dst_ref=dst,
                send_sem=x_send.at[n, i],
                recv_sem=x_recv.at[n, mine],
                device_id=to,
                device_id_type=MESH,
            )
            for n, (src, dst) in enumerate(parts)
        ]
        local = [
            pltpu.make_async_copy(src, dst, x_recv.at[n, mine])
            for n, (src, dst) in enumerate(parts)
        ]
        return own, remote, local

    def send_heads(i, carry):
        own, remote, local = head_copies(i)

        @pl.when(own)
        def _():
            for copy in local:
                copy.start()

        @pl.when(jnp.logical_not(own))
        def _():
            for copy in remote:
                copy.start()

        return carry

    lax.fori_loop(0, 8, send_heads, 0)

    def await_heads(j, carry):
        pltpu.make_async_copy(qg.at[j], qg.at[j], x_recv.at[0, j]).wait()
        at = pl.ds(pl.multiple_of(j * 128, 128), 128)
        kd = kg.at[0, core, at, :]
        pltpu.make_async_copy(kd, kd, x_recv.at[1, j]).wait()
        vd = vg.at[0, core, :, :, at]
        pltpu.make_async_copy(vd, vd, x_recv.at[2, j]).wait()
        return carry

    lax.fori_loop(0, 8, await_heads, 0)

    def remote(src, dst, send, recv, to):
        return pltpu.make_async_remote_copy(
            src_ref=src,
            dst_ref=dst,
            send_sem=send,
            recv_sem=recv,
            device_id=to,
            device_id_type=MESH,
        )

    def to_sibling(slot):
        return [
            remote(g.at[slot, core], g.at[slot, core], sib_send.at[n, slot], sib_recv.at[n, slot], sibling)
            for n, g in enumerate((kg, vg))
        ]

    def from_sibling(slot):
        return [
            remote(g.at[slot, 1 - core], g.at[slot, 1 - core], sib_send.at[n, slot], sib_recv.at[n, slot], sibling)
            for n, g in enumerate((kg, vg))
        ]

    k_right = remote(kg.at[0, core], kg.at[1, core], ring_send.at[0, 0], ring_recv.at[0, 0], right)
    v_right = remote(vg.at[0, core], vg.at[1, core], ring_send.at[1, 0], ring_recv.at[1, 0], right)
    k_left = remote(kg.at[0, core], kg.at[2, core], ring_send.at[0, 1], ring_recv.at[0, 1], left)
    v_left = remote(vg.at[0, core], vg.at[2, core], ring_send.at[1, 1], ring_recv.at[1, 1], left)
    k_on = remote(kg.at[1, core], kg.at[3, core], ring_send.at[0, 2], ring_recv.at[0, 2], right)
    v_on = remote(vg.at[2, core], vg.at[3, core], ring_send.at[1, 2], ring_recv.at[1, 2], left)
    for copy in (k_right, k_left, v_right, v_left):
        copy.start()
    for copy in to_sibling(0):
        copy.start()

    far_chip = device(ylo, x, z, 1 - yhi, core)
    far_exp = (exp + 2) % 4
    w_local = pltpu.make_async_copy(wo_ref, wo_all.at[exp], w_own)
    w_across = remote(wo_ref, wo_all.at[exp], w_send.at[0], w_recv.at[0], far_chip)
    w_beside = remote(wo_ref, wo_all.at[exp], w_send.at[1], w_recv.at[1], sibling)
    w_on = remote(
        wo_all.at[far_exp], wo_all.at[far_exp], w_send.at[2], w_recv.at[2], sibling
    )
    w_across.start()
    w_beside.start()
    w_local.start()
    e_beside = [
        remote(src, dst, e_send.at[n], e_recv.at[n], sibling)
        for n, (src, dst) in enumerate(
            ((gate_ref, wg.at[1]), (up_ref, wu.at[1]), (down_ref, wd.at[1]))
        )
    ]
    weight_loads = [
        pltpu.make_async_copy(src, dst.at[0], w_sem.at[n])
        for n, (src, dst) in enumerate(((gate_ref, wg), (up_ref, wu), (down_ref, wd)))
    ]
    for copy in weight_loads:
        copy.start()
    for copy in e_beside:
        copy.start()

    zero = jnp.zeros((HD, 256), BF)
    for j in range(8):
        q2[j, 0, 0:HD] = qg[j]
        q2[j, 0, HD : 2 * HD] = zero
        q2[j, 1, 0:HD] = zero
        q2[j, 1, HD : 2 * HD] = qg[j]
    acc[...] = jnp.zeros_like(acc)
    mx[...] = jnp.full_like(mx, LOWEST)
    ls[...] = jnp.zeros_like(ls)

    def score(phase, tile, p):
        j = (tile + mine) % 8
        keys = kg[phase // 2, (phase + core) % 2]
        for u in range(2):
            s_ref[p, u] = lax.dot_general(
                keys, q2[j, u], (((1,), (0,)), ((), ())), preferred_element_type=F32
            )

    def absorb(phase, tile, p):
        j = (tile + mine) % 8
        s0 = s_ref[p, 0]
        s1 = s_ref[p, 1]
        old = mx[j]
        new = jnp.maximum(
            old,
            jnp.maximum(jnp.max(s0, axis=0, keepdims=True), jnp.max(s1, axis=0, keepdims=True)),
        )
        fade = jnp.exp2((old - new) * ALPHA)
        e0 = jnp.exp2((s0 - new) * ALPHA)
        e1 = jnp.exp2((s1 - new) * ALPHA)
        slot, half = phase // 2, (phase + core) % 2
        ls[j] = ls[j] * fade + (
            jnp.sum(e0, axis=0, keepdims=True) + jnp.sum(e1, axis=0, keepdims=True)
        )
        acc[j] = acc[j] * fade + (
            jnp.dot(vg[slot, half, 0], e0.astype(BF), preferred_element_type=F32)
            + jnp.dot(vg[slot, half, 1], e1.astype(BF), preferred_element_type=F32)
        )
        mx[j] = new

    head = yhi * 8 + mine

    def out_copy(i):
        j, to_yhi = i % 8, i // 8
        to = device(j // 4, x, j % 4, to_yhi, core)
        return (
            remote(ost.at[j, to_yhi], at_ref.at[head], o_send.at[i], o_recv.at[head], to),
            pltpu.make_async_copy(ost.at[j, to_yhi], at_ref.at[head], o_recv.at[head]),
        )

    def send_out(tile):
        j = (tile + mine) % 8
        o = (acc[j] / ls[j]).astype(BF)
        ost[j, 0] = o[:, 0:128]
        ost[j, 1] = o[:, 128:256]
        for to_yhi in range(2):
            i = to_yhi * 8 + j
            away, local = out_copy(i)

            @pl.when(i == head)
            def _(local=local):
                local.start()

            @pl.when(i != head)
            def _(away=away):
                away.start()

    score(0, 0, 0)

    def turn(g, carry):
        phase, pair = g // 4, g % 4
        last = pair == 3

        for slot in (0, 1, 2, 3):

            @pl.when(last & (phase == 2 * slot))
            def _(slot=slot):
                for copy in from_sibling(slot):
                    copy.wait_recv()

        @pl.when(last & (phase == 1))
        def _():
            for copy in (k_right, k_left, v_right, v_left):
                copy.wait_recv()
            k_on.start()
            v_on.start()
            for slot in (1, 2):
                for copy in to_sibling(slot):
                    copy.start()

        @pl.when(last & (phase == 5))
        def _():
            k_on.wait_recv()
            v_on.wait_recv()
            w_across.wait_recv()
            w_on.start()
            for copy in to_sibling(3):
                copy.start()

        score(phase, 2 * pair + 1, 1)
        absorb(phase, 2 * pair, 0)
        later = jnp.minimum(g + 1, 31)
        score(later // 4, 2 * (later % 4), 0)
        absorb(phase, 2 * pair + 1, 1)

        @pl.when(phase == 7)
        def _():
            send_out(2 * pair)
            send_out(2 * pair + 1)

        return carry

    lax.fori_loop(0, 32, turn, 0)

    rows = at_ref.shape[2]
    experts, cap = rows_out.shape[0], rows_out.shape[1]
    places = experts * cap
    ids = lax.broadcasted_iota(jnp.int32, (experts, rows), 0)
    picks = (routes_ref[0:1, :] == ids) | (routes_ref[1:2, :] == ids)
    marks = jnp.where(picks, 1.0, 0.0).astype(BF)
    before = lax.broadcasted_iota(jnp.int32, (rows, rows), 0) < lax.broadcasted_iota(
        jnp.int32, (rows, rows), 1
    )
    slots = jnp.dot(
        marks, jnp.where(before, 1.0, 0.0).astype(BF), preferred_element_type=F32
    ).astype(BF)
    spread = jnp.where(
        lax.broadcasted_iota(jnp.int32, (places, experts), 0) // cap
        == lax.broadcasted_iota(jnp.int32, (places, experts), 1),
        1.0,
        0.0,
    ).astype(BF)
    wide = lambda v: jnp.dot(spread, v, preferred_element_type=F32)
    order = (lax.broadcasted_iota(jnp.int32, (places, rows), 0) % cap).astype(F32)
    here = (wide(marks) > 0.5) & (wide(slots) == order)
    table = jnp.where(here, 1.0, 0.0).astype(BF)

    def await_out(i, carry):
        pltpu.make_async_copy(at_ref.at[i], at_ref.at[i], o_recv.at[i]).wait()
        return carry

    lax.fori_loop(0, 16, await_out, 0)

    w_local.wait()
    w_beside.wait_recv()
    w_on.wait_recv()
    mixed = lax.dot_general(
        at_ref[...].reshape(D, rows),
        wo_all[...].reshape(D, D),
        (((0,), (0,)), ((), ())),
        preferred_element_type=F32,
    )
    own_rows = x_ref[pl.ds(pl.multiple_of(exp * rows, rows), rows), :]
    residual = own_rows.astype(F32) + mixed
    inv = lax.rsqrt(jnp.mean(residual * residual, axis=-1, keepdims=True) + EPSILON)
    normed = (residual * inv * gain_ref[...]).astype(BF)
    picked = jnp.dot(table, normed, preferred_element_type=F32)
    rows_out[...] = picked.reshape(rows_out.shape).astype(BF)

    def pair(n):
        return pl.ds(pl.multiple_of(2 * n, 2), 2)

    def row_copy(i):
        to = shifted(i, 1, ctx, exp)
        return pltpu.make_async_remote_copy(
            src_ref=rows_out.at[pair(to[0])],
            dst_ref=got.at[i],
            send_sem=send.at[i],
            recv_sem=recv.at[i],
            device_id=to,
            device_id_type=MESH,
        )

    def back_copy(i):
        return pltpu.make_async_remote_copy(
            src_ref=stage.at[i],
            dst_ref=back.at[yhi, pair(ctx)],
            send_sem=b_send.at[i],
            recv_sem=b_recv.at[i],
            device_id=shifted(i, -1, ctx, exp),
            device_id_type=MESH,
        )

    def send_rows(i, carry):
        row_copy(i).start()
        return carry

    pltpu.make_async_copy(rows_out.at[pair(ctx)], got.at[0], recv.at[0]).start()
    lax.fori_loop(1, 64, send_rows, 0)

    logits = lax.dot_general(
        wr_ref[...], normed, (((1,), (1,)), ((), ())), preferred_element_type=F32
    )
    top = jnp.max(jnp.where(picks, logits, -jnp.inf), axis=0, keepdims=True)
    weights = jnp.where(picks, jnp.exp(jnp.where(picks, logits - top, 0.0)), 0.0)
    gates = weights / jnp.sum(weights, axis=0, keepdims=True)
    gate_hi = gates.astype(BF)
    gate_lo = (gates - gate_hi.astype(F32)).astype(BF)
    hi = jnp.where(here, wide(gate_hi), 0.0).astype(BF)
    lo = jnp.where(here, wide(gate_lo), 0.0).astype(BF)
    for copy in weight_loads:
        copy.wait()
    for copy in e_beside:
        copy.wait_recv()

    group = 32

    def serve(g, carry):
        first = g * group

        def await_rows(i, carry):
            pltpu.make_async_copy(got.at[first + i], got.at[first + i], recv.at[first + i]).wait()
            return carry

        lax.fori_loop(0, group, await_rows, 0)
        at = pl.ds(pl.multiple_of(first, group), group)

        def expert(j, carry):
            mine = got[at, j].astype(F32).reshape(group * cap, D).astype(BF)
            total = None
            for q in range(2):
                gate = jnp.dot(mine, wg[q, j], preferred_element_type=F32)
                up = jnp.dot(mine, wu[q, j], preferred_element_type=F32)
                hidden = (gate / (1.0 + jnp.exp(-gate)) * up).astype(BF)
                part = jnp.dot(hidden, wd[q, j], preferred_element_type=F32)
                total = part if total is None else total + part
            stage[at, j] = total.reshape(group, cap, D).astype(BF)
            return carry

        lax.fori_loop(0, 2, expert, 0)

        @pl.when(g == 0)
        def _():
            pltpu.make_async_copy(stage.at[0], back.at[yhi, pair(ctx)], b_recv.at[0]).start()

        def send_back(i, carry):
            @pl.when(first + i > 0)
            def _():
                back_copy(first + i).start()

            return carry

        lax.fori_loop(0, group, send_back, 0)
        return carry

    lax.fori_loop(0, 2, serve, 0)

    def await_back(i, carry):
        from_ctx, from_exp = shifted(i, 1, ctx, exp)
        block = back.at[from_exp // 2, pair(from_ctx)]
        pltpu.make_async_copy(block, block, b_recv.at[i]).wait()
        return carry

    lax.fori_loop(0, 64, await_back, 0)
    total = residual
    for n in range(2):
        served = back[n].astype(F32).reshape(places, D).astype(BF)
        for gate in (hi, lo):
            total = total + lax.dot_general(
                gate, served, (((0,), (0,)), ((), ())), preferred_element_type=F32
            )
    out_ref[...] = total.astype(BF)

    def sent(i, carry):
        row_copy(i).wait_send()
        back_copy(i).wait_send()
        return carry

    lax.fori_loop(1, 64, sent, 0)

    def sent_heads(i, carry):
        own, away, local = head_copies(i)

        @pl.when(jnp.logical_not(own))
        def _():
            for copy in away:
                copy.wait_send()

        return carry

    lax.fori_loop(0, 8, sent_heads, 0)

    def sent_out(i, carry):
        away, local = out_copy(i)

        @pl.when(i != head)
        def _():
            away.wait_send()

        return carry

    lax.fori_loop(0, 16, sent_out, 0)
    for copy in (k_right, k_left, v_right, v_left, k_on, v_on):
        copy.wait_send()
    for slot in range(4):
        for copy in to_sibling(slot):
            copy.wait_send()
    for copy in (w_across, w_beside, w_on):
        copy.wait_send()
    for copy in e_beside:
        copy.wait_send()


def layer(hit, gain_attn, wq, wk, wv, wo, gain, wr, w_gate, w_up, w_down, routes):
    experts = wr.shape[1]
    rows = routes.shape[0]
    cap = 8
    dma = pltpu.SemaphoreType.DMA
    return pl.pallas_call(
        layer_kernel,
        out_shape=jax.ShapeDtypeStruct((rows, D), BF),
        in_specs=[
            anywhere(),
            whole(),
            anywhere(),
            anywhere(),
            anywhere(),
            anywhere(),
            whole(),
            whole(),
            whole(),
            anywhere(),
            anywhere(),
            anywhere(),
        ],
        out_specs=whole(),
        scratch_shapes=[
            VMEM(hit.shape, BF),
            VMEM(wq.shape, BF),
            VMEM(wk.shape, BF),
            VMEM(wv.shape, BF),
            VMEM((2, 4, HD, 256), BF),
            VMEM((4, 2, 128, 128), BF),
            VMEM((4, 2, 2, HD, 128), BF),
            VMEM((8, HD, 256), BF),
            VMEM((4, 2, 1024, 128), BF),
            VMEM((4, 2, 2, HD, 1024), BF),
            VMEM((8, 2, 128, 256), BF),
            VMEM((2, 2, 1024, 256), F32),
            VMEM((8, HD, 256), F32),
            VMEM((8, 1, 256), F32),
            VMEM((8, 1, 256), F32),
            VMEM((8, 2, HD, 128), BF),
            VMEM((16, HD, 128), BF),
            VMEM((4,) + wo.shape, BF),
            VMEM((2,) + w_gate.shape, BF),
            VMEM((2,) + w_up.shape, BF),
            VMEM((2,) + w_down.shape, BF),
            VMEM((experts, cap, D), BF),
            VMEM((64, 2, cap, D), BF),
            VMEM((64, 2, cap, D), BF),
            VMEM((2, experts, cap, D), BF),
            dma((4,)),
            dma((3, 8)),
            dma((3, 8)),
            dma((2, 3)),
            dma((2, 3)),
            dma((2, 4)),
            dma((2, 4)),
            dma((16,)),
            dma((16,)),
            dma((3,)),
            dma((3,)),
            dma,
            dma((3,)),
            dma((3,)),
            dma((3,)),
            dma((64,)),
            dma((64,)),
            dma((64,)),
            dma((64,)),
        ],
        compiler_params=pltpu.CompilerParams(
            collective_id=0, has_side_effects=True, vmem_limit_bytes=60 << 20
        ),
        name="layer",
    )(
        hit,
        gain_attn.reshape(1, D),
        wq,
        wk,
        wv,
        wo,
        gain.reshape(1, D),
        wr.T,
        routes.T,
        w_gate,
        w_up,
        w_down,
    )


def solution(mesh):
    return jax.shard_map(
        layer,
        mesh=mesh,
        in_specs=(
            P("ctx", None),
            P(),
            P(None, "exp"),
            P(None, "exp"),
            P(None, "exp"),
            P("exp", None),
            P(),
            P(),
            P("ctx", None, "exp"),
            P("ctx", None, "exp"),
            P("ctx", "exp", None),
            P(("ctx", "exp"), None),
        ),
        out_specs=P(("ctx", "exp"), None),
        check_vma=False,
    )
```

time: 138 us -> 133 us (0.964)
  Pallas kernels: 135 us -> 130 us
    pallas_call x3 -> x1, Pallas kernels: 135 us -> 130 us  [layer(): pl.pallas_call(layer_kernel, out_shape=jax.ShapeDtypeStruct((rows, D), BF...]
where the time goes in v5:
time: 133 us; the launch traced here: 132 us
  Pallas kernels  130 us (98%)
  local copies, waits for them, and re-layouts  1.67 us (1%)
    pallas_call x1, Pallas kernels, layer(): pl.pallas_call(layer_kernel, out_shape=jax.ShapeDtypeStruct((rows, D), BF...  130 us

profile of v5, /device:TPU:1, one launch (start us, length us, event | category | flops | bytes accessed | tf_op | source)
XLA Modules:
  0.0 131.9 jit_solution(392389312943070285)
XLA Ops:
  0.0 130.3 %layer.1 = bf16[128,1024]{1,0:T(8,128)(2,1)} custom-call(bf16[512,1024]{1,0:T(8,128)(2,1)} %hit_hbm.1, f32[1,1024]{1,0:T(1,128)} %bitcast.5, bf16[1024,256]{1,0:T(8,128)(2,1)} %wq_hbm.1, bf16[1024,256]{1,0:T(8,128)(2,1)} %wk_hbm.1, bf16[1024,256]{1,0:T(8,128)(2,1)} %wv_hbm.1, bf16[256,1024]{1,0:T(8,128)(2,1)} %wo_ref.1, f32[1,1024]{1,0:T(1,128)} %bitcast.6, ...), custom_call_target="tpu_custom_call" | custom-call | tf_op jit(solution)/shard_map/layer/pallas_call | solution.py:590
  130.3 1.7 %copy.14 = bf16[128,1024]{1,0:T(8,128)(2,1)} copy(bf16[128,1024]{1,0:T(8,128)(2,1)} %layer.1) | data formatting | bytes 524288

commit v6 on v5

--- a/solution.py
+++ b/solution.py
@@ -28,11 +28,11 @@
 
 
 def shifted(i, sign, ctx, exp):
-    o = (i * 27) % 64
+    o = (i * 11) % 32
     ylo, x, z, yhi = ctx // 16, (ctx // 4) % 4, ctx % 4, exp // 2
     to_x = (x + 4 + sign * (o % 4)) % 4
-    to_y = (yhi * 2 + ylo + 4 + sign * ((o // 4) % 4)) % 4
-    to_z = (z + 4 + sign * (o // 16)) % 4
+    to_y = (yhi * 2 + ylo + 4 + sign * (((o // 4) % 2) * 2 + i // 32)) % 4
+    to_z = (z + 4 + sign * (o // 8)) % 4
     to_ctx = (to_y % 2) * 16 + to_x * 4 + to_z
     return to_ctx, (to_y // 2) * 2 + exp % 2
 
@@ -76,6 +76,9 @@
     got,
     stage,
     back,
+    table_ref,
+    res_ref,
+    normed_ref,
     load,
     x_send,
     x_recv,
@@ -209,190 +212,6 @@
 
     lax.fori_loop(0, 8, send_heads, 0)
 
-    def await_heads(j, carry):
-        pltpu.make_async_copy(qg.at[j], qg.at[j], x_recv.at[0, j]).wait()
-        at = pl.ds(pl.multiple_of(j * 128, 128), 128)
-        kd = kg.at[0, core, at, :]
-        pltpu.make_async_copy(kd, kd, x_recv.at[1, j]).wait()
-        vd = vg.at[0, core, :, :, at]
-        pltpu.make_async_copy(vd, vd, x_recv.at[2, j]).wait()
-        return carry
-
-    lax.fori_loop(0, 8, await_heads, 0)
-
-    def remote(src, dst, send, recv, to):
-        return pltpu.make_async_remote_copy(
-            src_ref=src,
-            dst_ref=dst,
-            send_sem=send,
-            recv_sem=recv,
-            device_id=to,
-            device_id_type=MESH,
-        )
-
-    def to_sibling(slot):
-        return [
-            remote(g.at[slot, core], g.at[slot, core], sib_send.at[n, slot], sib_recv.at[n, slot], sibling)
-            for n, g in enumerate((kg, vg))
-        ]
-
-    def from_sibling(slot):
-        return [
-            remote(g.at[slot, 1 - core], g.at[slot, 1 - core], sib_send.at[n, slot], sib_recv.at[n, slot], sibling)
-            for n, g in enumerate((kg, vg))
-        ]
-
-    k_right = remote(kg.at[0, core], kg.at[1, core], ring_send.at[0, 0], ring_recv.at[0, 0], right)
-    v_right = remote(vg.at[0, core], vg.at[1, core], ring_send.at[1, 0], ring_recv.at[1, 0], right)
-    k_left = remote(kg.at[0, core], kg.at[2, core], ring_send.at[0, 1], ring_recv.at[0, 1], left)
-    v_left = remote(vg.at[0, core], vg.at[2, core], ring_send.at[1, 1], ring_recv.at[1, 1], left)
-    k_on = remote(kg.at[1, core], kg.at[3, core], ring_send.at[0, 2], ring_recv.at[0, 2], right)
-    v_on = remote(vg.at[2, core], vg.at[3, core], ring_send.at[1, 2], ring_recv.at[1, 2], left)
-    for copy in (k_right, k_left, v_right, v_left):
-        copy.start()
-    for copy in to_sibling(0):
-        copy.start()
-
-    far_chip = device(ylo, x, z, 1 - yhi, core)
-    far_exp = (exp + 2) % 4
-    w_local = pltpu.make_async_copy(wo_ref, wo_all.at[exp], w_own)
-    w_across = remote(wo_ref, wo_all.at[exp], w_send.at[0], w_recv.at[0], far_chip)
-    w_beside = remote(wo_ref, wo_all.at[exp], w_send.at[1], w_recv.at[1], sibling)
-    w_on = remote(
-        wo_all.at[far_exp], wo_all.at[far_exp], w_send.at[2], w_recv.at[2], sibling
-    )
-    w_across.start()
-    w_beside.start()
-    w_local.start()
-    e_beside = [
-        remote(src, dst, e_send.at[n], e_recv.at[n], sibling)
-        for n, (src, dst) in enumerate(
-            ((gate_ref, wg.at[1]), (up_ref, wu.at[1]), (down_ref, wd.at[1]))
-        )
-    ]
-    weight_loads = [
-        pltpu.make_async_copy(src, dst.at[0], w_sem.at[n])
-        for n, (src, dst) in enumerate(((gate_ref, wg), (up_ref, wu), (down_ref, wd)))
-    ]
-    for copy in weight_loads:
-        copy.start()
-    for copy in e_beside:
-        copy.start()
-
-    zero = jnp.zeros((HD, 256), BF)
-    for j in range(8):
-        q2[j, 0, 0:HD] = qg[j]
-        q2[j, 0, HD : 2 * HD] = zero
-        q2[j, 1, 0:HD] = zero
-        q2[j, 1, HD : 2 * HD] = qg[j]
-    acc[...] = jnp.zeros_like(acc)
-    mx[...] = jnp.full_like(mx, LOWEST)
-    ls[...] = jnp.zeros_like(ls)
-
-    def score(phase, tile, p):
-        j = (tile + mine) % 8
-        keys = kg[phase // 2, (phase + core) % 2]
-        for u in range(2):
-            s_ref[p, u] = lax.dot_general(
-                keys, q2[j, u], (((1,), (0,)), ((), ())), preferred_element_type=F32
-            )
-
-    def absorb(phase, tile, p):
-        j = (tile + mine) % 8
-        s0 = s_ref[p, 0]
-        s1 = s_ref[p, 1]
-        old = mx[j]
-        new = jnp.maximum(
-            old,
-            jnp.maximum(jnp.max(s0, axis=0, keepdims=True), jnp.max(s1, axis=0, keepdims=True)),
-        )
-        fade = jnp.exp2((old - new) * ALPHA)
-        e0 = jnp.exp2((s0 - new) * ALPHA)
-        e1 = jnp.exp2((s1 - new) * ALPHA)
-        slot, half = phase // 2, (phase + core) % 2
-        ls[j] = ls[j] * fade + (
-            jnp.sum(e0, axis=0, keepdims=True) + jnp.sum(e1, axis=0, keepdims=True)
-        )
-        acc[j] = acc[j] * fade + (
-            jnp.dot(vg[slot, half, 0], e0.astype(BF), preferred_element_type=F32)
-            + jnp.dot(vg[slot, half, 1], e1.astype(BF), preferred_element_type=F32)
-        )
-        mx[j] = new
-
-    head = yhi * 8 + mine
-
-    def out_copy(i):
-        j, to_yhi = i % 8, i // 8
-        to = device(j // 4, x, j % 4, to_yhi, core)
-        return (
-            remote(ost.at[j, to_yhi], at_ref.at[head], o_send.at[i], o_recv.at[head], to),
-            pltpu.make_async_copy(ost.at[j, to_yhi], at_ref.at[head], o_recv.at[head]),
-        )
-
-    def send_out(tile):
-        j = (tile + mine) % 8
-        o = (acc[j] / ls[j]).astype(BF)
-        ost[j, 0] = o[:, 0:128]
-        ost[j, 1] = o[:, 128:256]
-        for to_yhi in range(2):
-            i = to_yhi * 8 + j
-            away, local = out_copy(i)
-
-            @pl.when(i == head)
-            def _(local=local):
-                local.start()
-
-            @pl.when(i != head)
-            def _(away=away):
-                away.start()
-
-    score(0, 0, 0)
-
-    def turn(g, carry):
-        phase, pair = g // 4, g % 4
-        last = pair == 3
-
-        for slot in (0, 1, 2, 3):
-
-            @pl.when(last & (phase == 2 * slot))
-            def _(slot=slot):
-                for copy in from_sibling(slot):
-                    copy.wait_recv()
-
-        @pl.when(last & (phase == 1))
-        def _():
-            for copy in (k_right, k_left, v_right, v_left):
-                copy.wait_recv()
-            k_on.start()
-            v_on.start()
-            for slot in (1, 2):
-                for copy in to_sibling(slot):
-                    copy.start()
-
-        @pl.when(last & (phase == 5))
-        def _():
-            k_on.wait_recv()
-            v_on.wait_recv()
-            w_across.wait_recv()
-            w_on.start()
-            for copy in to_sibling(3):
-                copy.start()
-
-        score(phase, 2 * pair + 1, 1)
-        absorb(phase, 2 * pair, 0)
-        later = jnp.minimum(g + 1, 31)
-        score(later // 4, 2 * (later % 4), 0)
-        absorb(phase, 2 * pair + 1, 1)
-
-        @pl.when(phase == 7)
-        def _():
-            send_out(2 * pair)
-            send_out(2 * pair + 1)
-
-        return carry
-
-    lax.fori_loop(0, 32, turn, 0)
-
     rows = at_ref.shape[2]
     experts, cap = rows_out.shape[0], rows_out.shape[1]
     places = experts * cap
@@ -414,29 +233,146 @@
     wide = lambda v: jnp.dot(spread, v, preferred_element_type=F32)
     order = (lax.broadcasted_iota(jnp.int32, (places, rows), 0) % cap).astype(F32)
     here = (wide(marks) > 0.5) & (wide(slots) == order)
-    table = jnp.where(here, 1.0, 0.0).astype(BF)
-
-    def await_out(i, carry):
-        pltpu.make_async_copy(at_ref.at[i], at_ref.at[i], o_recv.at[i]).wait()
-        return carry
-
-    lax.fori_loop(0, 16, await_out, 0)
-
-    w_local.wait()
-    w_beside.wait_recv()
-    w_on.wait_recv()
-    mixed = lax.dot_general(
-        at_ref[...].reshape(D, rows),
-        wo_all[...].reshape(D, D),
-        (((0,), (0,)), ((), ())),
-        preferred_element_type=F32,
+    table_ref[...] = jnp.where(here, 1.0, 0.0).astype(BF)
+
+    def await_heads(j, carry):
+        pltpu.make_async_copy(qg.at[j], qg.at[j], x_recv.at[0, j]).wait()
+        at = pl.ds(pl.multiple_of(j * 128, 128), 128)
+        kd = kg.at[0, core, at, :]
+        pltpu.make_async_copy(kd, kd, x_recv.at[1, j]).wait()
+        vd = vg.at[0, core, :, :, at]
+        pltpu.make_async_copy(vd, vd, x_recv.at[2, j]).wait()
+        return carry
+
+    lax.fori_loop(0, 8, await_heads, 0)
+
+    def remote(src, dst, send, recv, to):
+        return pltpu.make_async_remote_copy(
+            src_ref=src,
+            dst_ref=dst,
+            send_sem=send,
+            recv_sem=recv,
+            device_id=to,
+            device_id_type=MESH,
+        )
+
+    def to_sibling(slot):
+        return [
+            remote(g.at[slot, core], g.at[slot, core], sib_send.at[n, slot], sib_recv.at[n, slot], sibling)
+            for n, g in enumerate((kg, vg))
+        ]
+
+    def from_sibling(slot):
+        return [
+            remote(g.at[slot, 1 - core], g.at[slot, 1 - core], sib_send.at[n, slot], sib_recv.at[n, slot], sibling)
+            for n, g in enumerate((kg, vg))
+        ]
+
+    k_right = remote(kg.at[0, core], kg.at[1, core], ring_send.at[0, 0], ring_recv.at[0, 0], right)
+    v_right = remote(vg.at[0, core], vg.at[1, core], ring_send.at[1, 0], ring_recv.at[1, 0], right)
+    k_left = remote(kg.at[0, core], kg.at[2, core], ring_send.at[0, 1], ring_recv.at[0, 1], left)
+    v_left = remote(vg.at[0, core], vg.at[2, core], ring_send.at[1, 1], ring_recv.at[1, 1], left)
+    k_on = remote(kg.at[1, core], kg.at[3, core], ring_send.at[0, 2], ring_recv.at[0, 2], right)
+    v_on = remote(vg.at[2, core], vg.at[3, core], ring_send.at[1, 2], ring_recv.at[1, 2], left)
+    for copy in (k_right, k_left, v_right, v_left):
+        copy.start()
+    for copy in to_sibling(0):
+        copy.start()
+
+    far_chip = device(ylo, x, z, 1 - yhi, core)
+    far_exp = (exp + 2) % 4
+    w_local = pltpu.make_async_copy(wo_ref, wo_all.at[exp], w_own)
+    w_across = remote(wo_ref, wo_all.at[exp], w_send.at[0], w_recv.at[0], far_chip)
+    w_beside = remote(wo_ref, wo_all.at[exp], w_send.at[1], w_recv.at[1], sibling)
+    w_on = remote(
+        wo_all.at[far_exp], wo_all.at[far_exp], w_send.at[2], w_recv.at[2], sibling
     )
-    own_rows = x_ref[pl.ds(pl.multiple_of(exp * rows, rows), rows), :]
-    residual = own_rows.astype(F32) + mixed
-    inv = lax.rsqrt(jnp.mean(residual * residual, axis=-1, keepdims=True) + EPSILON)
-    normed = (residual * inv * gain_ref[...]).astype(BF)
-    picked = jnp.dot(table, normed, preferred_element_type=F32)
-    rows_out[...] = picked.reshape(rows_out.shape).astype(BF)
+    w_across.start()
+    w_beside.start()
+    w_local.start()
+    e_beside = [
+        remote(src, dst, e_send.at[n], e_recv.at[n], sibling)
+        for n, (src, dst) in enumerate(
+            ((gate_ref, wg.at[1]), (up_ref, wu.at[1]), (down_ref, wd.at[1]))
+        )
+    ]
+    weight_loads = [
+        pltpu.make_async_copy(src, dst.at[0], w_sem.at[n])
+        for n, (src, dst) in enumerate(((gate_ref, wg), (up_ref, wu), (down_ref, wd)))
+    ]
+    for copy in weight_loads:
+        copy.start()
+    for copy in e_beside:
+        copy.start()
+
+    zero = jnp.zeros((HD, 256), BF)
+    for j in range(8):
+        q2[j, 0, 0:HD] = qg[j]
+        q2[j, 0, HD : 2 * HD] = zero
+        q2[j, 1, 0:HD] = zero
+        q2[j, 1, HD : 2 * HD] = qg[j]
+    acc[...] = jnp.zeros_like(acc)
+    mx[...] = jnp.full_like(mx, LOWEST)
+    ls[...] = jnp.zeros_like(ls)
+
+    def score(phase, tile, p):
+        j = (tile // 4) * 4 + (tile + z) % 4
+        keys = kg[phase // 2, (phase + core) % 2]
+        for u in range(2):
+            s_ref[p, u] = lax.dot_general(
+                keys, q2[j, u], (((1,), (0,)), ((), ())), preferred_element_type=F32
+            )
+
+    def absorb(phase, tile, p):
+        j = (tile // 4) * 4 + (tile + z) % 4
+        s0 = s_ref[p, 0]
+        s1 = s_ref[p, 1]
+        old = mx[j]
+        new = jnp.maximum(
+            old,
+            jnp.maximum(jnp.max(s0, axis=0, keepdims=True), jnp.max(s1, axis=0, keepdims=True)),
+        )
+        fade = jnp.exp2((old - new) * ALPHA)
+        e0 = jnp.exp2((s0 - new) * ALPHA)
+        e1 = jnp.exp2((s1 - new) * ALPHA)
+        slot, half = phase // 2, (phase + core) % 2
+        ls[j] = ls[j] * fade + (
+            jnp.sum(e0, axis=0, keepdims=True) + jnp.sum(e1, axis=0, keepdims=True)
+        )
+        acc[j] = acc[j] * fade + (
+            jnp.dot(vg[slot, half, 0], e0.astype(BF), preferred_element_type=F32)
+            + jnp.dot(vg[slot, half, 1], e1.astype(BF), preferred_element_type=F32)
+        )
+        mx[j] = new
+
+    head = yhi * 8 + mine
+
+    def out_copy(i):
+        j, to_yhi = i % 8, i // 8
+        to = device(j // 4, x, j % 4, to_yhi, core)
+        return (
+            remote(ost.at[j, to_yhi], at_ref.at[head], o_send.at[i], o_recv.at[head], to),
+            pltpu.make_async_copy(ost.at[j, to_yhi], at_ref.at[head], o_recv.at[head]),
+        )
+
+    def send_out(tile):
+        j = (tile // 4) * 4 + (tile + z) % 4
+        o = (acc[j] / ls[j]).astype(BF)
+        ost[j, 0] = o[:, 0:128]
+        ost[j, 1] = o[:, 128:256]
+        for to_yhi in range(2):
+            i = to_yhi * 8 + j
+            away, local = out_copy(i)
+
+            @pl.when(i == head)
+            def _(local=local):
+                local.start()
+
+            @pl.when(i != head)
+            def _(away=away):
+                away.start()
+
+    score(0, 0, 0)
 
     def pair(n):
         return pl.ds(pl.multiple_of(2 * n, 2), 2)
@@ -462,13 +398,100 @@
             device_id_type=MESH,
         )
 
-    def send_rows(i, carry):
-        row_copy(i).start()
-        return carry
-
-    pltpu.make_async_copy(rows_out.at[pair(ctx)], got.at[0], recv.at[0]).start()
-    lax.fori_loop(1, 64, send_rows, 0)
-
+    def route_rows():
+        def await_out(i, carry):
+            pltpu.make_async_copy(at_ref.at[i], at_ref.at[i], o_recv.at[i]).wait()
+            return carry
+
+        lax.fori_loop(0, 16, await_out, 0)
+        w_local.wait()
+        w_beside.wait_recv()
+        w_on.wait_recv()
+        mixed = lax.dot_general(
+            at_ref[...].reshape(D, rows),
+            wo_all[...].reshape(D, D),
+            (((0,), (0,)), ((), ())),
+            preferred_element_type=F32,
+        )
+        own_rows = x_ref[pl.ds(pl.multiple_of(exp * rows, rows), rows), :]
+        residual = own_rows.astype(F32) + mixed
+        inv = lax.rsqrt(jnp.mean(residual * residual, axis=-1, keepdims=True) + EPSILON)
+        res_ref[...] = residual
+        normed = (residual * inv * gain_ref[...]).astype(BF)
+        normed_ref[...] = normed
+        picked = jnp.dot(table_ref[...], normed, preferred_element_type=F32)
+        rows_out[...] = picked.reshape(rows_out.shape).astype(BF)
+        pltpu.make_async_copy(rows_out.at[pair(ctx)], got.at[0], recv.at[0]).start()
+
+        def send_rows(i, carry):
+            row_copy((i % 2) * 32 + i // 2).start()
+            return carry
+
+        lax.fori_loop(1, 64, send_rows, 0)
+
+    def step_of(g):
+        late = jnp.minimum(g // 8, 1)
+        k = jnp.maximum(g - 8, 0)
+        phase = (1 - late) * (g // 4) + late * (2 + (k % 12) // 2)
+        pair = (1 - late) * (g % 4) + late * ((k // 12) * 2 + k % 2)
+        return phase, pair
+
+    def turn(g, carry):
+        phase, pair = step_of(g)
+
+        for slot, at in ((0, 3), (1, 9), (2, 13), (3, 17)):
+
+            @pl.when(g == at)
+            def _(slot=slot):
+                for copy in from_sibling(slot):
+                    copy.wait_recv()
+
+        @pl.when(g == 7)
+        def _():
+            for copy in (k_right, k_left, v_right, v_left):
+                copy.wait_recv()
+            k_on.start()
+            v_on.start()
+            for slot in (1, 2):
+                for copy in to_sibling(slot):
+                    copy.start()
+
+        @pl.when(g == 15)
+        def _():
+            k_on.wait_recv()
+            v_on.wait_recv()
+            for copy in to_sibling(3):
+                copy.start()
+            w_across.wait_recv()
+            w_on.start()
+
+        @pl.when((g == 23) & (ylo == 0))
+        def _():
+            route_rows()
+
+        score(phase, 2 * pair + 1, 1)
+        absorb(phase, 2 * pair, 0)
+        later = jnp.minimum(g + 1, 31)
+        next_phase, next_pair = step_of(later)
+        score(next_phase, 2 * next_pair, 0)
+        absorb(phase, 2 * pair + 1, 1)
+
+        @pl.when(phase == 7)
+        def _():
+            send_out(2 * pair)
+            send_out(2 * pair + 1)
+
+        return carry
+
+    lax.fori_loop(0, 32, turn, 0)
+
+    @pl.when(ylo == 1)
+    def _():
+        route_rows()
+
+
+    normed = normed_ref[...]
+    here = table_ref[...].astype(F32) > 0.5
     logits = lax.dot_general(
         wr_ref[...], normed, (((1,), (1,)), ((), ())), preferred_element_type=F32
     )
@@ -487,7 +510,7 @@
     group = 32
 
     def serve(g, carry):
-        first = g * group
+        first = ((ylo + g) % 2) * group
 
         def await_rows(i, carry):
             pltpu.make_async_copy(got.at[first + i], got.at[first + i], recv.at[first + i]).wait()
@@ -510,7 +533,7 @@
 
         lax.fori_loop(0, 2, expert, 0)
 
-        @pl.when(g == 0)
+        @pl.when(first == 0)
         def _():
             pltpu.make_async_copy(stage.at[0], back.at[yhi, pair(ctx)], b_recv.at[0]).start()
 
@@ -533,7 +556,7 @@
         return carry
 
     lax.fori_loop(0, 64, await_back, 0)
-    total = residual
+    total = res_ref[...]
     for n in range(2):
         served = back[n].astype(F32).reshape(places, D).astype(BF)
         for gate in (hi, lo):
@@ -631,6 +654,9 @@
             VMEM((64, 2, cap, D), BF),
             VMEM((64, 2, cap, D), BF),
             VMEM((2, experts, cap, D), BF),
+            VMEM((experts * cap, rows), BF),
+            VMEM((rows, D), F32),
+            VMEM((rows, D), BF),
             dma((4,)),
             dma((3, 8)),
             dma((3, 8)),

time: 133 us -> 148 us (1.11)
  Pallas kernels: 130 us -> 144 us
    pallas_call x1, Pallas kernels: 130 us -> 144 us  [layer(): pl.pallas_call(layer_kernel, out_shape=jax.ShapeDtypeStruct((rows, D), BF...]
where the time goes in v6:
time: 148 us; the launch traced here: 146 us
  Pallas kernels  144 us (97%)
  local copies, waits for them, and re-layouts  1.67 us (1%)
    pallas_call x1, Pallas kernels, layer(): pl.pallas_call(layer_kernel, out_shape=jax.ShapeDtypeStruct((rows, D), BF...  144 us

profile of v6, /device:TPU:1, one launch (start us, length us, event | category | flops | bytes accessed | tf_op | source)
XLA Modules:
  0.0 145.6 jit_solution(2017472058327591766)
XLA Ops:
  0.0 144.0 %layer.1 = bf16[128,1024]{1,0:T(8,128)(2,1)} custom-call(bf16[512,1024]{1,0:T(8,128)(2,1)} %hit_hbm.1, f32[1,1024]{1,0:T(1,128)} %bitcast.5, bf16[1024,256]{1,0:T(8,128)(2,1)} %wq_hbm.1, bf16[1024,256]{1,0:T(8,128)(2,1)} %wk_hbm.1, bf16[1024,256]{1,0:T(8,128)(2,1)} %wv_hbm.1, bf16[256,1024]{1,0:T(8,128)(2,1)} %wo_ref.1, f32[1,1024]{1,0:T(1,128)} %bitcast.6, ...), custom_call_target="tpu_custom_call" | custom-call | tf_op jit(solution)/shard_map/layer/pallas_call | solution.py:613
  144.0 1.7 %copy.14 = bf16[128,1024]{1,0:T(8,128)(2,1)} copy(bf16[128,1024]{1,0:T(8,128)(2,1)} %layer.1) | data formatting | bytes 524288

commit v7 on v6

--- a/solution.py
+++ b/solution.py
@@ -28,11 +28,11 @@
 
 
 def shifted(i, sign, ctx, exp):
-    o = (i * 11) % 32
+    o = (i * 27) % 64
     ylo, x, z, yhi = ctx // 16, (ctx // 4) % 4, ctx % 4, exp // 2
     to_x = (x + 4 + sign * (o % 4)) % 4
-    to_y = (yhi * 2 + ylo + 4 + sign * (((o // 4) % 2) * 2 + i // 32)) % 4
-    to_z = (z + 4 + sign * (o // 8)) % 4
+    to_y = (yhi * 2 + ylo + 4 + sign * ((o // 4) % 4)) % 4
+    to_z = (z + 4 + sign * (o // 16)) % 4
     to_ctx = (to_y % 2) * 16 + to_x * 4 + to_z
     return to_ctx, (to_y // 2) * 2 + exp % 2
 
@@ -168,45 +168,41 @@
 
     def head_copies(i):
         head, half = (z + 1 + i // 2) % 4, i % 2
-        to = device(core, x, head, yhi, half)
+        at = pl.ds(pl.multiple_of(mine * 128, 128), 128)
         parts = (
-            (qt_ref.at[half, head], qg.at[mine]),
-            (kp_ref.at[head, half], kg.at[0, half, pl.ds(pl.multiple_of(mine * 128, 128), 128), :]),
-            (
-                vt_ref.at[head, half],
-                vg.at[0, half, :, :, pl.ds(pl.multiple_of(mine * 128, 128), 128)],
-            ),
-        )
-        own = (core == ylo) & (head == z) & (half == core)
-        remote = [
+            (qt_ref.at[half, head], qg.at[half * 4 + z], half * 4 + z, ylo),
+            (kp_ref.at[head, half], kg.at[0, half, at, :], mine, half),
+            (vt_ref.at[head, half], vg.at[0, half, :, :, at], mine, half),
+        )
+        here = (core == ylo) & (head == z)
+        own = [here, here & (half == core), here & (half == core)]
+        away = [
             pltpu.make_async_remote_copy(
                 src_ref=src,
                 dst_ref=dst,
                 send_sem=x_send.at[n, i],
-                recv_sem=x_recv.at[n, mine],
-                device_id=to,
+                recv_sem=x_recv.at[n, at_sem],
+                device_id=device(core, x, head, yhi, to_core),
                 device_id_type=MESH,
             )
-            for n, (src, dst) in enumerate(parts)
+            for n, (src, dst, at_sem, to_core) in enumerate(parts)
         ]
         local = [
-            pltpu.make_async_copy(src, dst, x_recv.at[n, mine])
-            for n, (src, dst) in enumerate(parts)
+            pltpu.make_async_copy(src, dst, x_recv.at[n, at_sem])
+            for n, (src, dst, at_sem, to_core) in enumerate(parts)
         ]
-        return own, remote, local
+        return own, away, local
 
     def send_heads(i, carry):
-        own, remote, local = head_copies(i)
-
-        @pl.when(own)
-        def _():
-            for copy in local:
-                copy.start()
-
-        @pl.when(jnp.logical_not(own))
-        def _():
-            for copy in remote:
-                copy.start()
+        for own, away, local in zip(*head_copies(i)):
+
+            @pl.when(own)
+            def _(local=local):
+                local.start()
+
+            @pl.when(jnp.logical_not(own))
+            def _(away=away):
+                away.start()
 
         return carry
 
@@ -349,8 +345,10 @@
 
     def out_copy(i):
         j, to_yhi = i % 8, i // 8
-        to = device(j // 4, x, j % 4, to_yhi, core)
+        to = device(core, x, j % 4, to_yhi, j // 4)
+        own = (core == ylo) & (j % 4 == z) & (to_yhi == yhi) & (j // 4 == core)
         return (
+            own,
             remote(ost.at[j, to_yhi], at_ref.at[head], o_send.at[i], o_recv.at[head], to),
             pltpu.make_async_copy(ost.at[j, to_yhi], at_ref.at[head], o_recv.at[head]),
         )
@@ -362,13 +360,13 @@
         ost[j, 1] = o[:, 128:256]
         for to_yhi in range(2):
             i = to_yhi * 8 + j
-            away, local = out_copy(i)
-
-            @pl.when(i == head)
+            own, away, local = out_copy(i)
+
+            @pl.when(own)
             def _(local=local):
                 local.start()
 
-            @pl.when(i != head)
+            @pl.when(jnp.logical_not(own))
             def _(away=away):
                 away.start()
 
@@ -424,7 +422,7 @@
         pltpu.make_async_copy(rows_out.at[pair(ctx)], got.at[0], recv.at[0]).start()
 
         def send_rows(i, carry):
-            row_copy((i % 2) * 32 + i // 2).start()
+            row_copy(i).start()
             return carry
 
         lax.fori_loop(1, 64, send_rows, 0)
@@ -465,7 +463,7 @@
             w_across.wait_recv()
             w_on.start()
 
-        @pl.when((g == 23) & (ylo == 0))
+        @pl.when((g == 23) & (core == 0))
         def _():
             route_rows()
 
@@ -485,7 +483,7 @@
 
     lax.fori_loop(0, 32, turn, 0)
 
-    @pl.when(ylo == 1)
+    @pl.when(core == 1)
     def _():
         route_rows()
 
@@ -510,7 +508,7 @@
     group = 32
 
     def serve(g, carry):
-        first = ((ylo + g) % 2) * group
+        first = g * group
 
         def await_rows(i, carry):
             pltpu.make_async_copy(got.at[first + i], got.at[first + i], recv.at[first + i]).wait()
@@ -573,21 +571,20 @@
     lax.fori_loop(1, 64, sent, 0)
 
     def sent_heads(i, carry):
-        own, away, local = head_copies(i)
+        for own, away, _ in zip(*head_copies(i)):
+
+            @pl.when(jnp.logical_not(own))
+            def _(away=away):
+                away.wait_send()
+
+        return carry
+
+    lax.fori_loop(0, 8, sent_heads, 0)
+
+    def sent_out(i, carry):
+        own, away, local = out_copy(i)
 
         @pl.when(jnp.logical_not(own))
-        def _():
-            for copy in away:
-                copy.wait_send()
-
-        return carry
-
-    lax.fori_loop(0, 8, sent_heads, 0)
-
-    def sent_out(i, carry):
-        away, local = out_copy(i)
-
-        @pl.when(i != head)
         def _():
             away.wait_send()
 

time: 148 us -> 126 us (0.85); the launches traced: 146 us -> 126 us
  Pallas kernels: 144 us -> 124 us
    pallas_call x1, Pallas kernels: 144 us -> 124 us  [layer(): pl.pallas_call(layer_kernel, out_shape=jax.ShapeDtypeStruct((rows, D), BF...]
where the time goes in v7:
time: 126 us
  Pallas kernels  124 us (98%)
  local copies, waits for them, and re-layouts  1.67 us (1%)
    pallas_call x1, Pallas kernels, layer(): pl.pallas_call(layer_kernel, out_shape=jax.ShapeDtypeStruct((rows, D), BF...  124 us

profile of v7, /device:TPU:1, one launch (start us, length us, event | category | flops | bytes accessed | tf_op | source)
XLA Modules:
  0.0 126.1 jit_solution(8068009801450642960)
XLA Ops:
  0.0 124.4 %layer.1 = bf16[128,1024]{1,0:T(8,128)(2,1)} custom-call(bf16[512,1024]{1,0:T(8,128)(2,1)} %hit_hbm.1, f32[1,1024]{1,0:T(1,128)} %bitcast.5, bf16[1024,256]{1,0:T(8,128)(2,1)} %wq_hbm.1, bf16[1024,256]{1,0:T(8,128)(2,1)} %wk_hbm.1, bf16[1024,256]{1,0:T(8,128)(2,1)} %wv_hbm.1, bf16[256,1024]{1,0:T(8,128)(2,1)} %wo_ref.1, f32[1,1024]{1,0:T(1,128)} %bitcast.6, ...), custom_call_target="tpu_custom_call" | custom-call | tf_op jit(solution)/shard_map/layer/pallas_call | solution.py:610
  124.4 1.7 %copy.14 = bf16[128,1024]{1,0:T(8,128)(2,1)} copy(bf16[128,1024]{1,0:T(8,128)(2,1)} %layer.1) | data formatting | bytes 524288

commit v8 on v7

--- a/solution.py
+++ b/solution.py
@@ -98,6 +98,7 @@
     recv,
     b_send,
     b_recv,
+    known,
 ):
     ctx = lax.axis_index("ctx")
     exp = lax.axis_index("exp")
@@ -118,15 +119,18 @@
     barrier = pltpu.get_barrier_semaphore()
 
     def greet(i, carry):
-        pl.semaphore_signal(
-            barrier, inc=1, device_id=shifted(i, 1, ctx, exp), device_id_type=MESH
-        )
-        return carry
-
-    def greet_plane(i, carry):
-        to = device(i // 8, x, (i // 2) % 4, i % 2, 1 - core)
-        pl.semaphore_signal(barrier, inc=1, device_id=to, device_id_type=MESH)
-        return carry
+        @pl.when(i != mine * 2 + core)
+        def _():
+            to = device(i // 8, x, (i // 2) % 4, yhi, i % 2)
+            pl.semaphore_signal(barrier, inc=1, device_id=to, device_id_type=MESH)
+
+        return carry
+
+    far_chip = device(ylo, x, z, 1 - yhi, core)
+
+    def tell(sem, *others):
+        for to in others:
+            pl.semaphore_signal(sem, inc=1, device_id=to, device_id_type=MESH)
 
     loads = [
         pltpu.make_async_copy(src, dst, load.at[m])
@@ -136,8 +140,8 @@
     ]
     for copy in loads:
         copy.start()
-    lax.fori_loop(0, 16, greet_plane, 0)
-    lax.fori_loop(1, 64, greet, 0)
+    lax.fori_loop(0, 16, greet, 0)
+    tell(barrier, left, right, far_chip)
 
     for copy in loads[:2]:
         copy.wait()
@@ -164,7 +168,8 @@
                 at = half * 256 + u * 128
                 vt_ref[head, half, u] = vt[head * HD : head * HD + HD, at : at + 128]
 
-    pl.semaphore_wait(barrier, 79)
+    pl.semaphore_wait(barrier, 18)
+    tell(known.at[0], far_chip)
 
     def head_copies(i):
         head, half = (z + 1 + i // 2) % 4, i % 2
@@ -207,6 +212,9 @@
         return carry
 
     lax.fori_loop(0, 8, send_heads, 0)
+
+    pl.semaphore_wait(known.at[0], 1)
+    tell(known.at[1], left, right)
 
     rows = at_ref.shape[2]
     experts, cap = rows_out.shape[0], rows_out.shape[1]
@@ -230,6 +238,8 @@
     order = (lax.broadcasted_iota(jnp.int32, (places, rows), 0) % cap).astype(F32)
     here = (wide(marks) > 0.5) & (wide(slots) == order)
     table_ref[...] = jnp.where(here, 1.0, 0.0).astype(BF)
+    pl.semaphore_wait(known.at[1], 2)
+    tell(known.at[2], left, right)
 
     def await_heads(j, carry):
         pltpu.make_async_copy(qg.at[j], qg.at[j], x_recv.at[0, j]).wait()
@@ -241,6 +251,7 @@
         return carry
 
     lax.fori_loop(0, 8, await_heads, 0)
+    pl.semaphore_wait(known.at[2], 2)
 
     def remote(src, dst, send, recv, to):
         return pltpu.make_async_remote_copy(
@@ -275,7 +286,6 @@
     for copy in to_sibling(0):
         copy.start()
 
-    far_chip = device(ylo, x, z, 1 - yhi, core)
     far_exp = (exp + 2) % 4
     w_local = pltpu.make_async_copy(wo_ref, wo_all.at[exp], w_own)
     w_across = remote(wo_ref, wo_all.at[exp], w_send.at[0], w_recv.at[0], far_chip)
@@ -673,6 +683,7 @@
             dma((64,)),
             dma((64,)),
             dma((64,)),
+            pltpu.SemaphoreType.REGULAR((3,)),
         ],
         compiler_params=pltpu.CompilerParams(
             collective_id=0, has_side_effects=True, vmem_limit_bytes=60 << 20

time: 126 us -> 124 us (0.984)
  Pallas kernels: 124 us -> 122 us
    pallas_call x1, Pallas kernels: 124 us -> 122 us  [layer(): pl.pallas_call(layer_kernel, out_shape=jax.ShapeDtypeStruct((rows, D), BF...]
where the time goes in v8:
time: 124 us
  Pallas kernels  122 us (98%)
  local copies, waits for them, and re-layouts  1.67 us (1%)
    pallas_call x1, Pallas kernels, layer(): pl.pallas_call(layer_kernel, out_shape=jax.ShapeDtypeStruct((rows, D), BF...  122 us

profile of v8, /device:TPU:1, one launch (start us, length us, event | category | flops | bytes accessed | tf_op | source)
XLA Modules:
  0.0 123.9 jit_solution(2571912218115333720)
XLA Ops:
  0.0 122.2 %layer.1 = bf16[128,1024]{1,0:T(8,128)(2,1)} custom-call(bf16[512,1024]{1,0:T(8,128)(2,1)} %hit_hbm.1, f32[1,1024]{1,0:T(1,128)} %bitcast.5, bf16[1024,256]{1,0:T(8,128)(2,1)} %wq_hbm.1, bf16[1024,256]{1,0:T(8,128)(2,1)} %wk_hbm.1, bf16[1024,256]{1,0:T(8,128)(2,1)} %wv_hbm.1, bf16[256,1024]{1,0:T(8,128)(2,1)} %wo_ref.1, f32[1,1024]{1,0:T(1,128)} %bitcast.6, ...), custom_call_target="tpu_custom_call" | custom-call | tf_op jit(solution)/shard_map/layer/pallas_call | solution.py:620
  122.2 1.7 %copy.14 = bf16[128,1024]{1,0:T(8,128)(2,1)} copy(bf16[128,1024]{1,0:T(8,128)(2,1)} %layer.1) | data formatting | bytes 524288

commit v9 on v8

--- a/solution.py
+++ b/solution.py
@@ -28,7 +28,7 @@
 
 
 def shifted(i, sign, ctx, exp):
-    o = (i * 27) % 64
+    o = (i * 11) % 64
     ylo, x, z, yhi = ctx // 16, (ctx // 4) % 4, ctx % 4, exp // 2
     to_x = (x + 4 + sign * (o % 4)) % 4
     to_y = (yhi * 2 + ylo + 4 + sign * ((o // 4) % 4)) % 4
@@ -498,6 +498,53 @@
         route_rows()
 
 
+    for copy in weight_loads:
+        copy.wait()
+    for copy in e_beside:
+        copy.wait_recv()
+
+    group = 32
+
+    def serve(g, carry):
+        first = g * group
+
+        def await_rows(i, carry):
+            pltpu.make_async_copy(got.at[first + i], got.at[first + i], recv.at[first + i]).wait()
+            return carry
+
+        lax.fori_loop(0, group, await_rows, 0)
+        at = pl.ds(pl.multiple_of(first, group), group)
+
+        def expert(j, carry):
+            mine = got[at, j].astype(F32).reshape(group * cap, D).astype(BF)
+            total = None
+            for q in range(2):
+                gate = jnp.dot(mine, wg[q, j], preferred_element_type=F32)
+                up = jnp.dot(mine, wu[q, j], preferred_element_type=F32)
+                hidden = (gate / (1.0 + jnp.exp(-gate)) * up).astype(BF)
+                part = jnp.dot(hidden, wd[q, j], preferred_element_type=F32)
+                total = part if total is None else total + part
+            stage[at, j] = total.reshape(group, cap, D).astype(BF)
+            return carry
+
+        lax.fori_loop(0, 2, expert, 0)
+
+        @pl.when(first == 0)
+        def _():
+            pltpu.make_async_copy(stage.at[0], back.at[yhi, pair(ctx)], b_recv.at[0]).start()
+
+        def send_back(i, carry):
+            @pl.when(first + i > 0)
+            def _():
+                back_copy(first + i).start()
+
+            return carry
+
+        lax.fori_loop(0, group, send_back, 0)
+        return carry
+
+    lax.fori_loop(0, 2, serve, 0)
+
     normed = normed_ref[...]
     here = table_ref[...].astype(F32) > 0.5
     logits = lax.dot_general(
@@ -510,52 +557,6 @@
     gate_lo = (gates - gate_hi.astype(F32)).astype(BF)
     hi = jnp.where(here, wide(gate_hi), 0.0).astype(BF)
     lo = jnp.where(here, wide(gate_lo), 0.0).astype(BF)
-    for copy in weight_loads:
-        copy.wait()
-    for copy in e_beside:
-        copy.wait_recv()
-
-    group = 32
-
-    def serve(g, carry):
-        first = g * group
-
-        def await_rows(i, carry):
-            pltpu.make_async_copy(got.at[first + i], got.at[first + i], recv.at[first + i]).wait()
-            return carry
-
-        lax.fori_loop(0, group, await_rows, 0)
-        at = pl.ds(pl.multiple_of(first, group), group)
-
-        def expert(j, carry):
-            mine = got[at, j].astype(F32).reshape(group * cap, D).astype(BF)
-            total = None
-            for q in range(2):
-                gate = jnp.dot(mine, wg[q, j], preferred_element_type=F32)
-                up = jnp.dot(mine, wu[q, j], preferred_element_type=F32)
-                hidden = (gate / (1.0 + jnp.exp(-gate)) * up).astype(BF)
-                part = jnp.dot(hidden, wd[q, j], preferred_element_type=F32)
-                total = part if total is None else total + part
-            stage[at, j] = total.reshape(group, cap, D).astype(BF)
-            return carry
-
-        lax.fori_loop(0, 2, expert, 0)
-
-        @pl.when(first == 0)
-        def _():
-            pltpu.make_async_copy(stage.at[0], back.at[yhi, pair(ctx)], b_recv.at[0]).start()
-
-        def send_back(i, carry):
-            @pl.when(first + i > 0)
-            def _():
-                back_copy(first + i).start()
-
-            return carry
-
-        lax.fori_loop(0, group, send_back, 0)
-        return carry
-
-    lax.fori_loop(0, 2, serve, 0)
 
     def await_back(i, carry):
         from_ctx, from_exp = shifted(i, 1, ctx, exp)

time: 124 us -> 124 us (level)
  no operation moved by 1% of the time
where the time goes in v9:
time: 124 us
  Pallas kernels  122 us (98%)
  local copies, waits for them, and re-layouts  1.67 us (1%)
    pallas_call x1, Pallas kernels, layer(): pl.pallas_call(layer_kernel, out_shape=jax.ShapeDtypeStruct((rows, D), BF...  122 us

profile of v9, /device:TPU:1, one launch (start us, length us, event | category | flops | bytes accessed | tf_op | source)
XLA Modules:
  0.0 123.9 jit_solution(13593764044056756577)
XLA Ops:
  0.0 122.2 %layer.1 = bf16[128,1024]{1,0:T(8,128)(2,1)} custom-call(bf16[512,1024]{1,0:T(8,128)(2,1)} %hit_hbm.1, f32[1,1024]{1,0:T(1,128)} %bitcast.5, bf16[1024,256]{1,0:T(8,128)(2,1)} %wq_hbm.1, bf16[1024,256]{1,0:T(8,128)(2,1)} %wk_hbm.1, bf16[1024,256]{1,0:T(8,128)(2,1)} %wv_hbm.1, bf16[256,1024]{1,0:T(8,128)(2,1)} %wo_ref.1, f32[1,1024]{1,0:T(1,128)} %bitcast.6, ...), custom_call_target="tpu_custom_call" | custom-call | tf_op jit(solution)/shard_map/layer/pallas_call | solution.py:621
  122.2 1.7 %copy.14 = bf16[128,1024]{1,0:T(8,128)(2,1)} copy(bf16[128,1024]{1,0:T(8,128)(2,1)} %layer.1) | data formatting | bytes 524288

commit v10 on v8

--- a/solution.py
+++ b/solution.py
@@ -508,8 +508,9 @@
     gates = weights / jnp.sum(weights, axis=0, keepdims=True)
     gate_hi = gates.astype(BF)
     gate_lo = (gates - gate_hi.astype(F32)).astype(BF)
-    hi = jnp.where(here, wide(gate_hi), 0.0).astype(BF)
-    lo = jnp.where(here, wide(gate_lo), 0.0).astype(BF)
+    hi = jnp.where(here, wide(gate_hi), 0.0).T.astype(BF)
+    lo = jnp.where(here, wide(gate_lo), 0.0).T.astype(BF)
+    hi_lo = jnp.concatenate([hi, lo], axis=0)
     for copy in weight_loads:
         copy.wait()
     for copy in e_beside:
@@ -567,10 +568,8 @@
     total = res_ref[...]
     for n in range(2):
         served = back[n].astype(F32).reshape(places, D).astype(BF)
-        for gate in (hi, lo):
-            total = total + lax.dot_general(
-                gate, served, (((0,), (0,)), ((), ())), preferred_element_type=F32
-            )
+        both = jnp.dot(hi_lo, served, preferred_element_type=F32)
+        total = total + (both[:rows] + both[rows:])
     out_ref[...] = total.astype(BF)
 
     def sent(i, carry):

time: 124 us -> 124 us (level)
  no operation moved by 1% of the time
where the time goes in v10:
time: 124 us
  Pallas kernels  122 us (98%)
  local copies, waits for them, and re-layouts  1.67 us (1%)
    pallas_call x1, Pallas kernels, layer(): pl.pallas_call(layer_kernel, out_shape=jax.ShapeDtypeStruct((rows, D), BF...  122 us

profile of v10, /device:TPU:1, one launch (start us, length us, event | category | flops | bytes accessed | tf_op | source)
XLA Modules:
  0.0 123.8 jit_solution(2031786108545154108)
XLA Ops:
  0.0 122.1 %layer.1 = bf16[128,1024]{1,0:T(8,128)(2,1)} custom-call(bf16[512,1024]{1,0:T(8,128)(2,1)} %hit_hbm.1, f32[1,1024]{1,0:T(1,128)} %bitcast.5, bf16[1024,256]{1,0:T(8,128)(2,1)} %wq_hbm.1, bf16[1024,256]{1,0:T(8,128)(2,1)} %wk_hbm.1, bf16[1024,256]{1,0:T(8,128)(2,1)} %wv_hbm.1, bf16[256,1024]{1,0:T(8,128)(2,1)} %wo_ref.1, f32[1,1024]{1,0:T(1,128)} %bitcast.6, ...), custom_call_target="tpu_custom_call" | custom-call | tf_op jit(solution)/shard_map/layer/pallas_call | solution.py:619
  122.1 1.7 %copy.14 = bf16[128,1024]{1,0:T(8,128)(2,1)} copy(bf16[128,1024]{1,0:T(8,128)(2,1)} %layer.1) | data formatting | bytes 524288
